TPU v7x, 256 devices: a whole 4x4x8 slice. The times are simulated.
256 devices in a mesh: gx: 32 (over z, x), gy: 8 (over y, core).
Axes of the slice: x: 4, y: 4, z: 8, core: 2. Of those that a mesh axis runs over, the one named last changes fastest.
Arguments:
- right_side: float32 [8192, 512], P(('gx', 'gy')), may hold values from -6 to 6
- diagonal: float32 [8192, 512], P(('gx', 'gy')), may hold values from 0.5 to 2
- features: float32 [8192, 64, 512], P(('gx', 'gy')), may hold values from -0.078125 to 0.078125
- neighbours: int32 [8192, 27], P(('gx', 'gy')), may hold values from -1 to 8191, as said below
- vertex_features: float32 [64, 262144], P(None, ('gx', 'gy')), may hold values from -0.75 to 0.75
- vertex_bricks: int32 [262144], P(('gx', 'gy')), may hold values from 0 to 8191, as said below
Outputs:
- solution_field: float32 [8192, 512], P(('gx', 'gy'))
- residual: float32 [8192, 512], P(('gx', 'gy'))
- vertex_values: float32 [262144], P(('gx', 'gy'))
Inputs may be any that keep to these rules, and one draw needn't show every extreme that they name: `neighbours`: bricks sit at distinct integer brick coordinates; slot k of a row names the brick at the offset (k // 9 - 1, k // 3 % 3 - 1, k % 3 - 1) from its own, or -1 where no brick is there, so slot 13 names the brick itself and the relation is symmetric. Every brick whose coordinates differ from a brick's by at most two in each direction is held by a device whose gx and gy indices each differ from that brick's holder's by at most one. `vertex_bricks`: vertex n names a brick of its own gx slab: a brick from (n // 8192) * 256 to (n // 8192) * 256 + 255.
All inputs are finite; a program needn't handle non-finite values.
Results may differ from a plain program's by a relative error of at most 0.0002.
Values sent between devices are 32-bit elements; how exact they have to be, the bound alone decides.
No kernel may reach another device: no remote copies, remote signals or barrier semaphores. Data moves between devices by JAX's collectives and lax.ppermute only.
A program may use at most 64 MiB of HBM per device.

v0:
```python
import jax
import jax.numpy as jnp
from jax import lax
from jax.sharding import PartitionSpec as P

ITERS = 3


def with_halo(cells, sides, width):
    for axis, dim in sides:
        count = lax.axis_size(axis)
        ends = count - 1
        head = lax.slice_in_dim(cells, 0, width, axis=dim)
        tail = lax.slice_in_dim(cells, cells.shape[dim] - width, cells.shape[dim], axis=dim)
        cells = jnp.concatenate(
            [
                lax.ppermute(tail, axis, [(i, (i + 1) % count) for i in range(ends)]),
                cells,
                lax.ppermute(head, axis, [((i + 1) % count, i) for i in range(ends)]),
            ],
            axis=dim,
        )
    return cells


def coefficient(features, field):
    return jnp.einsum("bfv,bv->bf", features, field, precision=lax.Precision.HIGHEST)


def squares(values):
    return lax.psum(jnp.sum(values * values), ("gx", "gy"))


def per_device(right_side, diagonal, features, neighbours, vertex_features, vertex_bricks):
    nrows = features.shape[0]
    width = features.shape[1]
    across = lax.axis_size("gy")
    row_index = lax.axis_index("gx")
    col_index = lax.axis_index("gy")
    targets = jnp.arange(9 * nrows, dtype=jnp.int32)
    valid = neighbours >= 0
    safe_ids = jnp.where(valid, neighbours, 0)
    owner = safe_ids // nrows
    offset_x = owner // across - row_index + 1
    offset_y = owner % across - col_index + 1
    inside = valid & (offset_x >= 0) & (offset_x < 3) & (offset_y >= 0) & (offset_y < 3)
    position, inside = ((offset_x * 3 + offset_y) * nrows + safe_ids % nrows, inside)
    hits = (position[:, :, None] == targets[None, None, :]) & inside[:, :, None]
    counts = jnp.sum(hits.astype(jnp.float32), axis=1)

    def first_halo(values):
        cycle = with_halo(values.reshape(1, 1, nrows, width), (("gx", 0), ("gy", 1)), 1)
        return cycle.reshape(9 * nrows, width)

    def first_sum(values):
        return jnp.dot(counts, first_halo(values), precision=lax.Precision.HIGHEST)

    solution_field = jnp.zeros_like(right_side)
    residual = right_side
    direction = right_side
    norm_now = squares(residual)
    for step in range(ITERS):
        second_cycle = with_halo(
            first_sum(coefficient(features, direction)).reshape(1, 1, nrows, width),
            (("gx", 0), ("gy", 1)),
            1,
        )
        second = jnp.dot(
            counts, second_cycle.reshape(9 * nrows, width), precision=lax.Precision.HIGHEST
        )
        image = diagonal * direction + jnp.einsum(
            "bfv,bf->bv", features, second, precision=lax.Precision.HIGHEST
        )
        alpha = norm_now / lax.psum(jnp.sum(direction * image), ("gx", "gy"))
        solution_field = solution_field + alpha * direction
        residual = residual - alpha * image
        norm_next = squares(residual)
        direction = residual + norm_next / norm_now * direction
        norm_now = norm_next
    surface = first_sum(coefficient(features, solution_field))
    slab_rows = lax.all_gather(surface, "gy", axis=0, tiled=True)
    local_ids = vertex_bricks - row_index * across * nrows
    picked = jnp.take(slab_rows, local_ids, axis=0)
    vertex_values = jnp.sum(vertex_features * picked.T, axis=0)
    return (solution_field, residual, vertex_values)


def solution(mesh):
    placed = (
        P(("gx", "gy"), None),
        P(("gx", "gy"), None),
        P(("gx", "gy"), None, None),
        P(("gx", "gy"), None),
        P(None, ("gx", "gy")),
        P(("gx", "gy")),
    )
    return jax.shard_map(
        per_device,
        mesh=mesh,
        in_specs=placed,
        out_specs=(P(("gx", "gy"), None), P(("gx", "gy"), None), P(("gx", "gy"))),
        check_vma=False,
    )
```

profile of v0, /device:TPU:1, one launch (start us, length us, event | category | flops | bytes accessed | tf_op | source)
XLA Modules:
  0.0 557.5 jit_solution(662496368784365687)
XLA Ops:
  0.7 5.8 %fusion.8 = f32[32,1,64]{2,1,0:T(1,128)S(1)} fusion(f32[32,64,512]{2,1,0:T(8,128)} %param.8, f32[32,512,1]{1,0,2:T(8,128)} %bitcast.92), kind=kOutput, calls=%fused_computation.25 | convolution fusion | flops 12582912 | bytes 4268032 | tf_op jit(solution)/shard_map/bfv,bv->bf/dot_general | solution.py:27
  7.8 4.6 collective-permute-start
  13.2 5.7 %collective-permute-start.3 = (f32[3,1,32,64]{3,2,1,0:T(8,128)S(1)}, f32[3,1,32,64]{3,2,1,0:T(8,128)S(1)}, u32[]{:S(2)}, u32[]{:S(2)}) collective-permute-start(f32[3,1,32,64]{3,2,1,0:T(8,128)S(1)} %pad_maximum_fusion.7), channel_id=1, source_target_pairs={{1,0},{2,1},{3,2},{4,3},{5,4},{6,5},{7,6},{9,8},{10,9},{11,10},{12... | collective-permute-start | bytes 73736 | tf_op jit(solution)/shard_map/ppermute | solution.py:19
  23.6 4.6 collective-permute-start.4
  29.0 2.9 collective-permute-start.7
  31.9 4.1 collective-permute-start.6
  37.4 4.3 fusion.25
  42.3 86.3 %all-reduce = (f32[]{:T(128)}, f32[]{:T(128)}) all-reduce(f32[]{:T(128)} %get-tuple-element.4, f32[]{:T(128)} %get-tuple-element.3), channel_id=1, replica_groups=mesh['gx'=32,'gy'=8] {'gx','gy'}, use_global_device_ids=true, to_apply=%region_1.2 | all-reduce | flops 2 | bytes 16 | tf_op jit(solution)/shard_map/psum | solution.py:31
  130.6 74.0 %psum.44 = f32[]{:T(128)} all-reduce(f32[]{:T(128)} %get-tuple-element.9), channel_id=1, replica_groups=mesh['gx'=32,'gy'=8] {'gx','gy'}, use_global_device_ids=true, to_apply=%region_6.7 | all-reduce | flops 1 | bytes 8 | tf_op jit(solution)/shard_map/psum | solution.py:31
  205.9 5.4 fusion.6
  212.7 4.0 collective-permute-start.8
  217.5 3.7 collective-permute-start.11
  225.9 4.6 collective-permute-start.12
  231.3 2.9 collective-permute-start.15
  234.2 4.2 collective-permute-start.14
  239.7 2.1 fusion.27
  242.4 81.2 %psum.45 = f32[]{:T(128)} all-reduce(f32[]{:T(128)} %multiply_reduce_fusion.2), channel_id=1, replica_groups=mesh['gx'=32,'gy'=8] {'gx','gy'}, use_global_device_ids=true, to_apply=%region_8.9 | all-reduce | flops 1 | bytes 8 | tf_op jit(solution)/shard_map/psum | solution.py:74
  325.6 74.4 %psum.46 = f32[]{:T(128)} all-reduce(f32[]{:T(128)} %get-tuple-element.7), channel_id=1, replica_groups=mesh['gx'=32,'gy'=8] {'gx','gy'}, use_global_device_ids=true, to_apply=%region_10.11 | all-reduce | flops 1 | bytes 8 | tf_op jit(solution)/shard_map/psum | solution.py:31
  401.4 5.4 fusion.4
  408.2 4.0 collective-permute-start.16
  413.0 3.7 collective-permute-start.19
  416.7 2.2 collective-permute-start.18
  421.6 4.6 collective-permute-start.20
  427.0 2.7 collective-permute-start.23
  429.7 4.4 collective-permute-start.22
  435.5 2.1 fusion.29
  438.2 81.3 %psum.47 = f32[]{:T(128)} all-reduce(f32[]{:T(128)} %multiply_reduce_fusion), channel_id=1, replica_groups=mesh['gx'=32,'gy'=8] {'gx','gy'}, use_global_device_ids=true, to_apply=%region_12.13 | all-reduce | flops 1 | bytes 8 | tf_op jit(solution)/shard_map/psum | solution.py:74
  521.5 5.3 fusion.2
  528.1 4.0 collective-permute-start.24
  533.0 4.3 collective-permute-start.27
  540.6 13.1 %all_gather.3 = f32[256,64]{1,0:T(8,128)S(1)} all-gather(f32[32,64]{1,0:T(8,128)S(1)} %fusion.30), channel_id=1, replica_groups=mesh['gx'=32,'gy'=8] {'gy'}, dimensions={0}, use_global_device_ids=true | all-gather | bytes 73728 | tf_op jit(solution)/shard_map/all_gather | solution.py:81
  553.7 2.8 gather_fusion
  (92 shorter events, 35.1 us)
Async XLA Ops:
  0.6 41.0 %copy-start.2 = (f32[32,512]{1,0:T(8,128)S(1)}, f32[32,512]{1,0:T(8,128)}, u32[]{:S(2)}) copy-start(f32[32,512]{1,0:T(8,128)} %param.7) | copy-start | bytes 196612
  0.7 41.0 %copy-start.3 = (f32[32,512]{1,0:T(8,128)S(1)}, f32[32,512]{1,0:T(8,128)}, u32[]{:S(2)}) copy-start(f32[32,512]{1,0:T(8,128)} %param.6) | copy-start | bytes 196612
  6.5 6.2 %collective-permute-start.1 = (f32[1,1,32,64]{3,2,1,0:T(8,128)S(1)}, f32[1,1,32,64]{3,2,1,0:T(8,128)S(1)}, u32[]{:S(2)}, u32[]{:S(2)}) collective-permute-start(f32[1,1,32,64]{3,2,1,0:T(8,128)S(1)} %bitcast.101), channel_id=1, source_target_pairs={{8,0},{16,8},{24,16},{32,24},{40,32},{48,40},{56,48},{64,56},{72,6... | collective-permute-start | bytes 24584 | tf_op jit(solution)/shard_map/ppermute | solution.py:19
  7.8 5.4 collective-permute-start
  13.2 7.9 %collective-permute-start.3 = (f32[3,1,32,64]{3,2,1,0:T(8,128)S(1)}, f32[3,1,32,64]{3,2,1,0:T(8,128)S(1)}, u32[]{:S(2)}, u32[]{:S(2)}) collective-permute-start(f32[3,1,32,64]{3,2,1,0:T(8,128)S(1)} %pad_maximum_fusion.7), channel_id=1, source_target_pairs={{1,0},{2,1},{3,2},{4,3},{5,4},{6,5},{7,6},{9,8},{10,9},{11,10},{12... | collective-permute-start | bytes 73736 | tf_op jit(solution)/shard_map/ppermute | solution.py:19
  18.9 3.1 collective-permute-start.2
  22.3 5.9 %collective-permute-start.5 = (f32[1,1,32,64]{3,2,1,0:T(8,128)S(1)}, f32[1,1,32,64]{3,2,1,0:T(8,128)S(1)}, u32[]{:S(2)}, u32[]{:S(2)}) collective-permute-start(f32[1,1,32,64]{3,2,1,0:T(8,128)S(1)} %convolution_bitcast_fusion.2), channel_id=1, source_target_pairs={{8,0},{16,8},{24,16},{32,24},{40,32},{48,40},{56,48},{64,56},{72,6... | collective-permute-start | bytes 24584 | tf_op jit(solution)/shard_map/ppermute | solution.py:19
  23.6 5.4 collective-permute-start.4
  29.0 7.0 %collective-permute-start.7 = (f32[3,1,32,64]{3,2,1,0:T(8,128)S(1)}, f32[3,1,32,64]{3,2,1,0:T(8,128)S(1)}, u32[]{:S(2)}, u32[]{:S(2)}) collective-permute-start(f32[3,1,32,64]{3,2,1,0:T(8,128)S(1)} %pad_maximum_fusion.8), channel_id=1, source_target_pairs={{1,0},{2,1},{3,2},{4,3},{5,4},{6,5},{7,6},{9,8},{10,9},{11,10},{12... | collective-permute-start | bytes 73736 | tf_op jit(solution)/shard_map/ppermute | solution.py:19
  31.9 5.2 collective-permute-start.6
  211.4 5.3 collective-permute-start.9
  212.7 4.8 collective-permute-start.8
  217.5 5.6 %collective-permute-start.11 = (f32[3,1,32,64]{3,2,1,0:T(8,128)S(1)}, f32[3,1,32,64]{3,2,1,0:T(8,128)S(1)}, u32[]{:S(2)}, u32[]{:S(2)}) collective-permute-start(f32[3,1,32,64]{3,2,1,0:T(8,128)S(1)} %pad_maximum_fusion.9), channel_id=1, source_target_pairs={{1,0},{2,1},{3,2},{4,3},{5,4},{6,5},{7,6},{9,8},{10,9},{11,10},{12... | collective-permute-start | bytes 73736 | tf_op jit(solution)/shard_map/ppermute | solution.py:19
  221.2 3.1 collective-permute-start.10
  224.6 5.9 %collective-permute-start.13 = (f32[1,1,32,64]{3,2,1,0:T(8,128)S(1)}, f32[1,1,32,64]{3,2,1,0:T(8,128)S(1)}, u32[]{:S(2)}, u32[]{:S(2)}) collective-permute-start(f32[1,1,32,64]{3,2,1,0:T(8,128)S(1)} %convolution_bitcast_fusion.1), channel_id=1, source_target_pairs={{8,0},{16,8},{24,16},{32,24},{40,32},{48,40},{56,48},{64,56},{72,6... | collective-permute-start | bytes 24584 | tf_op jit(solution)/shard_map/ppermute | solution.py:19
  225.9 5.4 collective-permute-start.12
  231.3 7.2 %collective-permute-start.15 = (f32[3,1,32,64]{3,2,1,0:T(8,128)S(1)}, f32[3,1,32,64]{3,2,1,0:T(8,128)S(1)}, u32[]{:S(2)}, u32[]{:S(2)}) collective-permute-start(f32[3,1,32,64]{3,2,1,0:T(8,128)S(1)} %pad_maximum_fusion.10), channel_id=1, source_target_pairs={{1,0},{2,1},{3,2},{4,3},{5,4},{6,5},{7,6},{9,8},{10,9},{11,10},{12... | collective-permute-start | bytes 73736 | tf_op jit(solution)/shard_map/ppermute | solution.py:19
  234.2 5.2 collective-permute-start.14
  406.9 5.3 collective-permute-start.17
  408.2 4.8 collective-permute-start.16
  413.0 5.9 %collective-permute-start.19 = (f32[3,1,32,64]{3,2,1,0:T(8,128)S(1)}, f32[3,1,32,64]{3,2,1,0:T(8,128)S(1)}, u32[]{:S(2)}, u32[]{:S(2)}) collective-permute-start(f32[3,1,32,64]{3,2,1,0:T(8,128)S(1)} %pad_maximum_fusion.11), channel_id=1, source_target_pairs={{1,0},{2,1},{3,2},{4,3},{5,4},{6,5},{7,6},{9,8},{10,9},{11,10},{12... | collective-permute-start | bytes 73736 | tf_op jit(solution)/shard_map/ppermute | solution.py:19
  416.7 3.4 collective-permute-start.18
  420.3 5.9 %collective-permute-start.21 = (f32[1,1,32,64]{3,2,1,0:T(8,128)S(1)}, f32[1,1,32,64]{3,2,1,0:T(8,128)S(1)}, u32[]{:S(2)}, u32[]{:S(2)}) collective-permute-start(f32[1,1,32,64]{3,2,1,0:T(8,128)S(1)} %convolution_bitcast_fusion), channel_id=1, source_target_pairs={{8,0},{16,8},{24,16},{32,24},{40,32},{48,40},{56,48},{64,56},{72,6... | collective-permute-start | bytes 24584 | tf_op jit(solution)/shard_map/ppermute | solution.py:19
  421.6 5.4 collective-permute-start.20
  427.0 7.0 %collective-permute-start.23 = (f32[3,1,32,64]{3,2,1,0:T(8,128)S(1)}, f32[3,1,32,64]{3,2,1,0:T(8,128)S(1)}, u32[]{:S(2)}, u32[]{:S(2)}) collective-permute-start(f32[3,1,32,64]{3,2,1,0:T(8,128)S(1)} %pad_maximum_fusion.12), channel_id=1, source_target_pairs={{1,0},{2,1},{3,2},{4,3},{5,4},{6,5},{7,6},{9,8},{10,9},{11,10},{12... | collective-permute-start | bytes 73736 | tf_op jit(solution)/shard_map/ppermute | solution.py:19
  429.7 5.5 collective-permute-start.22
  435.5 96.7 %copy-start.7 = (s32[1024]{0:T(1024)S(1)}, s32[1024]{0:T(1024)}, u32[]{:S(2)}) copy-start(s32[1024]{0:T(1024)} %param.11) | copy-start | bytes 12292
  435.5 103.7 %copy-start.5 = (f32[64,1024]{1,0:T(8,128)S(1)}, f32[64,1024]{1,0:T(8,128)}, u32[]{:S(2)}) copy-start(f32[64,1024]{1,0:T(8,128)} %param.10) | copy-start | bytes 786436
  526.8 5.3 collective-permute-start.25
  528.1 4.8 collective-permute-start.24
  533.0 6.4 %collective-permute-start.27 = (f32[3,1,32,64]{3,2,1,0:T(8,128)S(1)}, f32[3,1,32,64]{3,2,1,0:T(8,128)S(1)}, u32[]{:S(2)}, u32[]{:S(2)}) collective-permute-start(f32[3,1,32,64]{3,2,1,0:T(8,128)S(1)} %pad_maximum_fusion.13), channel_id=1, source_target_pairs={{1,0},{2,1},{3,2},{4,3},{5,4},{6,5},{7,6},{9,8},{10,9},{11,10},{12... | collective-permute-start | bytes 73736 | tf_op jit(solution)/shard_map/ppermute | solution.py:19
  537.2 3.1 collective-permute-start.26
  (4 other events, 114.7 us)
where the time goes:
time: 563 us; the launch traced here: 558 us
  blocking collectives  410 us (73%)
  starting transfers between devices  85.7 us (15%)
  matrix products  32 us (6%)
  waiting for transfers between devices  13 us (2%)
  between operations  7.94 us (1%)
    psum x3, blocking collectives, squares(): return lax.psum(jnp.sum(values * values), ('gx', 'gy'))  235 us
    psum x2, blocking collectives, per_device(): alpha = norm_now / lax.psum(jnp.sum(direction * image), ('gx', 'gy'))  163 us
    ppermute x14, starting transfers between devices, with_halo(): lax.ppermute(tail, axis, [(i, (i + 1) % count) for i in range(ends)])  50.8 us
    ppermute x14, starting transfers between devices, with_halo(): lax.ppermute(head, axis, [((i + 1) % count, i) for i in range(ends)])  34.8 us
    dot_general x4, matrix products, coefficient(): jnp.einsum('bfv,bv->bf', features, field, precision=lax.Precision.HIGHEST)  22 us
    all_gather x1, blocking collectives, per_device(): slab_rows = lax.all_gather(surface, 'gy', axis=0, tiled=True)  13.1 us
    ppermute x14, waiting for transfers between devices, with_halo(): lax.ppermute(tail, axis, [(i, (i + 1) % count) for i in range(ends)])  13 us
  transfers between devices with their start and end apart: 28, of which 14 were waited for; matrix products, arithmetic and copies ran while one was open for 0% of the time, Pallas kernels for 0%

commit v1 on v0

v1 whole, which is shorter than its diff:
```python
import jax
import jax.numpy as jnp
from jax import lax
from jax.sharding import PartitionSpec as P

ITERS = 3
SHIFT = 1.25
HIGHEST = lax.Precision.HIGHEST


def ring(axis, step):
    count = lax.axis_size(axis)
    return [(i, (i + step) % count) for i in range(count)]


def with_halo(block):
    column = jnp.stack(
        [lax.ppermute(block, "gx", ring("gx", 1)), block, lax.ppermute(block, "gx", ring("gx", -1))]
    )
    square = jnp.stack(
        [lax.ppermute(column, "gy", ring("gy", 1)), column, lax.ppermute(column, "gy", ring("gy", -1))],
        axis=1,
    )
    return square.reshape(9 * block.shape[0], block.shape[1])


def spread(values, axis):
    count = lax.axis_size(axis)
    return lax.all_to_all(jnp.broadcast_to(values[None], (count,) + values.shape), axis, 0, 0)


def coefficient(features, field):
    return jnp.einsum("bfv,bv->bf", features, field, precision=HIGHEST)


def expand(features, coeff):
    return jnp.einsum("bfv,bf->bv", features, coeff, precision=HIGHEST)


def one_hot_counts(ids, nrows):
    across = lax.axis_size("gy")
    owner = ids // nrows
    offset_x = owner // across - lax.axis_index("gx") + 1
    offset_y = owner % across - lax.axis_index("gy") + 1
    inside = (ids >= 0) & (offset_x >= 0) & (offset_x < 3) & (offset_y >= 0) & (offset_y < 3)
    position = jnp.where(inside, (offset_x * 3 + offset_y) * nrows + ids % nrows, -1)
    targets = jnp.arange(9 * nrows, dtype=jnp.int32)
    hits = position[:, :, None] == targets[None, None, :]
    return jnp.sum(hits.astype(jnp.float32), axis=1)


def cg_weights(mu):
    def dot(left, right):
        return sum(left[i] * right[j] * mu[i + j] for i in range(len(left)) for j in range(len(right)))

    def apply(poly):
        out = [SHIFT * p for p in poly] + [0.0]
        for i, p in enumerate(poly):
            out[i + 1] = out[i + 1] + p
        return out

    def axpy(left, scale, right):
        size = max(len(left), len(right))
        left = left + [0.0] * (size - len(left))
        return [l + scale * right[i] if i < len(right) else l for i, l in enumerate(left)]

    field, residual, direction, norm_now = [], [1.0], [1.0], mu[0]
    for step in range(ITERS):
        image = apply(direction)
        alpha = norm_now / dot(direction, image)
        field = axpy(field, alpha, direction)
        residual = axpy(residual, -alpha, image)
        if step + 1 < ITERS:
            norm_next = dot(residual, residual)
            direction = axpy(residual, norm_next / norm_now, direction)
            norm_now = norm_next
    return field, residual


def per_device(right_side, diagonal, features, neighbours, vertex_features, vertex_bricks):
    nrows, width, _ = features.shape
    slots = neighbours.shape[1]
    shifted = diagonal - SHIFT
    powers = [right_side]
    sums = []
    moments = [jnp.sum(right_side * right_side)]
    own = one_hot_counts(neighbours, nrows)
    for step in range(ITERS):
        coeff = coefficient(features, powers[-1])
        extra = neighbours.astype(jnp.float32) if step == 0 else jnp.zeros((nrows, slots), jnp.float32)
        block = jnp.concatenate([coeff, jnp.pad(extra, ((0, 0), (0, 128 - width - slots)))], axis=1)
        around = with_halo(block)
        if step == 0:
            near = one_hot_counts(around[:, width : width + slots].astype(jnp.int32), nrows)
            twice = jnp.dot(own, near, precision=HIGHEST)
        sums.append(jnp.dot(own, around[:, :width], precision=HIGHEST))
        second = jnp.dot(twice, around[:, :width], precision=HIGHEST)
        new = shifted * powers[-1] + expand(features, second)
        moments.append(jnp.sum(powers[-1] * new))
        if step + 1 < ITERS:
            moments.append(jnp.sum(new * new))
        powers.append(new)
    part = jnp.pad(jnp.stack(moments), (0, 128 - len(moments)))
    packed = jnp.concatenate(sums, axis=1).reshape(-1, 128)
    packed = jnp.concatenate([packed, jnp.broadcast_to(part[None], (8, 128))], axis=0)
    slab = spread(packed, "gy")
    part = jnp.sum(slab[:, -1, :], axis=0, keepdims=True)
    total = jnp.sum(spread(part, "gx")[:, 0, :], axis=0)
    field, residual = cg_weights([total[i] for i in range(len(moments))])
    solution_field = sum(w * v for w, v in zip(field, powers))
    residual = sum(w * v for w, v in zip(residual, powers))
    slab_sums = slab[:, :-8, :].reshape(-1, ITERS * width)
    surface = sum(w * slab_sums[:, i * width : (i + 1) * width] for i, w in enumerate(field))
    local_ids = vertex_bricks - lax.axis_index("gx") * surface.shape[0]
    picks = (jnp.arange(surface.shape[0], dtype=jnp.int32)[:, None] == local_ids[None, :]).astype(jnp.float32)
    picked = lax.dot_general(surface, picks, (((0,), (0,)), ((), ())), precision=HIGHEST)
    vertex_values = jnp.sum(vertex_features * picked, axis=0)
    return solution_field, residual, vertex_values


def solution(mesh):
    placed = (
        P(("gx", "gy"), None),
        P(("gx", "gy"), None),
        P(("gx", "gy"), None, None),
        P(("gx", "gy"), None),
        P(None, ("gx", "gy")),
        P(("gx", "gy")),
    )
    return jax.shard_map(
        per_device,
        mesh=mesh,
        in_specs=placed,
        out_specs=(P(("gx", "gy"), None), P(("gx", "gy"), None), P(("gx", "gy"))),
        check_vma=False,
    )
```

time: 563 us -> 126 us (0.22)
  blocking collectives: 410 us -> 0 us
  starting transfers between devices: 85.7 us -> 34.7 us
  waiting for transfers between devices: 13 us -> 32.9 us
  between operations: 7.94 us -> 20.8 us
    psum x5 -> x0, blocking collectives: 397 us -> none  [the longest x3 235 us: squares(): return lax.psum(jnp.sum(values * values), ('gx', 'gy'))]
    ppermute x28 -> x12, starting transfers between devices: 85.7 us -> 24 us  [the longest x3 10.9 us: with_halo(): lax.ppermute(column, 'gy', ring('gy', -1))]
    all_to_all x0 -> x2, waiting for transfers between devices: none -> 14.6 us  [spread(): lax.all_to_all(jnp.broadcast_to(values[None], (count,) + values.shape), a...]
    all_gather x1 -> x0, blocking collectives: 13.1 us -> none  [per_device(): slab_rows = lax.all_gather(surface, 'gy', axis=0, tiled=True)]
    all_to_all x0 -> x2, starting transfers between devices: none -> 10.7 us  [spread(): lax.all_to_all(jnp.broadcast_to(values[None], (count,) + values.shape), a...]
    ppermute x28 -> x12, waiting for transfers between devices: 13 us -> 18.3 us  [the longest x3 11.9 us: with_halo(): lax.ppermute(block, 'gx', ring('gx', 1))]
  transfers between devices with their start and end apart: 28 -> 14, of which waited for: 14 -> 13; matrix products, arithmetic and copies ran while one was open for 0% -> 1% of each run, Pallas kernels for 0% -> 0%
where the time goes in v1:
time: 126 us; the launch traced here: 125 us
  starting transfers between devices  34.7 us (28%)
  waiting for transfers between devices  32.9 us (26%)
  matrix products  26.5 us (21%)
  between operations  20.8 us (17%)
  local copies, waits for them, and re-layouts  6.33 us (5%)
  other arithmetic  4.24 us (3%)
    all_to_all x2, waiting for transfers between devices, spread(): lax.all_to_all(jnp.broadcast_to(values[None], (count,) + values.shape), a...  14.6 us
    dot_general x3, matrix products, coefficient(): return jnp.einsum('bfv,bv->bf', features, field, precision=HIGHEST)  13 us
    ppermute x3, waiting for transfers between devices, with_halo(): lax.ppermute(block, 'gx', ring('gx', 1))  11.9 us
    ppermute x3, starting transfers between devices, with_halo(): lax.ppermute(column, 'gy', ring('gy', -1))  10.9 us
    dot_general x3, matrix products, expand(): return jnp.einsum('bfv,bf->bv', features, coeff, precision=HIGHEST)  10.7 us
    all_to_all x2, starting transfers between devices, spread(): lax.all_to_all(jnp.broadcast_to(values[None], (count,) + values.shape), a...  10.7 us
    ppermute x3, starting transfers between devices, with_halo(): lax.ppermute(block, 'gx', ring('gx', -1))  8.95 us
    another operation x1, local copies, waits for them, and re-layouts, per_device(): part = jnp.pad(jnp.stack(moments), (0, 128 - len(moments)))  3.9 us
  transfers between devices with their start and end apart: 14, of which 13 were waited for; matrix products, arithmetic and copies ran while one was open for 1% of the time, Pallas kernels for 0%

profile of v1, /device:TPU:1, one launch (start us, length us, event | category | flops | bytes accessed | tf_op | source)
XLA Modules:
  0.0 125.4 jit_solution(16232932497054587899)
XLA Ops:
  0.6 5.8 %fusion.30 = f32[32,1,64]{2,1,0:T(1,128)S(1)} fusion(f32[32,64,512]{2,1,0:T(8,128)} %param.8, f32[32,512,1]{1,0,2:T(8,128)} %bitcast.101), kind=kOutput, calls=%fused_computation.56 | convolution fusion | flops 12582912 | bytes 4268032 | tf_op jit(solution)/shard_map/bfv,bv->bf/dot_general | solution.py:33
  6.6 8.6 %collective-permute-start.1 = (f32[32,128]{1,0:T(8,128)S(1)}, f32[32,128]{1,0:T(8,128)S(1)}, u32[]{:S(2)}, u32[]{:S(2)}) collective-permute-start(f32[32,128]{1,0:T(8,128)S(1)} %select_maximum_fusion), channel_id=1, source_target_pairs={{0,248},{8,0},{16,8},{24,16},{32,24},{40,32},{48,40},{56,48},{64,5... | collective-permute-start | bytes 49160 | tf_op jit(solution)/shard_map/ppermute | solution.py:18
  16.1 5.0 %collective-permute-done = f32[32,128]{1,0:T(8,128)S(1)} collective-permute-done((f32[32,128]{1,0:T(8,128)S(1)}, f32[32,128]{1,0:T(8,128)S(1)}, u32[]{:S(2)}, u32[]{:S(2)}) %collective-permute-start) | collective-permute-done | bytes 16416 | tf_op jit(solution)/shard_map/ppermute | solution.py:18
  21.1 2.1 %collective-permute-start.3 = (f32[3,32,128]{2,1,0:T(8,128)S(1)}, f32[3,32,128]{2,1,0:T(8,128)S(1)}, u32[]{:S(2)}, u32[]{:S(2)}) collective-permute-start(f32[3,32,128]{2,1,0:T(8,128)S(1)} %get-tuple-element.16), channel_id=1, source_target_pairs={{0,7},{1,0},{2,1},{3,2},{4,3},{5,4},{6,5},{7,6},{8,15},{9,8},{10,9... | collective-permute-start | bytes 147464 | tf_op jit(solution)/shard_map/ppermute | solution.py:21
  23.3 1.2 collective-permute-start.2
  24.5 1.7 %collective-permute-done.3 = f32[3,32,128]{2,1,0:T(8,128)S(1)} collective-permute-done((f32[3,32,128]{2,1,0:T(8,128)S(1)}, f32[3,32,128]{2,1,0:T(8,128)S(1)}, u32[]{:S(2)}, u32[]{:S(2)}) %collective-permute-start.3) | collective-permute-done | bytes 49184 | tf_op jit(solution)/shard_map/ppermute | solution.py:21
  26.8 1.6 %convert_reduce_fusion = f32[288,288]{1,0:T(8,128)S(1)} fusion(s32[288,27]{0,1:T(8,128)S(1)} %copy.24), kind=kLoop, calls=%fused_computation | loop fusion | flops 6635520 | bytes 362880 | tf_op jit(solution)/shard_map/reduce_sum | solution.py:49
  29.0 4.3 %fusion.49 = f32[32,1,512]{2,1,0:T(1,128)S(1)} fusion(f32[32,64,1]{1,2,0:T(1,128)S(1)} %bitcast.110, f32[32,64,512]{2,1,0:T(8,128)} %param.8), kind=kOutput, calls=%fused_computation.107 | convolution fusion | flops 12582912 | bytes 4268032 | tf_op jit(solution)/shard_map/bfv,bf->bv/dot_general | solution.py:37
  33.4 3.6 %fusion.28 = f32[32,1,64]{2,1,0:T(1,128)S(1)} fusion(f32[32,64,512]{2,1,0:T(8,128)S(1)} %copy-done, f32[32,512,1]{1,0,2:T(8,128)S(1)} %bitcast.96), kind=kOutput, calls=%fused_computation.54 | convolution fusion | flops 12582912 | bytes 4268032 | tf_op jit(solution)/shard_map/bfv,bv->bf/dot_general | solution.py:33
  37.2 1.5 %collective-permute-start.4 = (f32[32,128]{1,0:T(8,128)S(1)}, f32[32,128]{1,0:T(8,128)S(1)}, u32[]{:S(2)}, u32[]{:S(2)}) collective-permute-start(f32[32,128]{1,0:T(8,128)S(1)} %pad_maximum_fusion.8), channel_id=1, source_target_pairs={{0,8},{8,16},{16,24},{24,32},{32,40},{40,48},{48,56},{56,64},{64,7... | collective-permute-start | bytes 49160 | tf_op jit(solution)/shard_map/ppermute | solution.py:18
  38.7 1.1 collective-permute-done.5
  39.8 3.4 %collective-permute-done.4 = f32[32,128]{1,0:T(8,128)S(1)} collective-permute-done((f32[32,128]{1,0:T(8,128)S(1)}, f32[32,128]{1,0:T(8,128)S(1)}, u32[]{:S(2)}, u32[]{:S(2)}) %collective-permute-start.4) | collective-permute-done | bytes 16416 | tf_op jit(solution)/shard_map/ppermute | solution.py:18
  43.2 4.1 %collective-permute-start.7 = (f32[3,32,128]{2,1,0:T(8,128)S(1)}, f32[3,32,128]{2,1,0:T(8,128)S(1)}, u32[]{:S(2)}, u32[]{:S(2)}) collective-permute-start(f32[3,32,128]{2,1,0:T(8,128)S(1)} %get-tuple-element.14), channel_id=1, source_target_pairs={{0,7},{1,0},{2,1},{3,2},{4,3},{5,4},{6,5},{7,6},{8,15},{9,8},{10,9... | collective-permute-start | bytes 147464 | tf_op jit(solution)/shard_map/ppermute | solution.py:21
  47.6 0.7 collective-permute-done.7
  48.8 2.1 %fusion.50 = f32[32,1,512]{2,1,0:T(1,128)S(1)} fusion(f32[32,64,1]{1,2,0:T(1,128)S(1)} %bitcast.111, f32[32,64,512]{2,1,0:T(8,128)S(1)} %copy-done), kind=kOutput, calls=%fused_computation.108 | convolution fusion | flops 12582912 | bytes 4268032 | tf_op jit(solution)/shard_map/bfv,bf->bv/dot_general | solution.py:37
  51.0 3.6 %fusion.26 = f32[32,1,64]{2,1,0:T(1,128)S(1)} fusion(f32[32,64,512]{2,1,0:T(8,128)S(1)} %copy-done, f32[32,512,1]{1,0,2:T(8,128)S(1)} %bitcast.102), kind=kOutput, calls=%fused_computation.52 | convolution fusion | flops 12582912 | bytes 4268032 | tf_op jit(solution)/shard_map/bfv,bv->bf/dot_general | solution.py:33
  54.7 1.5 %collective-permute-start.8 = (f32[32,128]{1,0:T(8,128)S(1)}, f32[32,128]{1,0:T(8,128)S(1)}, u32[]{:S(2)}, u32[]{:S(2)}) collective-permute-start(f32[32,128]{1,0:T(8,128)S(1)} %pad_maximum_fusion.9), channel_id=1, source_target_pairs={{0,8},{8,16},{16,24},{24,32},{32,40},{40,48},{48,56},{56,64},{64,7... | collective-permute-start | bytes 49160 | tf_op jit(solution)/shard_map/ppermute | solution.py:18
  56.1 1.1 collective-permute-done.9
  57.3 3.4 %collective-permute-done.8 = f32[32,128]{1,0:T(8,128)S(1)} collective-permute-done((f32[32,128]{1,0:T(8,128)S(1)}, f32[32,128]{1,0:T(8,128)S(1)}, u32[]{:S(2)}, u32[]{:S(2)}) %collective-permute-start.8) | collective-permute-done | bytes 16416 | tf_op jit(solution)/shard_map/ppermute | solution.py:18
  60.7 4.7 %collective-permute-start.11 = (f32[3,32,128]{2,1,0:T(8,128)S(1)}, f32[3,32,128]{2,1,0:T(8,128)S(1)}, u32[]{:S(2)}, u32[]{:S(2)}) collective-permute-start(f32[3,32,128]{2,1,0:T(8,128)S(1)} %get-tuple-element.12), channel_id=1, source_target_pairs={{0,7},{1,0},{2,1},{3,2},{4,3},{5,4},{6,5},{7,6},{8,15},{9,8},{10,9... | collective-permute-start | bytes 147464 | tf_op jit(solution)/shard_map/ppermute | solution.py:21
  65.6 0.7 collective-permute-done.11
  67.2 4.3 %fusion.51 = f32[32,1,512]{2,1,0:T(1,128)S(1)} fusion(f32[32,64,1]{1,2,0:T(1,128)S(1)} %bitcast.109, f32[32,64,512]{2,1,0:T(8,128)} %param.8), kind=kOutput, calls=%fused_computation.109 | convolution fusion | flops 12582912 | bytes 4268032 | tf_op jit(solution)/shard_map/bfv,bf->bv/dot_general | solution.py:37
  71.5 0.7 multiply_reduce_fusion
  72.2 3.9 %stack.123 = f32[6]{0:T(128)S(1)} concatenate(f32[1]{0:T(128)} %bitcast.40, f32[1]{0:T(128)} %bitcast.41, f32[1]{0:T(128)} %bitcast.42, f32[1]{0:T(128)} %bitcast.43, f32[1]{0:T(128)} %bitcast.44, f32[1]{0:T(128)} %bitcast.48), dimensions={0} | concatenate | bytes 48 | tf_op jit(solution)/shard_map/stack | solution.py:103
  76.2 0.7 broadcast_in_dim.11
  76.8 6.8 %all-to-all-start = ((f32[8,56,128]{2,1,0:T(8,128)}), f32[8,56,128]{2,1,0:T(8,128)S(1)}, u32[]{:S(2)}, u32[]{:S(2)}) async-start(f32[8,56,128]{2,1,0:T(8,128)} %broadcast_in_dim.11), calls=%async_computation | async-start | bytes 458752 | tf_op jit(solution)/shard_map/all_to_all | solution.py:29
  83.7 6.2 %all-to-all-done = f32[8,56,128]{2,1,0:T(8,128)S(1)} async-done(((f32[8,56,128]{2,1,0:T(8,128)}), f32[8,56,128]{2,1,0:T(8,128)S(1)}, u32[]{:S(2)}, u32[]{:S(2)}) %all-to-all-start) | async-done | bytes 229408 | tf_op jit(solution)/shard_map/all_to_all | solution.py:29
  90.5 3.8 %all-to-all-start.1 = ((f32[32,1,128]{2,1,0:T(1,128)}), f32[32,1,128]{2,1,0:T(1,128)S(1)}, u32[]{:S(2)}, u32[]{:S(2)}) async-start(f32[32,1,128]{2,1,0:T(1,128)} %broadcast_in_dim.12), calls=%async_computation.1 | async-start | bytes 32768 | tf_op jit(solution)/shard_map/all_to_all | solution.py:29
  94.5 8.4 %all-to-all-done.1 = f32[32,1,128]{2,1,0:T(1,128)S(1)} async-done(((f32[32,1,128]{2,1,0:T(1,128)}), f32[32,1,128]{2,1,0:T(1,128)S(1)}, u32[]{:S(2)}, u32[]{:S(2)}) %all-to-all-start.1) | async-done | bytes 16416 | tf_op jit(solution)/shard_map/all_to_all | solution.py:29
  102.9 0.7 fusion.47
  123.5 1.2 fusion
  124.7 0.7 multiply_add_fusion
  (61 shorter events, 5.4 us)
Async XLA Ops:
  0.6 5.8 %copy-start.3 = (s32[32,27]{1,0:T(8,128)S(1)}, s32[32,27]{1,0:T(8,128)}, u32[]{:S(2)}) copy-start(s32[32,27]{1,0:T(8,128)} %param.9) | copy-start | bytes 10372
  6.4 26.9 %copy-start.1 = (f32[32,512]{1,0:T(8,128)S(1)}, f32[32,512]{1,0:T(8,128)}, u32[]{:S(2)}) copy-start(f32[32,512]{1,0:T(8,128)} %param.6) | copy-start | bytes 196612
  6.4 26.9 %copy-start.2 = (f32[32,512]{1,0:T(8,128)S(1)}, f32[32,512]{1,0:T(8,128)}, u32[]{:S(2)}) copy-start(f32[32,512]{1,0:T(8,128)} %param.7) | copy-start | bytes 196612
  6.6 9.5 %collective-permute-start.1 = (f32[32,128]{1,0:T(8,128)S(1)}, f32[32,128]{1,0:T(8,128)S(1)}, u32[]{:S(2)}, u32[]{:S(2)}) collective-permute-start(f32[32,128]{1,0:T(8,128)S(1)} %select_maximum_fusion), channel_id=1, source_target_pairs={{0,248},{8,0},{16,8},{24,16},{32,24},{40,32},{48,40},{56,48},{64,5... | collective-permute-start | bytes 49160 | tf_op jit(solution)/shard_map/ppermute | solution.py:18
  15.2 5.9 %collective-permute-start = (f32[32,128]{1,0:T(8,128)S(1)}, f32[32,128]{1,0:T(8,128)S(1)}, u32[]{:S(2)}, u32[]{:S(2)}) collective-permute-start(f32[32,128]{1,0:T(8,128)S(1)} %select_maximum_fusion), channel_id=1, source_target_pairs={{0,8},{8,16},{16,24},{24,32},{32,40},{40,48},{48,56},{56,64},{64,7... | collective-permute-start | bytes 49160 | tf_op jit(solution)/shard_map/ppermute | solution.py:18
  21.1 5.1 %collective-permute-start.3 = (f32[3,32,128]{2,1,0:T(8,128)S(1)}, f32[3,32,128]{2,1,0:T(8,128)S(1)}, u32[]{:S(2)}, u32[]{:S(2)}) collective-permute-start(f32[3,32,128]{2,1,0:T(8,128)S(1)} %get-tuple-element.16), channel_id=1, source_target_pairs={{0,7},{1,0},{2,1},{3,2},{4,3},{5,4},{6,5},{7,6},{8,15},{9,8},{10,9... | collective-permute-start | bytes 147464 | tf_op jit(solution)/shard_map/ppermute | solution.py:21
  23.3 3.0 %collective-permute-start.2 = (f32[3,32,128]{2,1,0:T(8,128)S(1)}, f32[3,32,128]{2,1,0:T(8,128)S(1)}, u32[]{:S(2)}, u32[]{:S(2)}) collective-permute-start(f32[3,32,128]{2,1,0:T(8,128)S(1)} %get-tuple-element.16), channel_id=1, source_target_pairs={{0,1},{1,2},{2,3},{3,4},{4,5},{5,6},{6,7},{7,0},{8,9},{9,10},{10,1... | collective-permute-start | bytes 147464 | tf_op jit(solution)/shard_map/ppermute | solution.py:21
  26.8 6.6 %copy-start = (f32[32,64,512]{2,1,0:T(8,128)S(1)}, f32[32,64,512]{2,1,0:T(8,128)}, u32[]{:S(2)}) copy-start(f32[32,64,512]{2,1,0:T(8,128)} %param.8) | copy-start | bytes 12582916
  37.0 2.8 %collective-permute-start.5 = (f32[32,128]{1,0:T(8,128)S(1)}, f32[32,128]{1,0:T(8,128)S(1)}, u32[]{:S(2)}, u32[]{:S(2)}) collective-permute-start(f32[32,128]{1,0:T(8,128)S(1)} %pad_maximum_fusion.8), channel_id=1, source_target_pairs={{0,248},{8,0},{16,8},{24,16},{32,24},{40,32},{48,40},{56,48},{64,5... | collective-permute-start | bytes 49160 | tf_op jit(solution)/shard_map/ppermute | solution.py:18
  37.2 6.0 %collective-permute-start.4 = (f32[32,128]{1,0:T(8,128)S(1)}, f32[32,128]{1,0:T(8,128)S(1)}, u32[]{:S(2)}, u32[]{:S(2)}) collective-permute-start(f32[32,128]{1,0:T(8,128)S(1)} %pad_maximum_fusion.8), channel_id=1, source_target_pairs={{0,8},{8,16},{16,24},{24,32},{32,40},{40,48},{48,56},{56,64},{64,7... | collective-permute-start | bytes 49160 | tf_op jit(solution)/shard_map/ppermute | solution.py:18
  43.2 5.0 %collective-permute-start.7 = (f32[3,32,128]{2,1,0:T(8,128)S(1)}, f32[3,32,128]{2,1,0:T(8,128)S(1)}, u32[]{:S(2)}, u32[]{:S(2)}) collective-permute-start(f32[3,32,128]{2,1,0:T(8,128)S(1)} %get-tuple-element.14), channel_id=1, source_target_pairs={{0,7},{1,0},{2,1},{3,2},{4,3},{5,4},{6,5},{7,6},{8,15},{9,8},{10,9... | collective-permute-start | bytes 147464 | tf_op jit(solution)/shard_map/ppermute | solution.py:21
  47.4 1.2 collective-permute-start.6
  54.6 39.8 %copy-start.4 = (s32[1024]{0:T(1024)S(1)}, s32[1024]{0:T(1024)}, u32[]{:S(2)}) copy-start(s32[1024]{0:T(1024)} %param.11) | copy-start | bytes 12292
  54.6 69.0 %copy-start.5 = (f32[64,1024]{1,0:T(8,128)S(1)}, f32[64,1024]{1,0:T(8,128)}, u32[]{:S(2)}) copy-start(f32[64,1024]{1,0:T(8,128)} %param.10) | copy-start | bytes 786436
  54.6 2.7 %collective-permute-start.9 = (f32[32,128]{1,0:T(8,128)S(1)}, f32[32,128]{1,0:T(8,128)S(1)}, u32[]{:S(2)}, u32[]{:S(2)}) collective-permute-start(f32[32,128]{1,0:T(8,128)S(1)} %pad_maximum_fusion.9), channel_id=1, source_target_pairs={{0,248},{8,0},{16,8},{24,16},{32,24},{40,32},{48,40},{56,48},{64,5... | collective-permute-start | bytes 49160 | tf_op jit(solution)/shard_map/ppermute | solution.py:18
  54.7 6.0 %collective-permute-start.8 = (f32[32,128]{1,0:T(8,128)S(1)}, f32[32,128]{1,0:T(8,128)S(1)}, u32[]{:S(2)}, u32[]{:S(2)}) collective-permute-start(f32[32,128]{1,0:T(8,128)S(1)} %pad_maximum_fusion.9), channel_id=1, source_target_pairs={{0,8},{8,16},{16,24},{24,32},{32,40},{40,48},{48,56},{56,64},{64,7... | collective-permute-start | bytes 49160 | tf_op jit(solution)/shard_map/ppermute | solution.py:18
  60.7 5.6 %collective-permute-start.11 = (f32[3,32,128]{2,1,0:T(8,128)S(1)}, f32[3,32,128]{2,1,0:T(8,128)S(1)}, u32[]{:S(2)}, u32[]{:S(2)}) collective-permute-start(f32[3,32,128]{2,1,0:T(8,128)S(1)} %get-tuple-element.12), channel_id=1, source_target_pairs={{0,7},{1,0},{2,1},{3,2},{4,3},{5,4},{6,5},{7,6},{8,15},{9,8},{10,9... | collective-permute-start | bytes 147464 | tf_op jit(solution)/shard_map/ppermute | solution.py:21
  65.4 1.2 collective-permute-start.10
  76.8 13.0 %all-to-all-start = ((f32[8,56,128]{2,1,0:T(8,128)}), f32[8,56,128]{2,1,0:T(8,128)S(1)}, u32[]{:S(2)}, u32[]{:S(2)}) async-start(f32[8,56,128]{2,1,0:T(8,128)} %broadcast_in_dim.11), calls=%async_computation | async-start | bytes 458752 | tf_op jit(solution)/shard_map/all_to_all | solution.py:29
  90.5 12.4 %all-to-all-start.1 = ((f32[32,1,128]{2,1,0:T(1,128)}), f32[32,1,128]{2,1,0:T(1,128)S(1)}, u32[]{:S(2)}, u32[]{:S(2)}) async-start(f32[32,1,128]{2,1,0:T(1,128)} %broadcast_in_dim.12), calls=%async_computation.1 | async-start | bytes 32768 | tf_op jit(solution)/shard_map/all_to_all | solution.py:29

commit v2 on v1

v2 whole, which is shorter than its diff:
```python
import functools

import jax
import jax.numpy as jnp
from jax import lax
from jax.experimental import pallas as pl
from jax.experimental.pallas import tpu as pltpu
from jax.sharding import PartitionSpec as P

ITERS = 3
SHIFT = 1.25
LANES = 128
MOMENTS = 2 * ITERS
CHUNKS = 8
VMEM = pl.BlockSpec(memory_space=pltpu.VMEM)
PARAMS = pltpu.CompilerParams(vmem_limit_bytes=24 * 1024 * 1024)
F32, BF16 = jnp.float32, jnp.bfloat16


def call(kernel, out_shape, *args, specs=None, scratch=()):
    many = isinstance(out_shape, (list, tuple))
    return pl.pallas_call(
        kernel,
        out_shape=out_shape,
        in_specs=specs or [VMEM] * len(args),
        out_specs=[VMEM] * len(out_shape) if many else VMEM,
        scratch_shapes=scratch,
        compiler_params=PARAMS,
    )(*args)


def f32(*shape):
    return jax.ShapeDtypeStruct(shape, F32)


def ring(axis, step):
    count = lax.axis_size(axis)
    return [(i, (i + step) % count) for i in range(count)]


def lane_iota(rows, lanes=LANES):
    return lax.broadcasted_iota(jnp.int32, (rows, lanes), 1)


def total(values):
    folded = values[:, :LANES]
    for start in range(LANES, values.shape[1], LANES):
        folded = folded + values[:, start : start + LANES]
    return jnp.sum(jnp.sum(folded, axis=0, keepdims=True), axis=1, keepdims=True)


def put(row, lane, value):
    return jnp.where(lane_iota(1) == lane, value, row)


def project(feature, field, columns, brick):
    product = feature * field
    folded = product[:, :LANES]
    for start in range(LANES, product.shape[1], LANES):
        folded = folded + product[:, start : start + LANES]
    column = jnp.sum(folded, axis=1, keepdims=True)
    return jnp.where(lane_iota(columns.shape[0]) == brick, column, columns)


def to_rows(columns, nrows):
    square = jnp.concatenate([columns, jnp.zeros((LANES - columns.shape[0], LANES), F32)], axis=0)
    return square.T[:nrows]


def first_kernel(features, field, neighbours, block, moments, buffer, sems):
    nrows, width, _ = features.shape
    each = nrows // CHUNKS
    copies = [
        pltpu.make_async_copy(
            features.at[pl.ds(i * each, each)], buffer.at[pl.ds(i * each, each)], sems.at[i]
        )
        for i in range(CHUNKS)
    ]
    for copy in copies:
        copy.start()
    value = field[...]
    moments[...] = put(jnp.zeros((1, LANES), F32), 0, total(value * value))
    columns = jnp.zeros((width, LANES), F32)
    for i, copy in enumerate(copies):
        copy.wait()
        for b in range(i * each, (i + 1) * each):
            columns = project(buffer[b], field[b : b + 1, :], columns, b)
    block[...] = to_rows(columns, nrows)
    block[:, width : width + neighbours.shape[1]] = neighbours[...].astype(F32)


def one_hot(block, nrows, width, slots, span, across, row_index, col_index):
    ids = block.astype(jnp.int32)
    bits = nrows.bit_length() - 1
    owner = lax.shift_right_arithmetic(ids, bits)
    offset_x = lax.shift_right_arithmetic(owner, across.bit_length() - 1) - row_index + 1
    offset_y = (owner & (across - 1)) - col_index + 1
    inside = (ids >= 0) & (offset_x >= 0) & (offset_x < 3) & (offset_y >= 0) & (offset_y < 3)
    position = jnp.where(inside, (offset_y * 3 + offset_x) * nrows + (ids & (nrows - 1)), -1)
    lanes = lane_iota(block.shape[0], span)
    out = jnp.zeros((block.shape[0], span), F32)
    for slot in range(width, width + slots):
        out = jnp.where(position[:, slot : slot + 1] == lanes, 1.0, out)
    return out.astype(BF16)


def middle_kernel(hot, index, column, out):
    out[...] = hot(column[...], row_index=index[0], col_index=index[1])


def advance(step, nrows, width, weights, around, features, diagonal, before, sums, moments, outs):
    last = step + 1 == ITERS
    parts = []
    rest = around
    for _ in range(3):
        part = rest.astype(BF16)
        rest = rest - part.astype(F32)
        parts.append(part)
    result = jnp.dot(weights, parts[0], preferred_element_type=F32)
    for part in parts[1:]:
        result = result + jnp.dot(weights, part, preferred_element_type=F32)
    turned = result.T[:width]
    lanes = lane_iota(width)
    shift = step * nrows
    moved = pltpu.roll(turned, shift, 1) if shift else turned
    sums = jnp.where((lanes >= shift) & (lanes < shift + nrows), moved, sums)
    old = before[...]
    base = (diagonal[...] - SHIFT) * old
    columns = jnp.zeros((width, LANES), F32)
    for b in range(nrows):
        second = turned[:, nrows + b : nrows + b + 1]
        image = jnp.sum(features[b] * second, axis=0, keepdims=True)
        new = base[b : b + 1, :] + image
        outs[0][b : b + 1, :] = new
        if not last:
            columns = project(features[b], new, columns, b)
    new = outs[0][...]
    moments = put(moments, 2 * step + 1, total(old * new))
    if not last:
        moments = put(moments, 2 * step + 2, total(new * new))
    return sums, moments, columns


def second_kernel(
    hot, index, left, column, right, middle, features, diagonal, before, moments,
    new, block, sums_out, moments_out, weights_out,
):
    nrows, width, _ = features.shape
    rows, cols = index[0], index[1]
    own = middle[nrows : 2 * nrows, :]
    near = [
        hot(left[...], row_index=rows, col_index=cols),
        middle[...],
        hot(right[...], row_index=rows, col_index=cols),
    ]
    near = jnp.concatenate(near, axis=0)
    twice = jnp.dot(own, near, preferred_element_type=F32).astype(BF16)
    pad = jnp.zeros((LANES - 2 * nrows, near.shape[1]), BF16)
    weights = jnp.concatenate([own, twice, pad], axis=0)
    weights_out[...] = weights
    around = jnp.concatenate([left[...], column[...], right[...]], axis=0)
    sums, moment, columns = advance(
        0, nrows, width, weights, around, features, diagonal, before,
        jnp.zeros((width, LANES), F32), moments[...], [new],
    )
    block[...] = to_rows(columns, nrows)
    sums_out[...] = sums
    moments_out[...] = moment


def third_kernel(
    left, column, right, weights, features, diagonal, before, sums, moments,
    new, block, sums_out, moments_out,
):
    nrows, width, _ = features.shape
    around = jnp.concatenate([left[...], column[...], right[...]], axis=0)
    total_sums, moment, columns = advance(
        1, nrows, width, weights[...], around, features, diagonal, before,
        sums[...], moments[...], [new],
    )
    block[...] = to_rows(columns, nrows)
    sums_out[...] = total_sums
    moments_out[...] = moment


def fourth_kernel(
    left, column, right, weights, features, diagonal, before, sums, moments,
    new, sums_out, moments_out,
):
    nrows, width, _ = features.shape
    around = jnp.concatenate([left[...], column[...], right[...]], axis=0)
    total_sums, moment, _ = advance(
        2, nrows, width, weights[...], around, features, diagonal, before,
        sums[...], moments[...], [new],
    )
    sums_out[...] = jnp.broadcast_to(total_sums[None], sums_out.shape)
    moments_out[...] = jnp.broadcast_to(moment, moments_out.shape)


def vertex_kernel(nrows, index, slab, bricks, vertex_features, out):
    across, width, _ = slab.shape
    local = bricks[...] - index[0] * across * nrows
    hot = lax.broadcasted_iota(jnp.int32, (across * nrows, local.shape[1]), 0) == local
    hot = jnp.where(hot, 1.0, 0.0).astype(BF16)
    group = LANES // nrows
    lanes = lane_iota(width)
    table = []
    for k in range(ITERS):
        tiles = []
        for start in range(0, across, group):
            tile = jnp.zeros((width, LANES), F32)
            for d in range(group):
                shift = (d - k) * nrows % LANES
                moved = pltpu.roll(slab[start + d], shift, 1) if shift else slab[start + d]
                tile = jnp.where((lanes >= d * nrows) & (lanes < (d + 1) * nrows), moved, tile)
            tiles.append(tile)
        table.append(jnp.concatenate(tiles, axis=1))
    rest = jnp.concatenate(table, axis=0)
    picked = None
    for _ in range(3):
        part = rest.astype(BF16)
        rest = rest - part.astype(F32)
        value = jnp.dot(part, hot, preferred_element_type=F32)
        picked = value if picked is None else picked + value
    for k in range(ITERS):
        product = vertex_features[...] * picked[k * width : (k + 1) * width, :]
        out[k : k + 1, :] = jnp.sum(product, axis=0, keepdims=True)


def cg_weights(mu):
    def dot(left, right):
        return sum(left[i] * right[j] * mu[i + j] for i in range(len(left)) for j in range(len(right)))

    def apply(poly):
        out = [SHIFT * p for p in poly] + [0.0]
        for i, p in enumerate(poly):
            out[i + 1] = out[i + 1] + p
        return out

    def axpy(left, scale, right):
        size = max(len(left), len(right))
        left = left + [0.0] * (size - len(left))
        return [l + scale * right[i] if i < len(right) else l for i, l in enumerate(left)]

    field, residual, direction, norm_now = [], [1.0], [1.0], mu[0]
    for step in range(ITERS):
        image = apply(direction)
        alpha = norm_now / dot(direction, image)
        field = axpy(field, alpha, direction)
        residual = axpy(residual, -alpha, image)
        if step + 1 < ITERS:
            norm_next = dot(residual, residual)
            direction = axpy(residual, norm_next / norm_now, direction)
            norm_now = norm_next
    return field, residual


def last_kernel(moments, v0, v1, v2, v3, vertices, field_out, residual_out, vertices_out):
    sums = jnp.sum(moments[...], axis=0, keepdims=True)
    field, residual = cg_weights([sums[:, i : i + 1] for i in range(MOMENTS)])
    powers = [v0[...], v1[...], v2[...], v3[...]]
    field_out[...] = sum(w * v for w, v in zip(field, powers))
    residual_out[...] = sum(w * v for w, v in zip(residual, powers))
    vertices_out[...] = sum(w * vertices[i : i + 1, :] for i, w in enumerate(field))


def neighbourhood(block):
    column = jnp.concatenate(
        [lax.ppermute(block, "gx", ring("gx", 1)), block, lax.ppermute(block, "gx", ring("gx", -1))]
    )
    return (
        lax.ppermute(column, "gy", ring("gy", 1)),
        column,
        lax.ppermute(column, "gy", ring("gy", -1)),
    )


def per_device(right_side, diagonal, features, neighbours, vertex_features, vertex_bricks):
    nrows, width, voxels = features.shape
    slots = neighbours.shape[1]
    across = lax.axis_size("gy")
    devices = across * lax.axis_size("gx")
    index = jnp.stack([lax.axis_index("gx"), lax.axis_index("gy")]).astype(jnp.int32)
    smem = pl.BlockSpec(memory_space=pltpu.SMEM)
    hot = functools.partial(
        one_hot, nrows=nrows, width=width, slots=slots, span=9 * nrows, across=across
    )
    power = f32(nrows, voxels)
    block_shape, row, table = f32(nrows, LANES), f32(1, LANES), f32(width, LANES)

    block, moments = call(
        first_kernel, [block_shape, row], features, right_side, neighbours,
        specs=[pl.BlockSpec(memory_space=pl.ANY), VMEM, VMEM],
        scratch=[pltpu.VMEM(features.shape, F32), pltpu.SemaphoreType.DMA((CHUNKS,))],
    )
    left, column, right = neighbourhood(block)
    middle = call(
        functools.partial(middle_kernel, hot),
        jax.ShapeDtypeStruct((3 * nrows, 9 * nrows), BF16), index, column, specs=[smem, VMEM],
    )
    v1, block, sums, moments, weights = call(
        functools.partial(second_kernel, hot),
        [power, block_shape, table, row, jax.ShapeDtypeStruct((LANES, 9 * nrows), BF16)],
        index, left, column, right, middle, features, diagonal, right_side, moments,
        specs=[smem] + [VMEM] * 8,
    )
    left, column, right = neighbourhood(block)
    v2, block, sums, moments = call(
        third_kernel, [power, block_shape, table, row],
        left, column, right, weights, features, diagonal, v1, sums, moments,
    )
    left, column, right = neighbourhood(block)
    v3, sums, moments = call(
        fourth_kernel, [power, f32(across, width, LANES), f32(devices, LANES)],
        left, column, right, weights, features, diagonal, v2, sums, moments,
    )
    moments = lax.all_to_all(moments, ("gx", "gy"), 0, 0, tiled=True)
    slab = lax.all_to_all(sums, "gy", 0, 0, tiled=True)
    vertices = call(
        functools.partial(vertex_kernel, nrows), f32(8, vertex_bricks.shape[0]),
        index, slab, vertex_bricks.reshape(1, -1), vertex_features, specs=[smem] + [VMEM] * 3,
    )
    field, residual, values = call(
        last_kernel, [power, power, f32(1, vertex_bricks.shape[0])],
        moments, right_side, v1, v2, v3, vertices,
    )
    return field, residual, values.reshape(-1)


def solution(mesh):
    placed = (
        P(("gx", "gy"), None),
        P(("gx", "gy"), None),
        P(("gx", "gy"), None, None),
        P(("gx", "gy"), None),
        P(None, ("gx", "gy")),
        P(("gx", "gy")),
    )
    return jax.shard_map(
        per_device,
        mesh=mesh,
        in_specs=placed,
        out_specs=(P(("gx", "gy"), None), P(("gx", "gy"), None), P(("gx", "gy"))),
        check_vma=False,
    )
```

time: 126 us -> 93.7 us (0.74)
  matrix products: 26.5 us -> 0 us
  between operations: 20.8 us -> 0.76 us
  Pallas kernels: 0 us -> 15.4 us
  waiting for transfers between devices: 32.9 us -> 17.9 us
  blocking collectives: 0 us -> 12.4 us
  starting transfers between devices: 34.7 us -> 40.9 us
  other arithmetic: 4.24 us -> 0.07 us
    dot_general x14 -> x0, matrix products: 26.5 us -> none  [the longest x3 13 us: coefficient(): return jnp.einsum('bfv,bv->bf', features, field, precision=HIGHEST)]
    pallas_call x0 -> x7, Pallas kernels: none -> 15.4 us  [call(): pl.pallas_call(kernel, out_shape=out_shape, in_specs=specs or [VMEM] * le...]
    all_to_all x0 -> x1, blocking collectives: none -> 12.4 us  [per_device(): slab = lax.all_to_all(sums, 'gy', 0, 0, tiled=True)]
    ppermute x12, waiting for transfers between devices: 18.3 us -> 6.1 us  [the longest x3 3.12 us: neighbourhood(): lax.ppermute(block, 'gx', ring('gx', 1))]
    ppermute x12, starting transfers between devices: 24 us -> 30.5 us  [the longest x3 16.9 us: neighbourhood(): lax.ppermute(block, 'gx', ring('gx', -1))]
    unnamed x12 -> x22, local copies, waits for them, and re-layouts: 0.03 us -> 5.95 us
    another operation x3 -> x0, local copies, waits for them, and re-layouts: 3.92 us -> none  [the longest x1 3.9 us: per_device(): part = jnp.pad(jnp.stack(moments), (0, 128 - len(moments)))]
    all_to_all x2 -> x1, waiting for transfers between devices: 14.6 us -> 11.8 us  [per_device(): moments = lax.all_to_all(moments, ('gx', 'gy'), 0, 0, tiled=True)]
  transfers between devices with their start and end apart: 14 -> 13, of which waited for: 13 -> 9; matrix products, arithmetic and copies ran while one was open for 1% -> 0% of each run, Pallas kernels for 0% -> 3%
where the time goes in v2:
time: 93.7 us; the launch traced here: 93.3 us
  starting transfers between devices  40.9 us (44%)
  waiting for transfers between devices  17.9 us (19%)
  Pallas kernels  15.4 us (16%)
  blocking collectives  12.4 us (13%)
  local copies, waits for them, and re-layouts  5.96 us (6%)
    ppermute x3, starting transfers between devices, neighbourhood(): lax.ppermute(block, 'gx', ring('gx', -1))  16.9 us
    pallas_call x7, Pallas kernels, call(): pl.pallas_call(kernel, out_shape=out_shape, in_specs=specs or [VMEM] * le...  15.4 us
    all_to_all x1, blocking collectives, per_device(): slab = lax.all_to_all(sums, 'gy', 0, 0, tiled=True)  12.4 us
    all_to_all x1, waiting for transfers between devices, per_device(): moments = lax.all_to_all(moments, ('gx', 'gy'), 0, 0, tiled=True)  11.8 us
    all_to_all x1, starting transfers between devices, per_device(): moments = lax.all_to_all(moments, ('gx', 'gy'), 0, 0, tiled=True)  10.4 us
    ppermute x3, starting transfers between devices, neighbourhood(): lax.ppermute(column, 'gy', ring('gy', -1))  10.2 us
    unnamed x22, local copies, waits for them, and re-layouts  5.95 us
    ppermute x3, waiting for transfers between devices, neighbourhood(): lax.ppermute(block, 'gx', ring('gx', 1))  3.12 us
  transfers between devices with their start and end apart: 13, of which 9 were waited for; matrix products, arithmetic and copies ran while one was open for 0% of the time, Pallas kernels for 3%

profile of v2, /device:TPU:1, one launch (start us, length us, event | category | flops | bytes accessed | tf_op | source)
XLA Modules:
  0.0 93.3 jit_solution(78455866608488274)
XLA Ops:
  0.6 2.2 %copy-done = f32[32,64,512]{2,1,0:T(8,128)S(1)} copy-done((f32[32,64,512]{2,1,0:T(8,128)S(1)}, f32[32,64,512]{2,1,0:T(8,128)}, u32[]{:S(2)}) %copy-start) | copy-done | bytes 4194328
  2.8 0.8 copy-done.3
  3.7 0.7 copy-done.6
  4.4 1.4 %shard_map.85 = (f32[32,128]{1,0:T(8,128)S(1)}, f32[1,128]{1,0:T(1,128)S(1)}) custom-call(f32[32,64,512]{2,1,0:T(8,128)S(1)} %copy-done, f32[32,512]{1,0:T(8,128)S(1)} %copy-done.3, s32[32,27]{1,0:T(8,128)S(1)} %copy-done.6), custom_call_target="tpu_custom_call" | custom-call | tf_op jit(solution)/shard_map/pallas_call | solution.py:22
  5.8 2.1 %collective-permute-start = (f32[32,128]{1,0:T(8,128)S(1)}, f32[32,128]{1,0:T(8,128)S(1)}, u32[]{:S(2)}, u32[]{:S(2)}) collective-permute-start(f32[32,128]{1,0:T(8,128)S(1)} %get-tuple-element.20), channel_id=1, source_target_pairs={{0,8},{8,16},{16,24},{24,32},{32,40},{40,48},{48,56},{56,64},{64,7... | collective-permute-start | bytes 49160 | tf_op jit(solution)/shard_map/ppermute | solution.py:269
  7.9 6.6 %collective-permute-start.1 = (f32[32,128]{1,0:T(8,128)S(1)}, f32[32,128]{1,0:T(8,128)S(1)}, u32[]{:S(2)}, u32[]{:S(2)}) collective-permute-start(f32[32,128]{1,0:T(8,128)S(1)} %get-tuple-element.20), channel_id=1, source_target_pairs={{0,248},{8,0},{16,8},{24,16},{32,24},{40,32},{48,40},{56,48},{64,5... | collective-permute-start | bytes 49160 | tf_op jit(solution)/shard_map/ppermute | solution.py:269
  14.6 1.0 %collective-permute-done = f32[32,128]{1,0:T(8,128)S(1)} collective-permute-done((f32[32,128]{1,0:T(8,128)S(1)}, f32[32,128]{1,0:T(8,128)S(1)}, u32[]{:S(2)}, u32[]{:S(2)}) %collective-permute-start) | collective-permute-done | bytes 16416 | tf_op jit(solution)/shard_map/ppermute | solution.py:269
  15.6 1.6 %collective-permute-start.3 = (f32[96,128]{1,0:T(8,128)S(1)}, f32[96,128]{1,0:T(8,128)S(1)}, u32[]{:S(2)}, u32[]{:S(2)}) collective-permute-start(f32[96,128]{1,0:T(8,128)S(1)} %constant_dynamic-update-slice_fusion.column), channel_id=1, source_target_pairs={{0,7},{1,0},{2,1},{3,2},{4,3},{5,4},{6,5},{7,6},{8,15},{9,8},{10,9... | collective-permute-start | bytes 147464 | tf_op jit(solution)/shard_map/ppermute | solution.py:274
  17.2 1.2 %collective-permute-start.2 = (f32[96,128]{1,0:T(8,128)S(1)}, f32[96,128]{1,0:T(8,128)S(1)}, u32[]{:S(2)}, u32[]{:S(2)}) collective-permute-start(f32[96,128]{1,0:T(8,128)S(1)} %constant_dynamic-update-slice_fusion.column), channel_id=1, source_target_pairs={{0,1},{1,2},{2,3},{3,4},{4,5},{5,6},{6,7},{7,0},{8,9},{9,10},{10,1... | collective-permute-start | bytes 147464 | tf_op jit(solution)/shard_map/ppermute | solution.py:272
  18.4 0.1 pad_add_fusion.index
  18.5 1.2 %shard_map.86.middle = bf16[96,288]{1,0:T(8,128)(2,1)S(1)} custom-call(s32[2]{0:T(128)S(1)} %pad_add_fusion.index, f32[96,128]{1,0:T(8,128)S(1)} %constant_dynamic-update-slice_fusion.column), custom_call_target="tpu_custom_call" | custom-call | tf_op jit(solution)/shard_map/pallas_call | solution.py:22
  19.6 0.5 collective-permute-done.3.right
  20.2 2.2 %copy-done.1 = f32[32,64,512]{2,1,0:T(8,128)S(1)} copy-done((f32[32,64,512]{2,1,0:T(8,128)S(1)}, f32[32,64,512]{2,1,0:T(8,128)}, u32[]{:S(2)}) %copy-start.1) | copy-done | bytes 4194328
  22.4 5.7 %shard_map.87 = (f32[32,512]{1,0:T(8,128)S(1)}, f32[32,128]{1,0:T(8,128)S(1)}, f32[64,128]{1,0:T(8,128)S(1)}, f32[1,128]{1,0:T(1,128)S(1)}, bf16[128,288]{1,0:T(8,128)(2,1)S(1)}) custom-call(s32[2]{0:T(128)S(1)} %pad_add_fusion.index, f32[96,128]{1,0:T(8,128)S(1)} %collective-permute-done.2.left, f32[96,128]{1,0:T(8,128)S(1)} %constant_dynamic-update-slice_fusion.column, ...), custom_call_target="tpu_custom_call" | custom-call | tf_op jit(solution)/shard_map/pallas_call | solution.py:22
  28.0 0.0 collective-permute-start.4
  28.1 5.2 %collective-permute-start.5 = (f32[32,128]{1,0:T(8,128)S(1)}, f32[32,128]{1,0:T(8,128)S(1)}, u32[]{:S(2)}, u32[]{:S(2)}) collective-permute-start(f32[32,128]{1,0:T(8,128)S(1)} %get-tuple-element.22), channel_id=1, source_target_pairs={{0,248},{8,0},{16,8},{24,16},{32,24},{40,32},{48,40},{56,48},{64,5... | collective-permute-start | bytes 49160 | tf_op jit(solution)/shard_map/ppermute | solution.py:269
  33.3 1.0 %collective-permute-done.4 = f32[32,128]{1,0:T(8,128)S(1)} collective-permute-done((f32[32,128]{1,0:T(8,128)S(1)}, f32[32,128]{1,0:T(8,128)S(1)}, u32[]{:S(2)}, u32[]{:S(2)}) %collective-permute-start.4) | collective-permute-done | bytes 16416 | tf_op jit(solution)/shard_map/ppermute | solution.py:269
  34.3 4.2 %collective-permute-start.7 = (f32[96,128]{1,0:T(8,128)S(1)}, f32[96,128]{1,0:T(8,128)S(1)}, u32[]{:S(2)}, u32[]{:S(2)}) collective-permute-start(f32[96,128]{1,0:T(8,128)S(1)} %constant_dynamic-update-slice_fusion.3.column), channel_id=1, source_target_pairs={{0,7},{1,0},{2,1},{3,2},{4,3},{5,4},{6,5},{7,6},{8,15},{9,8},{10,9... | collective-permute-start | bytes 147464 | tf_op jit(solution)/shard_map/ppermute | solution.py:274
  38.5 0.9 collective-permute-done.7.right
  39.4 0.3 collective-permute-done.6.left
  39.7 3.3 %shard_map.88 = (f32[32,512]{1,0:T(8,128)S(1)}, f32[32,128]{1,0:T(8,128)S(1)}, f32[64,128]{1,0:T(8,128)S(1)}, f32[1,128]{1,0:T(1,128)S(1)}) custom-call(f32[96,128]{1,0:T(8,128)S(1)} %collective-permute-done.6.left, f32[96,128]{1,0:T(8,128)S(1)} %constant_dynamic-update-slice_fusion.3.column, f32[96,128]{1,0:T(8,128)S(1)} %collective-permute-done.7.right, ...), custom_call_target="tpu_custom_call" | custom-call | tf_op jit(solution)/shard_map/pallas_call | solution.py:22
  43.1 5.1 %collective-permute-start.9 = (f32[32,128]{1,0:T(8,128)S(1)}, f32[32,128]{1,0:T(8,128)S(1)}, u32[]{:S(2)}, u32[]{:S(2)}) collective-permute-start(f32[32,128]{1,0:T(8,128)S(1)} %get-tuple-element.27), channel_id=1, source_target_pairs={{0,248},{8,0},{16,8},{24,16},{32,24},{40,32},{48,40},{56,48},{64,5... | collective-permute-start | bytes 49160 | tf_op jit(solution)/shard_map/ppermute | solution.py:269
  48.2 1.0 %collective-permute-done.8 = f32[32,128]{1,0:T(8,128)S(1)} collective-permute-done((f32[32,128]{1,0:T(8,128)S(1)}, f32[32,128]{1,0:T(8,128)S(1)}, u32[]{:S(2)}, u32[]{:S(2)}) %collective-permute-start.8) | collective-permute-done | bytes 16416 | tf_op jit(solution)/shard_map/ppermute | solution.py:269
  49.3 4.4 %collective-permute-start.11 = (f32[96,128]{1,0:T(8,128)S(1)}, f32[96,128]{1,0:T(8,128)S(1)}, u32[]{:S(2)}, u32[]{:S(2)}) collective-permute-start(f32[96,128]{1,0:T(8,128)S(1)} %constant_dynamic-update-slice_fusion.6.column), channel_id=1, source_target_pairs={{0,7},{1,0},{2,1},{3,2},{4,3},{5,4},{6,5},{7,6},{8,15},{9,8},{10,9... | collective-permute-start | bytes 147464 | tf_op jit(solution)/shard_map/ppermute | solution.py:274
  53.7 0.9 collective-permute-done.11.right
  54.6 0.3 collective-permute-done.10.left
  55.0 1.7 %shard_map.89 = (f32[32,512]{1,0:T(8,128)S(1)}, f32[8,64,128]{2,1,0:T(8,128)S(1)}, f32[256,128]{1,0:T(8,128)}) custom-call(f32[96,128]{1,0:T(8,128)S(1)} %collective-permute-done.10.left, f32[96,128]{1,0:T(8,128)S(1)} %constant_dynamic-update-slice_fusion.6.column, f32[96,128]{1,0:T(8,128)S(1)} %collective-permute-done.11.right, ...), custom_call_target="tpu_custom_call" | custom-call | tf_op jit(solution)/shard_map/pallas_call | solution.py:22
  56.7 12.4 %all_to_all.16.slab = f32[8,64,128]{2,1,0:T(8,128)S(1)} all-to-all(f32[8,64,128]{2,1,0:T(8,128)S(1)} %get-tuple-element.33), channel_id=1, replica_groups=mesh['gx'=32,'gy'=8] {'gy'}, dimensions={0} | all-to-all | bytes 524288 | tf_op jit(solution)/shard_map/all_to_all | solution.py:318
  69.1 10.4 %all-to-all-start = ((f32[256,1,128]{2,1,0:T(1,128)}), f32[256,1,128]{2,1,0:T(1,128)S(1)}, u32[]{:S(2)}, u32[]{:S(2)}) async-start(f32[256,1,128]{2,1,0:T(1,128)} %bitcast.3), calls=%async_computation | async-start | bytes 262144 | tf_op jit(solution)/shard_map/all_to_all | solution.py:317
  79.5 1.2 %shard_map.90.vertices = f32[8,1024]{1,0:T(8,128)S(1)} custom-call(s32[2]{0:T(128)S(1)} %pad_add_fusion.index, f32[8,64,128]{2,1,0:T(8,128)S(1)} %all_to_all.16.slab, s32[1,1024]{1,0:T(1,128)S(1)} %bitcast.9, f32[64,1024]{1,0:T(8,128)S(1)} %copy-done.5), custom_call_target="tpu_custom_call" | custom-call | tf_op jit(solution)/shard_map/pallas_call | solution.py:22
  80.7 11.8 %all-to-all-done = f32[256,1,128]{2,1,0:T(1,128)S(1)} async-done(((f32[256,1,128]{2,1,0:T(1,128)}), f32[256,1,128]{2,1,0:T(1,128)S(1)}, u32[]{:S(2)}, u32[]{:S(2)}) %all-to-all-start) | async-done | bytes 131104 | tf_op jit(solution)/shard_map/all_to_all | solution.py:317
  92.4 0.9 shard_map.91
  (28 shorter events, 0.1 us)
Async XLA Ops:
  0.6 2.2 %copy-start = (f32[32,64,512]{2,1,0:T(8,128)S(1)}, f32[32,64,512]{2,1,0:T(8,128)}, u32[]{:S(2)}) copy-start(f32[32,64,512]{2,1,0:T(8,128)} %features.7) | copy-start | bytes 12582916
  2.8 0.8 copy-start.3
  3.7 0.7 copy-start.6
  4.4 15.8 %copy-start.2 = (f32[32,512]{1,0:T(8,128)S(1)}, f32[32,512]{1,0:T(8,128)}, u32[]{:S(2)}) copy-start(f32[32,512]{1,0:T(8,128)} %diagonal.5) | copy-start | bytes 196612
  4.4 15.8 %copy-start.4 = (f32[32,512]{1,0:T(8,128)S(1)}, f32[32,512]{1,0:T(8,128)}, u32[]{:S(2)}) copy-start(f32[32,512]{1,0:T(8,128)} %v0.1) | copy-start | bytes 196612
  5.8 9.8 %collective-permute-start = (f32[32,128]{1,0:T(8,128)S(1)}, f32[32,128]{1,0:T(8,128)S(1)}, u32[]{:S(2)}, u32[]{:S(2)}) collective-permute-start(f32[32,128]{1,0:T(8,128)S(1)} %get-tuple-element.20), channel_id=1, source_target_pairs={{0,8},{8,16},{16,24},{24,32},{32,40},{40,48},{48,56},{56,64},{64,7... | collective-permute-start | bytes 49160 | tf_op jit(solution)/shard_map/ppermute | solution.py:269
  7.9 7.7 %collective-permute-start.1 = (f32[32,128]{1,0:T(8,128)S(1)}, f32[32,128]{1,0:T(8,128)S(1)}, u32[]{:S(2)}, u32[]{:S(2)}) collective-permute-start(f32[32,128]{1,0:T(8,128)S(1)} %get-tuple-element.20), channel_id=1, source_target_pairs={{0,248},{8,0},{16,8},{24,16},{32,24},{40,32},{48,40},{56,48},{64,5... | collective-permute-start | bytes 49160 | tf_op jit(solution)/shard_map/ppermute | solution.py:269
  15.6 4.5 %collective-permute-start.3 = (f32[96,128]{1,0:T(8,128)S(1)}, f32[96,128]{1,0:T(8,128)S(1)}, u32[]{:S(2)}, u32[]{:S(2)}) collective-permute-start(f32[96,128]{1,0:T(8,128)S(1)} %constant_dynamic-update-slice_fusion.column), channel_id=1, source_target_pairs={{0,7},{1,0},{2,1},{3,2},{4,3},{5,4},{6,5},{7,6},{8,15},{9,8},{10,9... | collective-permute-start | bytes 147464 | tf_op jit(solution)/shard_map/ppermute | solution.py:274
  17.2 3.0 %collective-permute-start.2 = (f32[96,128]{1,0:T(8,128)S(1)}, f32[96,128]{1,0:T(8,128)S(1)}, u32[]{:S(2)}, u32[]{:S(2)}) collective-permute-start(f32[96,128]{1,0:T(8,128)S(1)} %constant_dynamic-update-slice_fusion.column), channel_id=1, source_target_pairs={{0,1},{1,2},{2,3},{3,4},{4,5},{5,6},{6,7},{7,0},{8,9},{9,10},{10,1... | collective-permute-start | bytes 147464 | tf_op jit(solution)/shard_map/ppermute | solution.py:272
  20.2 2.2 %copy-start.1 = (f32[32,64,512]{2,1,0:T(8,128)S(1)}, f32[32,64,512]{2,1,0:T(8,128)}, u32[]{:S(2)}) copy-start(f32[32,64,512]{2,1,0:T(8,128)} %features.7) | copy-start | bytes 12582916
  28.0 6.3 %collective-permute-start.4 = (f32[32,128]{1,0:T(8,128)S(1)}, f32[32,128]{1,0:T(8,128)S(1)}, u32[]{:S(2)}, u32[]{:S(2)}) collective-permute-start(f32[32,128]{1,0:T(8,128)S(1)} %get-tuple-element.22), channel_id=1, source_target_pairs={{0,8},{8,16},{16,24},{24,32},{32,40},{40,48},{48,56},{56,64},{64,7... | collective-permute-start | bytes 49160 | tf_op jit(solution)/shard_map/ppermute | solution.py:269
  28.1 6.2 %collective-permute-start.5 = (f32[32,128]{1,0:T(8,128)S(1)}, f32[32,128]{1,0:T(8,128)S(1)}, u32[]{:S(2)}, u32[]{:S(2)}) collective-permute-start(f32[32,128]{1,0:T(8,128)S(1)} %get-tuple-element.22), channel_id=1, source_target_pairs={{0,248},{8,0},{16,8},{24,16},{32,24},{40,32},{48,40},{56,48},{64,5... | collective-permute-start | bytes 49160 | tf_op jit(solution)/shard_map/ppermute | solution.py:269
  34.3 5.1 %collective-permute-start.7 = (f32[96,128]{1,0:T(8,128)S(1)}, f32[96,128]{1,0:T(8,128)S(1)}, u32[]{:S(2)}, u32[]{:S(2)}) collective-permute-start(f32[96,128]{1,0:T(8,128)S(1)} %constant_dynamic-update-slice_fusion.3.column), channel_id=1, source_target_pairs={{0,7},{1,0},{2,1},{3,2},{4,3},{5,4},{6,5},{7,6},{8,15},{9,8},{10,9... | collective-permute-start | bytes 147464 | tf_op jit(solution)/shard_map/ppermute | solution.py:274
  38.5 1.2 %collective-permute-start.6 = (f32[96,128]{1,0:T(8,128)S(1)}, f32[96,128]{1,0:T(8,128)S(1)}, u32[]{:S(2)}, u32[]{:S(2)}) collective-permute-start(f32[96,128]{1,0:T(8,128)S(1)} %constant_dynamic-update-slice_fusion.3.column), channel_id=1, source_target_pairs={{0,1},{1,2},{2,3},{3,4},{4,5},{5,6},{6,7},{7,0},{8,9},{9,10},{10,1... | collective-permute-start | bytes 147464 | tf_op jit(solution)/shard_map/ppermute | solution.py:272
  39.7 39.7 %copy-start.5 = (f32[64,1024]{1,0:T(8,128)S(1)}, f32[64,1024]{1,0:T(8,128)}, u32[]{:S(2)}) copy-start(f32[64,1024]{1,0:T(8,128)} %vertex_features.1) | copy-start | bytes 786436
  39.7 39.7 %copy-start.7 = (s32[1024]{0:T(1024)S(1)}, s32[1024]{0:T(1024)}, u32[]{:S(2)}) copy-start(s32[1024]{0:T(1024)} %param.11) | copy-start | bytes 12292
  43.1 6.2 %collective-permute-start.8 = (f32[32,128]{1,0:T(8,128)S(1)}, f32[32,128]{1,0:T(8,128)S(1)}, u32[]{:S(2)}, u32[]{:S(2)}) collective-permute-start(f32[32,128]{1,0:T(8,128)S(1)} %get-tuple-element.27), channel_id=1, source_target_pairs={{0,8},{8,16},{16,24},{24,32},{32,40},{40,48},{48,56},{56,64},{64,7... | collective-permute-start | bytes 49160 | tf_op jit(solution)/shard_map/ppermute | solution.py:269
  43.1 6.2 %collective-permute-start.9 = (f32[32,128]{1,0:T(8,128)S(1)}, f32[32,128]{1,0:T(8,128)S(1)}, u32[]{:S(2)}, u32[]{:S(2)}) collective-permute-start(f32[32,128]{1,0:T(8,128)S(1)} %get-tuple-element.27), channel_id=1, source_target_pairs={{0,248},{8,0},{16,8},{24,16},{32,24},{40,32},{48,40},{56,48},{64,5... | collective-permute-start | bytes 49160 | tf_op jit(solution)/shard_map/ppermute | solution.py:269
  49.3 5.3 %collective-permute-start.11 = (f32[96,128]{1,0:T(8,128)S(1)}, f32[96,128]{1,0:T(8,128)S(1)}, u32[]{:S(2)}, u32[]{:S(2)}) collective-permute-start(f32[96,128]{1,0:T(8,128)S(1)} %constant_dynamic-update-slice_fusion.6.column), channel_id=1, source_target_pairs={{0,7},{1,0},{2,1},{3,2},{4,3},{5,4},{6,5},{7,6},{8,15},{9,8},{10,9... | collective-permute-start | bytes 147464 | tf_op jit(solution)/shard_map/ppermute | solution.py:274
  53.7 1.2 %collective-permute-start.10 = (f32[96,128]{1,0:T(8,128)S(1)}, f32[96,128]{1,0:T(8,128)S(1)}, u32[]{:S(2)}, u32[]{:S(2)}) collective-permute-start(f32[96,128]{1,0:T(8,128)S(1)} %constant_dynamic-update-slice_fusion.6.column), channel_id=1, source_target_pairs={{0,1},{1,2},{2,3},{3,4},{4,5},{5,6},{6,7},{7,0},{8,9},{9,10},{10,1... | collective-permute-start | bytes 147464 | tf_op jit(solution)/shard_map/ppermute | solution.py:272
  69.1 23.4 %all-to-all-start = ((f32[256,1,128]{2,1,0:T(1,128)}), f32[256,1,128]{2,1,0:T(1,128)S(1)}, u32[]{:S(2)}, u32[]{:S(2)}) async-start(f32[256,1,128]{2,1,0:T(1,128)} %bitcast.3), calls=%async_computation | async-start | bytes 262144 | tf_op jit(solution)/shard_map/all_to_all | solution.py:317

commit v3 on v2

--- a/solution.py
+++ b/solution.py
@@ -12,12 +12,13 @@
 LANES = 128
 MOMENTS = 2 * ITERS
 CHUNKS = 8
+MOMENT_LANE = 96
+FIRST_LIMIT = 60
 VMEM = pl.BlockSpec(memory_space=pltpu.VMEM)
-PARAMS = pltpu.CompilerParams(vmem_limit_bytes=24 * 1024 * 1024)
 F32, BF16 = jnp.float32, jnp.bfloat16
 
 
-def call(kernel, out_shape, *args, specs=None, scratch=()):
+def call(kernel, out_shape, *args, specs=None, scratch=(), limit=24):
     many = isinstance(out_shape, (list, tuple))
     return pl.pallas_call(
         kernel,
@@ -25,7 +26,7 @@
         in_specs=specs or [VMEM] * len(args),
         out_specs=[VMEM] * len(out_shape) if many else VMEM,
         scratch_shapes=scratch,
-        compiler_params=PARAMS,
+        compiler_params=pltpu.CompilerParams(vmem_limit_bytes=limit * 1024 * 1024),
     )(*args)
 
 
@@ -67,7 +68,7 @@
     return square.T[:nrows]
 
 
-def first_kernel(features, field, neighbours, block, moments, buffer, sems):
+def first_kernel(features, field, neighbours, block, moments, values, ids, buffer, sems):
     nrows, width, _ = features.shape
     each = nrows // CHUNKS
     copies = [
@@ -76,36 +77,58 @@
         )
         for i in range(CHUNKS)
     ]
-    for copy in copies:
+    small = [
+        pltpu.make_async_copy(field, values, sems.at[CHUNKS]),
+        pltpu.make_async_copy(neighbours, ids, sems.at[CHUNKS + 1]),
+    ]
+    for copy in small + copies:
         copy.start()
-    value = field[...]
-    moments[...] = put(jnp.zeros((1, LANES), F32), 0, total(value * value))
+    for copy in small:
+        copy.wait()
+    value = values[...]
+    moments[...] = put(jnp.zeros((1, LANES), F32), MOMENT_LANE, total(value * value))
     columns = jnp.zeros((width, LANES), F32)
     for i, copy in enumerate(copies):
         copy.wait()
         for b in range(i * each, (i + 1) * each):
-            columns = project(buffer[b], field[b : b + 1, :], columns, b)
+            columns = project(buffer[b], values[b : b + 1, :], columns, b)
     block[...] = to_rows(columns, nrows)
-    block[:, width : width + neighbours.shape[1]] = neighbours[...].astype(F32)
-
-
-def one_hot(block, nrows, width, slots, span, across, row_index, col_index):
+    block[:, width : width + neighbours.shape[1]] = ids[...].astype(F32)
+
+
+def positions(block, nrows, across, row_index, col_index):
     ids = block.astype(jnp.int32)
-    bits = nrows.bit_length() - 1
-    owner = lax.shift_right_arithmetic(ids, bits)
+    owner = lax.shift_right_arithmetic(ids, nrows.bit_length() - 1)
     offset_x = lax.shift_right_arithmetic(owner, across.bit_length() - 1) - row_index + 1
     offset_y = (owner & (across - 1)) - col_index + 1
     inside = (ids >= 0) & (offset_x >= 0) & (offset_x < 3) & (offset_y >= 0) & (offset_y < 3)
-    position = jnp.where(inside, (offset_y * 3 + offset_x) * nrows + (ids & (nrows - 1)), -1)
-    lanes = lane_iota(block.shape[0], span)
-    out = jnp.zeros((block.shape[0], span), F32)
+    return jnp.where(inside, offset_y * LANES + offset_x * nrows + (ids & (nrows - 1)), -1)
+
+
+def one_hot(position, first, lanes, width, slots):
+    targets = lane_iota(position.shape[0], lanes) + first
+    out = jnp.zeros((position.shape[0], lanes), F32)
     for slot in range(width, width + slots):
-        out = jnp.where(position[:, slot : slot + 1] == lanes, 1.0, out)
+        out = jnp.where(position[:, slot : slot + 1] == targets, 1.0, out)
     return out.astype(BF16)
 
 
-def middle_kernel(hot, index, column, out):
-    out[...] = hot(column[...], row_index=index[0], col_index=index[1])
+def padded(third):
+    return jnp.concatenate([third, jnp.zeros((LANES - third.shape[0], third.shape[1]), third.dtype)])
+
+
+def own_kernel(shape, index, block, features, out):
+    nrows, width, slots, across = shape
+    place = positions(block[...], nrows, across, index[0], index[1])
+    out[...] = one_hot(place, 0, 3 * LANES, width, slots)
+
+
+def middle_kernel(shape, index, column, own, out):
+    nrows, width, slots, across = shape
+    others = jnp.concatenate([column[:nrows, :], column[2 * nrows :, :]], axis=0)
+    place = positions(others, nrows, across, index[0], index[1])
+    hot = one_hot(place, 0, 3 * LANES, width, slots)
+    out[...] = padded(jnp.concatenate([hot[:nrows], own[...], hot[nrows:]], axis=0))
 
 
 def advance(step, nrows, width, weights, around, features, diagonal, before, sums, moments, outs):
@@ -135,30 +158,34 @@
         if not last:
             columns = project(features[b], new, columns, b)
     new = outs[0][...]
-    moments = put(moments, 2 * step + 1, total(old * new))
+    moments = put(moments, MOMENT_LANE + 2 * step + 1, total(old * new))
     if not last:
-        moments = put(moments, 2 * step + 2, total(new * new))
+        moments = put(moments, MOMENT_LANE + 2 * step + 2, total(new * new))
     return sums, moments, columns
 
 
 def second_kernel(
-    hot, index, left, column, right, middle, features, diagonal, before, moments,
+    shape, index, left, column, right, middle, features, diagonal, before, moments,
     new, block, sums_out, moments_out, weights_out,
 ):
-    nrows, width, _ = features.shape
-    rows, cols = index[0], index[1]
+    nrows, width, slots, across = shape
     own = middle[nrows : 2 * nrows, :]
-    near = [
-        hot(left[...], row_index=rows, col_index=cols),
-        middle[...],
-        hot(right[...], row_index=rows, col_index=cols),
-    ]
-    near = jnp.concatenate(near, axis=0)
-    twice = jnp.dot(own, near, preferred_element_type=F32).astype(BF16)
-    pad = jnp.zeros((LANES - 2 * nrows, near.shape[1]), BF16)
+    pieces = [own[:, d * LANES : (d + 1) * LANES] for d in range(3)]
+    centre = middle[...]
+    thirds = [jnp.dot(pieces[1], centre[:, d * LANES : (d + 1) * LANES], preferred_element_type=F32) for d in range(3)]
+    for d, side in ((0, left), (2, right)):
+        place = positions(side[...], nrows, across, index[0], index[1])
+        hot = padded(one_hot(place, d * LANES, LANES, width, slots))
+        thirds[d] = thirds[d] + jnp.dot(pieces[d], hot, preferred_element_type=F32)
+        across_dy = centre[:, d * LANES : (d + 1) * LANES]
+        thirds[1] = thirds[1] + lax.dot_general(
+            pieces[d], across_dy, (((1,), (1,)), ((), ())), preferred_element_type=F32
+        )
+    twice = jnp.concatenate(thirds, axis=1).astype(BF16)
+    pad = jnp.zeros((LANES - 2 * nrows, 3 * LANES), BF16)
     weights = jnp.concatenate([own, twice, pad], axis=0)
     weights_out[...] = weights
-    around = jnp.concatenate([left[...], column[...], right[...]], axis=0)
+    around = jnp.concatenate([padded(side[...]) for side in (left, column, right)], axis=0)
     sums, moment, columns = advance(
         0, nrows, width, weights, around, features, diagonal, before,
         jnp.zeros((width, LANES), F32), moments[...], [new],
@@ -173,7 +200,7 @@
     new, block, sums_out, moments_out,
 ):
     nrows, width, _ = features.shape
-    around = jnp.concatenate([left[...], column[...], right[...]], axis=0)
+    around = jnp.concatenate([padded(side[...]) for side in (left, column, right)], axis=0)
     total_sums, moment, columns = advance(
         1, nrows, width, weights[...], around, features, diagonal, before,
         sums[...], moments[...], [new],
@@ -185,16 +212,24 @@
 
 def fourth_kernel(
     left, column, right, weights, features, diagonal, before, sums, moments,
-    new, sums_out, moments_out,
+    new, sums_out,
 ):
     nrows, width, _ = features.shape
-    around = jnp.concatenate([left[...], column[...], right[...]], axis=0)
+    around = jnp.concatenate([padded(side[...]) for side in (left, column, right)], axis=0)
     total_sums, moment, _ = advance(
         2, nrows, width, weights[...], around, features, diagonal, before,
         sums[...], moments[...], [new],
     )
-    sums_out[...] = jnp.broadcast_to(total_sums[None], sums_out.shape)
-    moments_out[...] = jnp.broadcast_to(moment, moments_out.shape)
+    rows = lax.broadcasted_iota(jnp.int32, total_sums.shape, 0)
+    mixed = total_sums + jnp.where(rows == 0, moment, 0.0)
+    sums_out[...] = jnp.broadcast_to(mixed[None], sums_out.shape)
+
+
+def fold_kernel(slab, out):
+    row = slab[0, 0:1, :]
+    for d in range(1, slab.shape[0]):
+        row = row + slab[d, 0:1, :]
+    out[...] = jnp.broadcast_to(row, out.shape)
 
 
 def vertex_kernel(nrows, index, slab, bricks, vertex_features, out):
@@ -257,7 +292,7 @@
 
 def last_kernel(moments, v0, v1, v2, v3, vertices, field_out, residual_out, vertices_out):
     sums = jnp.sum(moments[...], axis=0, keepdims=True)
-    field, residual = cg_weights([sums[:, i : i + 1] for i in range(MOMENTS)])
+    field, residual = cg_weights([sums[:, MOMENT_LANE + i : MOMENT_LANE + i + 1] for i in range(MOMENTS)])
     powers = [v0[...], v1[...], v2[...], v3[...]]
     field_out[...] = sum(w * v for w, v in zip(field, powers))
     residual_out[...] = sum(w * v for w, v in zip(residual, powers))
@@ -278,29 +313,35 @@
 def per_device(right_side, diagonal, features, neighbours, vertex_features, vertex_bricks):
     nrows, width, voxels = features.shape
     slots = neighbours.shape[1]
-    across = lax.axis_size("gy")
-    devices = across * lax.axis_size("gx")
+    across, along = lax.axis_size("gy"), lax.axis_size("gx")
     index = jnp.stack([lax.axis_index("gx"), lax.axis_index("gy")]).astype(jnp.int32)
-    smem = pl.BlockSpec(memory_space=pltpu.SMEM)
-    hot = functools.partial(
-        one_hot, nrows=nrows, width=width, slots=slots, span=9 * nrows, across=across
-    )
+    smem, hbm = pl.BlockSpec(memory_space=pltpu.SMEM), pl.BlockSpec(memory_space=pltpu.HBM)
+    shape = (nrows, width, slots, across)
     power = f32(nrows, voxels)
     block_shape, row, table = f32(nrows, LANES), f32(1, LANES), f32(width, LANES)
 
     block, moments = call(
         first_kernel, [block_shape, row], features, right_side, neighbours,
-        specs=[pl.BlockSpec(memory_space=pl.ANY), VMEM, VMEM],
-        scratch=[pltpu.VMEM(features.shape, F32), pltpu.SemaphoreType.DMA((CHUNKS,))],
+        specs=[hbm] * 3, limit=FIRST_LIMIT,
+        scratch=[
+            pltpu.VMEM(right_side.shape, F32),
+            pltpu.VMEM(neighbours.shape, jnp.int32),
+            pltpu.VMEM(features.shape, F32),
+            pltpu.SemaphoreType.DMA((CHUNKS + 2,)),
+        ],
+    )
+    own = call(
+        functools.partial(own_kernel, shape), jax.ShapeDtypeStruct((nrows, 3 * LANES), BF16),
+        index, block, features, specs=[smem, VMEM, VMEM],
     )
     left, column, right = neighbourhood(block)
     middle = call(
-        functools.partial(middle_kernel, hot),
-        jax.ShapeDtypeStruct((3 * nrows, 9 * nrows), BF16), index, column, specs=[smem, VMEM],
+        functools.partial(middle_kernel, shape), jax.ShapeDtypeStruct((LANES, 3 * LANES), BF16),
+        index, column, own, specs=[smem, VMEM, VMEM],
     )
     v1, block, sums, moments, weights = call(
-        functools.partial(second_kernel, hot),
-        [power, block_shape, table, row, jax.ShapeDtypeStruct((LANES, 9 * nrows), BF16)],
+        functools.partial(second_kernel, shape),
+        [power, block_shape, table, row, jax.ShapeDtypeStruct((LANES, 3 * LANES), BF16)],
         index, left, column, right, middle, features, diagonal, right_side, moments,
         specs=[smem] + [VMEM] * 8,
     )
@@ -310,12 +351,12 @@
         left, column, right, weights, features, diagonal, v1, sums, moments,
     )
     left, column, right = neighbourhood(block)
-    v3, sums, moments = call(
-        fourth_kernel, [power, f32(across, width, LANES), f32(devices, LANES)],
+    v3, sums = call(
+        fourth_kernel, [power, f32(across, width, LANES)],
         left, column, right, weights, features, diagonal, v2, sums, moments,
     )
-    moments = lax.all_to_all(moments, ("gx", "gy"), 0, 0, tiled=True)
     slab = lax.all_to_all(sums, "gy", 0, 0, tiled=True)
+    moments = lax.all_to_all(call(fold_kernel, f32(along, LANES), slab), "gx", 0, 0, tiled=True)
     vertices = call(
         functools.partial(vertex_kernel, nrows), f32(8, vertex_bricks.shape[0]),
         index, slab, vertex_bricks.reshape(1, -1), vertex_features, specs=[smem] + [VMEM] * 3,

time: 93.7 us -> 85.9 us (0.917)
  starting transfers between devices: 40.9 us -> 36.5 us
  waiting for transfers between devices: 17.9 us -> 14.3 us
  Pallas kernels: 15.4 us -> 17.3 us
  local copies, waits for them, and re-layouts: 5.96 us -> 4.06 us
    all_to_all x1, waiting for transfers between devices: 11.8 us -> 7.3 us  [per_device(): lax.all_to_all(call(fold_kernel, f32(along, LANES), slab), 'gx', 0, 0, ti...]
    ppermute x3, starting transfers between devices: 10.2 us -> 8.14 us  [neighbourhood(): lax.ppermute(column, 'gy', ring('gy', -1))]
    all_to_all x1, starting transfers between devices: 10.4 us -> 8.35 us  [per_device(): lax.all_to_all(call(fold_kernel, f32(along, LANES), slab), 'gx', 0, 0, ti...]
    pallas_call x7 -> x9, Pallas kernels: 15.4 us -> 17.3 us  [call(): pl.pallas_call(kernel, out_shape=out_shape, in_specs=specs or [VMEM] * le...]
    unnamed x22, local copies, waits for them, and re-layouts: 5.95 us -> 4.05 us
  transfers between devices with their start and end apart: 13 -> 13, of which waited for: 9 -> 8; matrix products, arithmetic and copies ran while one was open for 0% -> 1% of each run, Pallas kernels for 3% -> 3%
where the time goes in v3:
time: 85.9 us; the launch traced here: 85.5 us
  starting transfers between devices  36.5 us (42%)
  Pallas kernels  17.3 us (20%)
  waiting for transfers between devices  14.3 us (17%)
  blocking collectives  12.4 us (14%)
  local copies, waits for them, and re-layouts  4.06 us (5%)
    pallas_call x9, Pallas kernels, call(): pl.pallas_call(kernel, out_shape=out_shape, in_specs=specs or [VMEM] * le...  17.3 us
    ppermute x3, starting transfers between devices, neighbourhood(): lax.ppermute(block, 'gx', ring('gx', -1))  16.4 us
    all_to_all x1, blocking collectives, per_device(): slab = lax.all_to_all(sums, 'gy', 0, 0, tiled=True)  12.4 us
    all_to_all x1, starting transfers between devices, per_device(): lax.all_to_all(call(fold_kernel, f32(along, LANES), slab), 'gx', 0, 0, ti...  8.35 us
    ppermute x3, starting transfers between devices, neighbourhood(): lax.ppermute(column, 'gy', ring('gy', -1))  8.14 us
    all_to_all x1, waiting for transfers between devices, per_device(): lax.all_to_all(call(fold_kernel, f32(along, LANES), slab), 'gx', 0, 0, ti...  7.3 us
    unnamed x22, local copies, waits for them, and re-layouts  4.05 us
    ppermute x3, waiting for transfers between devices, neighbourhood(): lax.ppermute(block, 'gx', ring('gx', 1))  3.41 us
  transfers between devices with their start and end apart: 13, of which 8 were waited for; matrix products, arithmetic and copies ran while one was open for 1% of the time, Pallas kernels for 3%

profile of v3, /device:TPU:1, one launch (start us, length us, event | category | flops | bytes accessed | tf_op | source)
XLA Modules:
  0.0 85.5 jit_solution(13046762299678613603)
XLA Ops:
  0.7 3.1 %shard_map.85 = (f32[32,128]{1,0:T(8,128)}, f32[1,128]{1,0:T(1,128)}) custom-call(f32[32,64,512]{2,1,0:T(8,128)} %features.9, f32[32,512]{1,0:T(8,128)} %v0.1, s32[32,27]{1,0:T(8,128)} %neighbours.1), custom_call_target="tpu_custom_call" | custom-call | tf_op jit(solution)/shard_map/pallas_call | solution.py:23
  3.8 2.1 %collective-permute-start = (f32[32,128]{1,0:T(8,128)}, f32[32,128]{1,0:T(8,128)S(1)}, u32[]{:S(2)}, u32[]{:S(2)}) collective-permute-start(f32[32,128]{1,0:T(8,128)} %get-tuple-element.19.block), channel_id=1, source_target_pairs={{0,8},{8,16},{16,24},{24,32},{32,40},{40,48},{48,56},{56,64},{64,7... | collective-permute-start | bytes 49160 | tf_op jit(solution)/shard_map/ppermute | solution.py:304
  5.9 6.6 %collective-permute-start.1 = (f32[32,128]{1,0:T(8,128)}, f32[32,128]{1,0:T(8,128)S(1)}, u32[]{:S(2)}, u32[]{:S(2)}) collective-permute-start(f32[32,128]{1,0:T(8,128)} %get-tuple-element.19.block), channel_id=1, source_target_pairs={{0,248},{8,0},{16,8},{24,16},{32,24},{40,32},{48,40},{56,48},{64,5... | collective-permute-start | bytes 49160 | tf_op jit(solution)/shard_map/ppermute | solution.py:304
  12.5 1.2 %collective-permute-done = f32[32,128]{1,0:T(8,128)S(1)} collective-permute-done((f32[32,128]{1,0:T(8,128)}, f32[32,128]{1,0:T(8,128)S(1)}, u32[]{:S(2)}, u32[]{:S(2)}) %collective-permute-start) | collective-permute-done | bytes 16416 | tf_op jit(solution)/shard_map/ppermute | solution.py:304
  13.8 0.7 constant_dynamic-update-slice_fusion.1
  14.5 1.5 %collective-permute-start.3 = (f32[96,128]{1,0:T(8,128)S(1)}, f32[96,128]{1,0:T(8,128)S(1)}, u32[]{:S(2)}, u32[]{:S(2)}) collective-permute-start(f32[96,128]{1,0:T(8,128)S(1)} %constant_dynamic-update-slice_fusion.column), channel_id=1, source_target_pairs={{0,7},{1,0},{2,1},{3,2},{4,3},{5,4},{6,5},{7,6},{8,15},{9,8},{10,9... | collective-permute-start | bytes 147464 | tf_op jit(solution)/shard_map/ppermute | solution.py:309
  16.1 1.2 %collective-permute-start.2 = (f32[96,128]{1,0:T(8,128)S(1)}, f32[96,128]{1,0:T(8,128)S(1)}, u32[]{:S(2)}, u32[]{:S(2)}) collective-permute-start(f32[96,128]{1,0:T(8,128)S(1)} %constant_dynamic-update-slice_fusion.column), channel_id=1, source_target_pairs={{0,1},{1,2},{2,3},{3,4},{4,5},{5,6},{6,7},{7,0},{8,9},{9,10},{10,1... | collective-permute-start | bytes 147464 | tf_op jit(solution)/shard_map/ppermute | solution.py:307
  17.3 2.2 %copy-done = f32[32,64,512]{2,1,0:T(8,128)S(1)} copy-done((f32[32,64,512]{2,1,0:T(8,128)S(1)}, f32[32,64,512]{2,1,0:T(8,128)}, u32[]{:S(2)}) %copy-start) | copy-done | bytes 4194328
  19.5 0.7 copy-done.5
  20.3 0.8 shard_map.86.own
  21.0 1.0 %shard_map.87.middle = bf16[128,384]{1,0:T(8,128)(2,1)S(1)} custom-call(s32[2]{0:T(128)S(1)} %pad_add_fusion.index, f32[96,128]{1,0:T(8,128)S(1)} %constant_dynamic-update-slice_fusion.column, bf16[32,384]{1,0:T(8,128)(2,1)S(1)} %shard_map.86.own), custom_call_target="tpu_custom_call" | custom-call | tf_op jit(solution)/shard_map/pallas_call | solution.py:23
  22.0 0.4 copy-done.1
  22.4 5.4 %shard_map.88 = (f32[32,512]{1,0:T(8,128)S(1)}, f32[32,128]{1,0:T(8,128)S(1)}, f32[64,128]{1,0:T(8,128)S(1)}, f32[1,128]{1,0:T(1,128)S(1)}, bf16[128,384]{1,0:T(8,128)(2,1)S(1)}) custom-call(s32[2]{0:T(128)S(1)} %pad_add_fusion.index, f32[96,128]{1,0:T(8,128)S(1)} %collective-permute-done.2.left, f32[96,128]{1,0:T(8,128)S(1)} %constant_dynamic-update-slice_fusion.column, ...), custom_call_target="tpu_custom_call" | custom-call | tf_op jit(solution)/shard_map/pallas_call | solution.py:23
  27.8 4.8 %collective-permute-start.5 = (f32[32,128]{1,0:T(8,128)S(1)}, f32[32,128]{1,0:T(8,128)S(1)}, u32[]{:S(2)}, u32[]{:S(2)}) collective-permute-start(f32[32,128]{1,0:T(8,128)S(1)} %get-tuple-element.21), channel_id=1, source_target_pairs={{0,248},{8,0},{16,8},{24,16},{32,24},{40,32},{48,40},{56,48},{64,5... | collective-permute-start | bytes 49160 | tf_op jit(solution)/shard_map/ppermute | solution.py:304
  32.6 1.1 %collective-permute-done.4 = f32[32,128]{1,0:T(8,128)S(1)} collective-permute-done((f32[32,128]{1,0:T(8,128)S(1)}, f32[32,128]{1,0:T(8,128)S(1)}, u32[]{:S(2)}, u32[]{:S(2)}) %collective-permute-start.4) | collective-permute-done | bytes 16416 | tf_op jit(solution)/shard_map/ppermute | solution.py:304
  33.8 1.5 %collective-permute-start.7 = (f32[96,128]{1,0:T(8,128)S(1)}, f32[96,128]{1,0:T(8,128)S(1)}, u32[]{:S(2)}, u32[]{:S(2)}) collective-permute-start(f32[96,128]{1,0:T(8,128)S(1)} %constant_dynamic-update-slice_fusion.3.column), channel_id=1, source_target_pairs={{0,7},{1,0},{2,1},{3,2},{4,3},{5,4},{6,5},{7,6},{8,15},{9,8},{10,9... | collective-permute-start | bytes 147464 | tf_op jit(solution)/shard_map/ppermute | solution.py:309
  35.3 0.2 collective-permute-start.6
  35.5 1.8 %collective-permute-done.7.right = f32[96,128]{1,0:T(8,128)S(1)} collective-permute-done((f32[96,128]{1,0:T(8,128)S(1)}, f32[96,128]{1,0:T(8,128)S(1)}, u32[]{:S(2)}, u32[]{:S(2)}) %collective-permute-start.7) | collective-permute-done | bytes 49184 | tf_op jit(solution)/shard_map/ppermute | solution.py:309
  37.3 0.5 collective-permute-done.6.left
  37.8 3.3 %shard_map.89 = (f32[32,512]{1,0:T(8,128)S(1)}, f32[32,128]{1,0:T(8,128)S(1)}, f32[64,128]{1,0:T(8,128)S(1)}, f32[1,128]{1,0:T(1,128)S(1)}) custom-call(f32[96,128]{1,0:T(8,128)S(1)} %collective-permute-done.6.left, f32[96,128]{1,0:T(8,128)S(1)} %constant_dynamic-update-slice_fusion.3.column, f32[96,128]{1,0:T(8,128)S(1)} %collective-permute-done.7.right, ...), custom_call_target="tpu_custom_call" | custom-call | tf_op jit(solution)/shard_map/pallas_call | solution.py:23
  41.2 5.0 %collective-permute-start.9 = (f32[32,128]{1,0:T(8,128)S(1)}, f32[32,128]{1,0:T(8,128)S(1)}, u32[]{:S(2)}, u32[]{:S(2)}) collective-permute-start(f32[32,128]{1,0:T(8,128)S(1)} %get-tuple-element.26), channel_id=1, source_target_pairs={{0,248},{8,0},{16,8},{24,16},{32,24},{40,32},{48,40},{56,48},{64,5... | collective-permute-start | bytes 49160 | tf_op jit(solution)/shard_map/ppermute | solution.py:304
  46.2 1.0 %collective-permute-done.8 = f32[32,128]{1,0:T(8,128)S(1)} collective-permute-done((f32[32,128]{1,0:T(8,128)S(1)}, f32[32,128]{1,0:T(8,128)S(1)}, u32[]{:S(2)}, u32[]{:S(2)}) %collective-permute-start.8) | collective-permute-done | bytes 16416 | tf_op jit(solution)/shard_map/ppermute | solution.py:304
  47.2 5.0 %collective-permute-start.11 = (f32[96,128]{1,0:T(8,128)S(1)}, f32[96,128]{1,0:T(8,128)S(1)}, u32[]{:S(2)}, u32[]{:S(2)}) collective-permute-start(f32[96,128]{1,0:T(8,128)S(1)} %constant_dynamic-update-slice_fusion.6.column), channel_id=1, source_target_pairs={{0,7},{1,0},{2,1},{3,2},{4,3},{5,4},{6,5},{7,6},{8,15},{9,8},{10,9... | collective-permute-start | bytes 147464 | tf_op jit(solution)/shard_map/ppermute | solution.py:309
  52.3 0.9 %collective-permute-done.11.right = f32[96,128]{1,0:T(8,128)S(1)} collective-permute-done((f32[96,128]{1,0:T(8,128)S(1)}, f32[96,128]{1,0:T(8,128)S(1)}, u32[]{:S(2)}, u32[]{:S(2)}) %collective-permute-start.11) | collective-permute-done | bytes 49184 | tf_op jit(solution)/shard_map/ppermute | solution.py:309
  53.1 0.3 collective-permute-done.10.left
  53.5 1.1 %shard_map.90 = (f32[32,512]{1,0:T(8,128)S(1)}, f32[8,64,128]{2,1,0:T(8,128)S(1)}) custom-call(f32[96,128]{1,0:T(8,128)S(1)} %collective-permute-done.10.left, f32[96,128]{1,0:T(8,128)S(1)} %constant_dynamic-update-slice_fusion.6.column, f32[96,128]{1,0:T(8,128)S(1)} %collective-permute-done.11.right, bf16[128,384]{1,0:T(8,128)(2,1)S(1)} %get-tuple-element.22.weights, ...), custom_call_target="tpu_custom_call" | custom-call | tf_op jit(solution)/shard_map/pallas_call | solution.py:23
  54.6 12.4 %all_to_all.16.slab = f32[8,64,128]{2,1,0:T(8,128)S(1)} all-to-all(f32[8,64,128]{2,1,0:T(8,128)S(1)} %get-tuple-element.30), channel_id=1, replica_groups=mesh['gx'=32,'gy'=8] {'gy'}, dimensions={0} | all-to-all | bytes 524288 | tf_op jit(solution)/shard_map/all_to_all | solution.py:358
  67.1 0.6 shard_map.91
  67.7 8.3 %all-to-all-start.1 = ((f32[32,1,128]{2,1,0:T(1,128)}), f32[32,1,128]{2,1,0:T(1,128)S(1)}, u32[]{:S(2)}, u32[]{:S(2)}) async-start(f32[32,1,128]{2,1,0:T(1,128)} %bitcast.3), calls=%async_computation.1 | async-start | bytes 32768 | tf_op jit(solution)/shard_map/all_to_all | solution.py:359
  76.1 1.2 %shard_map.92.vertices = f32[8,1024]{1,0:T(8,128)S(1)} custom-call(s32[2]{0:T(128)S(1)} %pad_add_fusion.index, f32[8,64,128]{2,1,0:T(8,128)S(1)} %all_to_all.16.slab, s32[1,1024]{1,0:T(1,128)S(1)} %bitcast.9, f32[64,1024]{1,0:T(8,128)S(1)} %copy-done.4), custom_call_target="tpu_custom_call" | custom-call | tf_op jit(solution)/shard_map/pallas_call | solution.py:23
  77.2 7.3 %all-to-all-done.1 = f32[32,1,128]{2,1,0:T(1,128)S(1)} async-done(((f32[32,1,128]{2,1,0:T(1,128)}), f32[32,1,128]{2,1,0:T(1,128)S(1)}, u32[]{:S(2)}, u32[]{:S(2)}) %all-to-all-start.1) | async-done | bytes 16416 | tf_op jit(solution)/shard_map/all_to_all | solution.py:359
  84.5 0.9 %shard_map.93 = (f32[32,512]{1,0:T(8,128)}, f32[32,512]{1,0:T(8,128)}, f32[1,1024]{1,0:T(1,128)}) custom-call(f32[32,128]{1,0:T(8,128)S(1)} %bitcast.8, f32[32,512]{1,0:T(8,128)S(1)} %copy-done.3, f32[32,512]{1,0:T(8,128)S(1)} %get-tuple-element.23.before.v1, f32[32,512]{1,0:T(8,128)S(1)} %get-tuple-element.27.before.v2, ...), custom_call_target="tpu_custom_call" | custom-call | tf_op jit(solution)/shard_map/pallas_call | solution.py:23
  (30 shorter events, 0.2 us)
Async XLA Ops:
  0.6 21.4 %copy-start.3 = (f32[32,512]{1,0:T(8,128)S(1)}, f32[32,512]{1,0:T(8,128)}, u32[]{:S(2)}) copy-start(f32[32,512]{1,0:T(8,128)} %v0.1) | copy-start | bytes 196612
  0.6 21.4 %copy-start.2 = (f32[32,512]{1,0:T(8,128)S(1)}, f32[32,512]{1,0:T(8,128)}, u32[]{:S(2)}) copy-start(f32[32,512]{1,0:T(8,128)} %diagonal.5) | copy-start | bytes 196612
  3.8 18.3 %copy-start.7 = (f32[1,128]{1,0:T(1,128)S(1)}, f32[1,128]{1,0:T(1,128)}, u32[]{:S(2)}) copy-start(f32[1,128]{1,0:T(1,128)} %get-tuple-element.20.moments) | copy-start | bytes 1540
  3.8 10.0 %collective-permute-start = (f32[32,128]{1,0:T(8,128)}, f32[32,128]{1,0:T(8,128)S(1)}, u32[]{:S(2)}, u32[]{:S(2)}) collective-permute-start(f32[32,128]{1,0:T(8,128)} %get-tuple-element.19.block), channel_id=1, source_target_pairs={{0,8},{8,16},{16,24},{24,32},{32,40},{40,48},{48,56},{56,64},{64,7... | collective-permute-start | bytes 49160 | tf_op jit(solution)/shard_map/ppermute | solution.py:304
  5.9 8.6 %collective-permute-start.1 = (f32[32,128]{1,0:T(8,128)}, f32[32,128]{1,0:T(8,128)S(1)}, u32[]{:S(2)}, u32[]{:S(2)}) collective-permute-start(f32[32,128]{1,0:T(8,128)} %get-tuple-element.19.block), channel_id=1, source_target_pairs={{0,248},{8,0},{16,8},{24,16},{32,24},{40,32},{48,40},{56,48},{64,5... | collective-permute-start | bytes 49160 | tf_op jit(solution)/shard_map/ppermute | solution.py:304
  14.5 7.5 %collective-permute-start.3 = (f32[96,128]{1,0:T(8,128)S(1)}, f32[96,128]{1,0:T(8,128)S(1)}, u32[]{:S(2)}, u32[]{:S(2)}) collective-permute-start(f32[96,128]{1,0:T(8,128)S(1)} %constant_dynamic-update-slice_fusion.column), channel_id=1, source_target_pairs={{0,7},{1,0},{2,1},{3,2},{4,3},{5,4},{6,5},{7,6},{8,15},{9,8},{10,9... | collective-permute-start | bytes 147464 | tf_op jit(solution)/shard_map/ppermute | solution.py:309
  16.1 5.9 %collective-permute-start.2 = (f32[96,128]{1,0:T(8,128)S(1)}, f32[96,128]{1,0:T(8,128)S(1)}, u32[]{:S(2)}, u32[]{:S(2)}) collective-permute-start(f32[96,128]{1,0:T(8,128)S(1)} %constant_dynamic-update-slice_fusion.column), channel_id=1, source_target_pairs={{0,1},{1,2},{2,3},{3,4},{4,5},{5,6},{6,7},{7,0},{8,9},{9,10},{10,1... | collective-permute-start | bytes 147464 | tf_op jit(solution)/shard_map/ppermute | solution.py:307
  17.3 2.2 %copy-start = (f32[32,64,512]{2,1,0:T(8,128)S(1)}, f32[32,64,512]{2,1,0:T(8,128)}, u32[]{:S(2)}) copy-start(f32[32,64,512]{2,1,0:T(8,128)} %features.9) | copy-start | bytes 12582916
  19.5 0.7 copy-start.5
  20.3 2.2 %copy-start.1 = (f32[32,64,512]{2,1,0:T(8,128)S(1)}, f32[32,64,512]{2,1,0:T(8,128)}, u32[]{:S(2)}) copy-start(f32[32,64,512]{2,1,0:T(8,128)} %features.9) | copy-start | bytes 12582916
  27.8 5.9 %collective-permute-start.4 = (f32[32,128]{1,0:T(8,128)S(1)}, f32[32,128]{1,0:T(8,128)S(1)}, u32[]{:S(2)}, u32[]{:S(2)}) collective-permute-start(f32[32,128]{1,0:T(8,128)S(1)} %get-tuple-element.21), channel_id=1, source_target_pairs={{0,8},{8,16},{16,24},{24,32},{32,40},{40,48},{48,56},{56,64},{64,7... | collective-permute-start | bytes 49160 | tf_op jit(solution)/shard_map/ppermute | solution.py:304
  27.8 5.9 %collective-permute-start.5 = (f32[32,128]{1,0:T(8,128)S(1)}, f32[32,128]{1,0:T(8,128)S(1)}, u32[]{:S(2)}, u32[]{:S(2)}) collective-permute-start(f32[32,128]{1,0:T(8,128)S(1)} %get-tuple-element.21), channel_id=1, source_target_pairs={{0,248},{8,0},{16,8},{24,16},{32,24},{40,32},{48,40},{56,48},{64,5... | collective-permute-start | bytes 49160 | tf_op jit(solution)/shard_map/ppermute | solution.py:304
  33.8 3.5 %collective-permute-start.7 = (f32[96,128]{1,0:T(8,128)S(1)}, f32[96,128]{1,0:T(8,128)S(1)}, u32[]{:S(2)}, u32[]{:S(2)}) collective-permute-start(f32[96,128]{1,0:T(8,128)S(1)} %constant_dynamic-update-slice_fusion.3.column), channel_id=1, source_target_pairs={{0,7},{1,0},{2,1},{3,2},{4,3},{5,4},{6,5},{7,6},{8,15},{9,8},{10,9... | collective-permute-start | bytes 147464 | tf_op jit(solution)/shard_map/ppermute | solution.py:309
  35.3 2.5 %collective-permute-start.6 = (f32[96,128]{1,0:T(8,128)S(1)}, f32[96,128]{1,0:T(8,128)S(1)}, u32[]{:S(2)}, u32[]{:S(2)}) collective-permute-start(f32[96,128]{1,0:T(8,128)S(1)} %constant_dynamic-update-slice_fusion.3.column), channel_id=1, source_target_pairs={{0,1},{1,2},{2,3},{3,4},{4,5},{5,6},{6,7},{7,0},{8,9},{9,10},{10,1... | collective-permute-start | bytes 147464 | tf_op jit(solution)/shard_map/ppermute | solution.py:307
  37.8 38.2 %copy-start.4 = (f32[64,1024]{1,0:T(8,128)S(1)}, f32[64,1024]{1,0:T(8,128)}, u32[]{:S(2)}) copy-start(f32[64,1024]{1,0:T(8,128)} %vertex_features.1) | copy-start | bytes 786436
  37.8 38.2 %copy-start.6 = (s32[1024]{0:T(1024)S(1)}, s32[1024]{0:T(1024)}, u32[]{:S(2)}) copy-start(s32[1024]{0:T(1024)} %param.11) | copy-start | bytes 12292
  41.1 6.1 %collective-permute-start.8 = (f32[32,128]{1,0:T(8,128)S(1)}, f32[32,128]{1,0:T(8,128)S(1)}, u32[]{:S(2)}, u32[]{:S(2)}) collective-permute-start(f32[32,128]{1,0:T(8,128)S(1)} %get-tuple-element.26), channel_id=1, source_target_pairs={{0,8},{8,16},{16,24},{24,32},{32,40},{40,48},{48,56},{56,64},{64,7... | collective-permute-start | bytes 49160 | tf_op jit(solution)/shard_map/ppermute | solution.py:304
  41.2 6.0 %collective-permute-start.9 = (f32[32,128]{1,0:T(8,128)S(1)}, f32[32,128]{1,0:T(8,128)S(1)}, u32[]{:S(2)}, u32[]{:S(2)}) collective-permute-start(f32[32,128]{1,0:T(8,128)S(1)} %get-tuple-element.26), channel_id=1, source_target_pairs={{0,248},{8,0},{16,8},{24,16},{32,24},{40,32},{48,40},{56,48},{64,5... | collective-permute-start | bytes 49160 | tf_op jit(solution)/shard_map/ppermute | solution.py:304
  47.2 5.9 %collective-permute-start.11 = (f32[96,128]{1,0:T(8,128)S(1)}, f32[96,128]{1,0:T(8,128)S(1)}, u32[]{:S(2)}, u32[]{:S(2)}) collective-permute-start(f32[96,128]{1,0:T(8,128)S(1)} %constant_dynamic-update-slice_fusion.6.column), channel_id=1, source_target_pairs={{0,7},{1,0},{2,1},{3,2},{4,3},{5,4},{6,5},{7,6},{8,15},{9,8},{10,9... | collective-permute-start | bytes 147464 | tf_op jit(solution)/shard_map/ppermute | solution.py:309
  52.3 1.2 %collective-permute-start.10 = (f32[96,128]{1,0:T(8,128)S(1)}, f32[96,128]{1,0:T(8,128)S(1)}, u32[]{:S(2)}, u32[]{:S(2)}) collective-permute-start(f32[96,128]{1,0:T(8,128)S(1)} %constant_dynamic-update-slice_fusion.6.column), channel_id=1, source_target_pairs={{0,1},{1,2},{2,3},{3,4},{4,5},{5,6},{6,7},{7,0},{8,9},{9,10},{10,1... | collective-permute-start | bytes 147464 | tf_op jit(solution)/shard_map/ppermute | solution.py:307
  67.7 16.9 %all-to-all-start.1 = ((f32[32,1,128]{2,1,0:T(1,128)}), f32[32,1,128]{2,1,0:T(1,128)S(1)}, u32[]{:S(2)}, u32[]{:S(2)}) async-start(f32[32,1,128]{2,1,0:T(1,128)} %bitcast.3), calls=%async_computation.1 | async-start | bytes 32768 | tf_op jit(solution)/shard_map/all_to_all | solution.py:359

commit v4 on v3

--- a/solution.py
+++ b/solution.py
@@ -12,6 +12,7 @@
 LANES = 128
 MOMENTS = 2 * ITERS
 CHUNKS = 8
+AHEAD = 3
 MOMENT_LANE = 96
 FIRST_LIMIT = 60
 VMEM = pl.BlockSpec(memory_space=pltpu.VMEM)
@@ -81,7 +82,7 @@
         pltpu.make_async_copy(field, values, sems.at[CHUNKS]),
         pltpu.make_async_copy(neighbours, ids, sems.at[CHUNKS + 1]),
     ]
-    for copy in small + copies:
+    for copy in small + copies[:AHEAD]:
         copy.start()
     for copy in small:
         copy.wait()
@@ -90,6 +91,8 @@
     columns = jnp.zeros((width, LANES), F32)
     for i, copy in enumerate(copies):
         copy.wait()
+        if i + AHEAD < CHUNKS:
+            copies[i + AHEAD].start()
         for b in range(i * each, (i + 1) * each):
             columns = project(buffer[b], values[b : b + 1, :], columns, b)
     block[...] = to_rows(columns, nrows)
@@ -117,18 +120,10 @@
     return jnp.concatenate([third, jnp.zeros((LANES - third.shape[0], third.shape[1]), third.dtype)])
 
 
-def own_kernel(shape, index, block, features, out):
+def middle_kernel(shape, index, column, features, out):
     nrows, width, slots, across = shape
-    place = positions(block[...], nrows, across, index[0], index[1])
-    out[...] = one_hot(place, 0, 3 * LANES, width, slots)
-
-
-def middle_kernel(shape, index, column, own, out):
-    nrows, width, slots, across = shape
-    others = jnp.concatenate([column[:nrows, :], column[2 * nrows :, :]], axis=0)
-    place = positions(others, nrows, across, index[0], index[1])
-    hot = one_hot(place, 0, 3 * LANES, width, slots)
-    out[...] = padded(jnp.concatenate([hot[:nrows], own[...], hot[nrows:]], axis=0))
+    place = positions(column[...], nrows, across, index[0], index[1])
+    out[...] = padded(one_hot(place, 0, 3 * LANES, width, slots))
 
 
 def advance(step, nrows, width, weights, around, features, diagonal, before, sums, moments, outs):
@@ -232,34 +227,32 @@
     out[...] = jnp.broadcast_to(row, out.shape)
 
 
-def vertex_kernel(nrows, index, slab, bricks, vertex_features, out):
+def vertex_values(nrows, index, field, slab, bricks, vertex_features):
     across, width, _ = slab.shape
     local = bricks[...] - index[0] * across * nrows
     hot = lax.broadcasted_iota(jnp.int32, (across * nrows, local.shape[1]), 0) == local
     hot = jnp.where(hot, 1.0, 0.0).astype(BF16)
     group = LANES // nrows
     lanes = lane_iota(width)
-    table = []
-    for k in range(ITERS):
-        tiles = []
-        for start in range(0, across, group):
-            tile = jnp.zeros((width, LANES), F32)
-            for d in range(group):
+    tiles = []
+    for start in range(0, across, group):
+        tile = jnp.zeros((width, LANES), F32)
+        for d in range(group):
+            mixed = None
+            for k, weight in enumerate(field):
                 shift = (d - k) * nrows % LANES
                 moved = pltpu.roll(slab[start + d], shift, 1) if shift else slab[start + d]
-                tile = jnp.where((lanes >= d * nrows) & (lanes < (d + 1) * nrows), moved, tile)
-            tiles.append(tile)
-        table.append(jnp.concatenate(tiles, axis=1))
-    rest = jnp.concatenate(table, axis=0)
+                mixed = weight * moved if mixed is None else mixed + weight * moved
+            tile = jnp.where((lanes >= d * nrows) & (lanes < (d + 1) * nrows), mixed, tile)
+        tiles.append(tile)
+    rest = jnp.concatenate(tiles, axis=1)
     picked = None
     for _ in range(3):
         part = rest.astype(BF16)
         rest = rest - part.astype(F32)
         value = jnp.dot(part, hot, preferred_element_type=F32)
         picked = value if picked is None else picked + value
-    for k in range(ITERS):
-        product = vertex_features[...] * picked[k * width : (k + 1) * width, :]
-        out[k : k + 1, :] = jnp.sum(product, axis=0, keepdims=True)
+    return jnp.sum(vertex_features[...] * picked, axis=0, keepdims=True)
 
 
 def cg_weights(mu):
@@ -290,13 +283,16 @@
     return field, residual
 
 
-def last_kernel(moments, v0, v1, v2, v3, vertices, field_out, residual_out, vertices_out):
+def last_kernel(
+    nrows, index, moments, v0, v1, v2, v3, slab, bricks, vertex_features,
+    field_out, residual_out, vertices_out,
+):
     sums = jnp.sum(moments[...], axis=0, keepdims=True)
     field, residual = cg_weights([sums[:, MOMENT_LANE + i : MOMENT_LANE + i + 1] for i in range(MOMENTS)])
     powers = [v0[...], v1[...], v2[...], v3[...]]
     field_out[...] = sum(w * v for w, v in zip(field, powers))
     residual_out[...] = sum(w * v for w, v in zip(residual, powers))
-    vertices_out[...] = sum(w * vertices[i : i + 1, :] for i, w in enumerate(field))
+    vertices_out[...] = vertex_values(nrows, index, field, slab, bricks, vertex_features)
 
 
 def neighbourhood(block):
@@ -330,14 +326,10 @@
             pltpu.SemaphoreType.DMA((CHUNKS + 2,)),
         ],
     )
-    own = call(
-        functools.partial(own_kernel, shape), jax.ShapeDtypeStruct((nrows, 3 * LANES), BF16),
-        index, block, features, specs=[smem, VMEM, VMEM],
-    )
     left, column, right = neighbourhood(block)
     middle = call(
         functools.partial(middle_kernel, shape), jax.ShapeDtypeStruct((LANES, 3 * LANES), BF16),
-        index, column, own, specs=[smem, VMEM, VMEM],
+        index, column, features, specs=[smem, VMEM, VMEM],
     )
     v1, block, sums, moments, weights = call(
         functools.partial(second_kernel, shape),
@@ -357,13 +349,10 @@
     )
     slab = lax.all_to_all(sums, "gy", 0, 0, tiled=True)
     moments = lax.all_to_all(call(fold_kernel, f32(along, LANES), slab), "gx", 0, 0, tiled=True)
-    vertices = call(
-        functools.partial(vertex_kernel, nrows), f32(8, vertex_bricks.shape[0]),
-        index, slab, vertex_bricks.reshape(1, -1), vertex_features, specs=[smem] + [VMEM] * 3,
-    )
     field, residual, values = call(
-        last_kernel, [power, power, f32(1, vertex_bricks.shape[0])],
-        moments, right_side, v1, v2, v3, vertices,
+        functools.partial(last_kernel, nrows), [power, power, f32(1, vertex_bricks.shape[0])],
+        index, moments, right_side, v1, v2, v3, slab, vertex_bricks.reshape(1, -1), vertex_features,
+        specs=[smem] + [VMEM] * 8,
     )
     return field, residual, values.reshape(-1)
 

time: 85.9 us -> 85.5 us (level)
  blocking collectives: 12.4 us -> 29.1 us
  waiting for transfers between devices: 14.3 us -> 5.92 us
  starting transfers between devices: 36.5 us -> 29.2 us
  local copies, waits for them, and re-layouts: 4.06 us -> 2.95 us
    all_to_all x0 -> x1, blocking collectives: none -> 16.7 us  [per_device(): lax.all_to_all(call(fold_kernel, f32(along, LANES), slab), 'gx', 0, 0, ti...]
    all_to_all x1 -> x0, starting transfers between devices: 8.35 us -> none  [per_device(): lax.all_to_all(call(fold_kernel, f32(along, LANES), slab), 'gx', 0, 0, ti...]
    all_to_all x1 -> x0, waiting for transfers between devices: 7.3 us -> none  [per_device(): lax.all_to_all(call(fold_kernel, f32(along, LANES), slab), 'gx', 0, 0, ti...]
    ppermute x3, starting transfers between devices: 8.14 us -> 9.3 us  [neighbourhood(): lax.ppermute(column, 'gy', ring('gy', -1))]
    unnamed x22 -> x18, local copies, waits for them, and re-layouts: 4.05 us -> 2.94 us
    ppermute x3, waiting for transfers between devices: 2.65 us -> 1.76 us  [neighbourhood(): lax.ppermute(column, 'gy', ring('gy', -1))]
    pallas_call x9 -> x7, Pallas kernels: 17.3 us -> 17.1 us  [call(): pl.pallas_call(kernel, out_shape=out_shape, in_specs=specs or [VMEM] * le...]
  transfers between devices with their start and end apart: 13 -> 12, of which waited for: 8 -> 7; matrix products, arithmetic and copies ran while one was open for 1% -> 1% of each run, Pallas kernels for 3% -> 1%
where the time goes in v4:
time: 85.5 us; the launch traced here: 85.2 us
  starting transfers between devices  29.2 us (34%)
  blocking collectives  29.1 us (34%)
  Pallas kernels  17.1 us (20%)
  waiting for transfers between devices  5.92 us (7%)
  local copies, waits for them, and re-layouts  2.95 us (3%)
    pallas_call x7, Pallas kernels, call(): pl.pallas_call(kernel, out_shape=out_shape, in_specs=specs or [VMEM] * le...  17.1 us
    all_to_all x1, blocking collectives, per_device(): lax.all_to_all(call(fold_kernel, f32(along, LANES), slab), 'gx', 0, 0, ti...  16.7 us
    ppermute x3, starting transfers between devices, neighbourhood(): lax.ppermute(block, 'gx', ring('gx', -1))  16.5 us
    all_to_all x1, blocking collectives, per_device(): slab = lax.all_to_all(sums, 'gy', 0, 0, tiled=True)  12.4 us
    ppermute x3, starting transfers between devices, neighbourhood(): lax.ppermute(column, 'gy', ring('gy', -1))  9.3 us
    ppermute x3, waiting for transfers between devices, neighbourhood(): lax.ppermute(block, 'gx', ring('gx', 1))  3.41 us
    unnamed x18, local copies, waits for them, and re-layouts  2.94 us
    ppermute x3, starting transfers between devices, neighbourhood(): lax.ppermute(block, 'gx', ring('gx', 1))  2.2 us
  transfers between devices with their start and end apart: 12, of which 7 were waited for; matrix products, arithmetic and copies ran while one was open for 1% of the time, Pallas kernels for 1%

profile of v4, /device:TPU:1, one launch (start us, length us, event | category | flops | bytes accessed | tf_op | source)
XLA Modules:
  0.0 85.2 jit_solution(9916652904852655285)
XLA Ops:
  0.7 4.4 %shard_map.85 = (f32[32,128]{1,0:T(8,128)}, f32[1,128]{1,0:T(1,128)}) custom-call(f32[32,64,512]{2,1,0:T(8,128)} %features.9, f32[32,512]{1,0:T(8,128)} %v0.1, s32[32,27]{1,0:T(8,128)} %neighbours.1), custom_call_target="tpu_custom_call" | custom-call | tf_op jit(solution)/shard_map/pallas_call | solution.py:24
  5.0 2.1 %collective-permute-start = (f32[32,128]{1,0:T(8,128)}, f32[32,128]{1,0:T(8,128)S(1)}, u32[]{:S(2)}, u32[]{:S(2)}) collective-permute-start(f32[32,128]{1,0:T(8,128)} %get-tuple-element.19), channel_id=1, source_target_pairs={{0,8},{8,16},{16,24},{24,32},{32,40},{40,48},{48,56},{56,64},{64,7... | collective-permute-start | bytes 49160 | tf_op jit(solution)/shard_map/ppermute | solution.py:300
  7.2 6.6 %collective-permute-start.1 = (f32[32,128]{1,0:T(8,128)}, f32[32,128]{1,0:T(8,128)S(1)}, u32[]{:S(2)}, u32[]{:S(2)}) collective-permute-start(f32[32,128]{1,0:T(8,128)} %get-tuple-element.19), channel_id=1, source_target_pairs={{0,248},{8,0},{16,8},{24,16},{32,24},{40,32},{48,40},{56,48},{64,5... | collective-permute-start | bytes 49160 | tf_op jit(solution)/shard_map/ppermute | solution.py:300
  13.8 1.2 %collective-permute-done = f32[32,128]{1,0:T(8,128)S(1)} collective-permute-done((f32[32,128]{1,0:T(8,128)}, f32[32,128]{1,0:T(8,128)S(1)}, u32[]{:S(2)}, u32[]{:S(2)}) %collective-permute-start) | collective-permute-done | bytes 16416 | tf_op jit(solution)/shard_map/ppermute | solution.py:300
  15.1 0.7 constant_dynamic-update-slice_fusion.1
  15.8 0.0 collective-permute-done.1
  15.8 1.5 %collective-permute-start.3 = (f32[96,128]{1,0:T(8,128)S(1)}, f32[96,128]{1,0:T(8,128)S(1)}, u32[]{:S(2)}, u32[]{:S(2)}) collective-permute-start(f32[96,128]{1,0:T(8,128)S(1)} %constant_dynamic-update-slice_fusion.column), channel_id=1, source_target_pairs={{0,7},{1,0},{2,1},{3,2},{4,3},{5,4},{6,5},{7,6},{8,15},{9,8},{10,9... | collective-permute-start | bytes 147464 | tf_op jit(solution)/shard_map/ppermute | solution.py:305
  17.3 1.2 %collective-permute-start.2 = (f32[96,128]{1,0:T(8,128)S(1)}, f32[96,128]{1,0:T(8,128)S(1)}, u32[]{:S(2)}, u32[]{:S(2)}) collective-permute-start(f32[96,128]{1,0:T(8,128)S(1)} %constant_dynamic-update-slice_fusion.column), channel_id=1, source_target_pairs={{0,1},{1,2},{2,3},{3,4},{4,5},{5,6},{6,7},{7,0},{8,9},{9,10},{10,1... | collective-permute-start | bytes 147464 | tf_op jit(solution)/shard_map/ppermute | solution.py:303
  18.5 0.1 pad_add_fusion.index
  18.6 2.2 %copy-done = f32[32,64,512]{2,1,0:T(8,128)S(1)} copy-done((f32[32,64,512]{2,1,0:T(8,128)S(1)}, f32[32,64,512]{2,1,0:T(8,128)}, u32[]{:S(2)}) %copy-start) | copy-done | bytes 4194328
  20.8 1.2 %shard_map.86.middle = bf16[128,384]{1,0:T(8,128)(2,1)S(1)} custom-call(s32[2]{0:T(128)S(1)} %pad_add_fusion.index, f32[96,128]{1,0:T(8,128)S(1)} %constant_dynamic-update-slice_fusion.column, f32[32,64,512]{2,1,0:T(8,128)S(1)} %copy-done), custom_call_target="tpu_custom_call" | custom-call | tf_op jit(solution)/shard_map/pallas_call | solution.py:24
  22.0 0.0 collective-permute-done.3.right
  22.0 0.0 collective-permute-done.2.left
  22.0 5.3 %shard_map.87 = (f32[32,512]{1,0:T(8,128)S(1)}, f32[32,128]{1,0:T(8,128)S(1)}, f32[64,128]{1,0:T(8,128)S(1)}, f32[1,128]{1,0:T(1,128)S(1)}, bf16[128,384]{1,0:T(8,128)(2,1)S(1)}) custom-call(s32[2]{0:T(128)S(1)} %pad_add_fusion.index, f32[96,128]{1,0:T(8,128)S(1)} %collective-permute-done.2.left, f32[96,128]{1,0:T(8,128)S(1)} %constant_dynamic-update-slice_fusion.column, ...), custom_call_target="tpu_custom_call" | custom-call | tf_op jit(solution)/shard_map/pallas_call | solution.py:24
  27.3 0.0 collective-permute-start.4
  27.4 4.8 %collective-permute-start.5 = (f32[32,128]{1,0:T(8,128)S(1)}, f32[32,128]{1,0:T(8,128)S(1)}, u32[]{:S(2)}, u32[]{:S(2)}) collective-permute-start(f32[32,128]{1,0:T(8,128)S(1)} %get-tuple-element.21), channel_id=1, source_target_pairs={{0,248},{8,0},{16,8},{24,16},{32,24},{40,32},{48,40},{56,48},{64,5... | collective-permute-start | bytes 49160 | tf_op jit(solution)/shard_map/ppermute | solution.py:300
  32.2 1.1 %collective-permute-done.4 = f32[32,128]{1,0:T(8,128)S(1)} collective-permute-done((f32[32,128]{1,0:T(8,128)S(1)}, f32[32,128]{1,0:T(8,128)S(1)}, u32[]{:S(2)}, u32[]{:S(2)}) %collective-permute-start.4) | collective-permute-done | bytes 16416 | tf_op jit(solution)/shard_map/ppermute | solution.py:300
  33.3 0.0 collective-permute-done.5
  33.3 2.8 %collective-permute-start.7 = (f32[96,128]{1,0:T(8,128)S(1)}, f32[96,128]{1,0:T(8,128)S(1)}, u32[]{:S(2)}, u32[]{:S(2)}) collective-permute-start(f32[96,128]{1,0:T(8,128)S(1)} %constant_dynamic-update-slice_fusion.3.column), channel_id=1, source_target_pairs={{0,7},{1,0},{2,1},{3,2},{4,3},{5,4},{6,5},{7,6},{8,15},{9,8},{10,9... | collective-permute-start | bytes 147464 | tf_op jit(solution)/shard_map/ppermute | solution.py:305
  36.1 0.9 %collective-permute-done.7.right = f32[96,128]{1,0:T(8,128)S(1)} collective-permute-done((f32[96,128]{1,0:T(8,128)S(1)}, f32[96,128]{1,0:T(8,128)S(1)}, u32[]{:S(2)}, u32[]{:S(2)}) %collective-permute-start.7) | collective-permute-done | bytes 49184 | tf_op jit(solution)/shard_map/ppermute | solution.py:305
  37.0 0.4 collective-permute-done.6.left
  37.4 3.3 %shard_map.88 = (f32[32,512]{1,0:T(8,128)S(1)}, f32[32,128]{1,0:T(8,128)S(1)}, f32[64,128]{1,0:T(8,128)S(1)}, f32[1,128]{1,0:T(1,128)S(1)}) custom-call(f32[96,128]{1,0:T(8,128)S(1)} %collective-permute-done.6.left, f32[96,128]{1,0:T(8,128)S(1)} %constant_dynamic-update-slice_fusion.3.column, f32[96,128]{1,0:T(8,128)S(1)} %collective-permute-done.7.right, ...), custom_call_target="tpu_custom_call" | custom-call | tf_op jit(solution)/shard_map/pallas_call | solution.py:24
  40.6 0.0 collective-permute-start.8
  40.7 5.1 %collective-permute-start.9 = (f32[32,128]{1,0:T(8,128)S(1)}, f32[32,128]{1,0:T(8,128)S(1)}, u32[]{:S(2)}, u32[]{:S(2)}) collective-permute-start(f32[32,128]{1,0:T(8,128)S(1)} %get-tuple-element.26), channel_id=1, source_target_pairs={{0,248},{8,0},{16,8},{24,16},{32,24},{40,32},{48,40},{56,48},{64,5... | collective-permute-start | bytes 49160 | tf_op jit(solution)/shard_map/ppermute | solution.py:300
  45.8 1.0 %collective-permute-done.8 = f32[32,128]{1,0:T(8,128)S(1)} collective-permute-done((f32[32,128]{1,0:T(8,128)S(1)}, f32[32,128]{1,0:T(8,128)S(1)}, u32[]{:S(2)}, u32[]{:S(2)}) %collective-permute-start.8) | collective-permute-done | bytes 16416 | tf_op jit(solution)/shard_map/ppermute | solution.py:300
  46.8 4.9 %collective-permute-start.11 = (f32[96,128]{1,0:T(8,128)S(1)}, f32[96,128]{1,0:T(8,128)S(1)}, u32[]{:S(2)}, u32[]{:S(2)}) collective-permute-start(f32[96,128]{1,0:T(8,128)S(1)} %constant_dynamic-update-slice_fusion.6.column), channel_id=1, source_target_pairs={{0,7},{1,0},{2,1},{3,2},{4,3},{5,4},{6,5},{7,6},{8,15},{9,8},{10,9... | collective-permute-start | bytes 147464 | tf_op jit(solution)/shard_map/ppermute | solution.py:305
  51.8 0.9 %collective-permute-done.11.right = f32[96,128]{1,0:T(8,128)S(1)} collective-permute-done((f32[96,128]{1,0:T(8,128)S(1)}, f32[96,128]{1,0:T(8,128)S(1)}, u32[]{:S(2)}, u32[]{:S(2)}) %collective-permute-start.11) | collective-permute-done | bytes 49184 | tf_op jit(solution)/shard_map/ppermute | solution.py:305
  52.7 0.3 collective-permute-done.10.left
  53.0 1.1 %shard_map.89 = (f32[32,512]{1,0:T(8,128)S(1)}, f32[8,64,128]{2,1,0:T(8,128)S(1)}) custom-call(f32[96,128]{1,0:T(8,128)S(1)} %collective-permute-done.10.left, f32[96,128]{1,0:T(8,128)S(1)} %constant_dynamic-update-slice_fusion.6.column, f32[96,128]{1,0:T(8,128)S(1)} %collective-permute-done.11.right, bf16[128,384]{1,0:T(8,128)(2,1)S(1)} %get-tuple-element.22.weights, ...), custom_call_target="tpu_custom_call" | custom-call | tf_op jit(solution)/shard_map/pallas_call | solution.py:24
  54.1 12.4 %all_to_all.16.slab = f32[8,64,128]{2,1,0:T(8,128)S(1)} all-to-all(f32[8,64,128]{2,1,0:T(8,128)S(1)} %get-tuple-element.30), channel_id=1, replica_groups=mesh['gx'=32,'gy'=8] {'gy'}, dimensions={0} | all-to-all | bytes 524288 | tf_op jit(solution)/shard_map/all_to_all | solution.py:350
  66.5 16.7 %all_to_all.17 = f32[32,1,128]{2,1,0:T(1,128)S(1)} all-to-all(f32[32,1,128]{2,1,0:T(1,128)S(1)} %bitcast.9), channel_id=1, replica_groups=mesh['gx'=32,'gy'=8] {'gx'}, dimensions={0} | all-to-all | bytes 32768 | tf_op jit(solution)/shard_map/all_to_all | solution.py:351
  83.3 1.9 %shard_map.91 = (f32[32,512]{1,0:T(8,128)}, f32[32,512]{1,0:T(8,128)}, f32[1,1024]{1,0:T(1,128)}) custom-call(s32[2]{0:T(128)S(1)} %pad_add_fusion.index, f32[32,128]{1,0:T(8,128)S(1)} %bitcast.8, f32[32,512]{1,0:T(8,128)S(1)} %copy-done.2, f32[32,512]{1,0:T(8,128)S(1)} %get-tuple-element.23.before.v1, f32[32,512]{1,0:T(8,128)S(1)} %get-tuple-element.27.before.v2, ...), custom_call_target="tpu_custom_call" | custom-call | tf_op jit(solution)/shard_map/pallas_call | solution.py:24
  (23 shorter events, 0.1 us)
Async XLA Ops:
  0.6 21.3 %copy-start.2 = (f32[32,512]{1,0:T(8,128)S(1)}, f32[32,512]{1,0:T(8,128)}, u32[]{:S(2)}) copy-start(f32[32,512]{1,0:T(8,128)} %v0.1) | copy-start | bytes 196612
  0.6 21.3 %copy-start.1 = (f32[32,512]{1,0:T(8,128)S(1)}, f32[32,512]{1,0:T(8,128)}, u32[]{:S(2)}) copy-start(f32[32,512]{1,0:T(8,128)} %diagonal.5) | copy-start | bytes 196612
  5.0 17.0 %copy-start.5 = (f32[1,128]{1,0:T(1,128)S(1)}, f32[1,128]{1,0:T(1,128)}, u32[]{:S(2)}) copy-start(f32[1,128]{1,0:T(1,128)} %get-tuple-element.20.moments) | copy-start | bytes 1540
  5.0 10.0 %collective-permute-start = (f32[32,128]{1,0:T(8,128)}, f32[32,128]{1,0:T(8,128)S(1)}, u32[]{:S(2)}, u32[]{:S(2)}) collective-permute-start(f32[32,128]{1,0:T(8,128)} %get-tuple-element.19), channel_id=1, source_target_pairs={{0,8},{8,16},{16,24},{24,32},{32,40},{40,48},{48,56},{56,64},{64,7... | collective-permute-start | bytes 49160 | tf_op jit(solution)/shard_map/ppermute | solution.py:300
  7.2 8.6 %collective-permute-start.1 = (f32[32,128]{1,0:T(8,128)}, f32[32,128]{1,0:T(8,128)S(1)}, u32[]{:S(2)}, u32[]{:S(2)}) collective-permute-start(f32[32,128]{1,0:T(8,128)} %get-tuple-element.19), channel_id=1, source_target_pairs={{0,248},{8,0},{16,8},{24,16},{32,24},{40,32},{48,40},{56,48},{64,5... | collective-permute-start | bytes 49160 | tf_op jit(solution)/shard_map/ppermute | solution.py:300
  15.8 6.2 %collective-permute-start.3 = (f32[96,128]{1,0:T(8,128)S(1)}, f32[96,128]{1,0:T(8,128)S(1)}, u32[]{:S(2)}, u32[]{:S(2)}) collective-permute-start(f32[96,128]{1,0:T(8,128)S(1)} %constant_dynamic-update-slice_fusion.column), channel_id=1, source_target_pairs={{0,7},{1,0},{2,1},{3,2},{4,3},{5,4},{6,5},{7,6},{8,15},{9,8},{10,9... | collective-permute-start | bytes 147464 | tf_op jit(solution)/shard_map/ppermute | solution.py:305
  17.3 4.6 %collective-permute-start.2 = (f32[96,128]{1,0:T(8,128)S(1)}, f32[96,128]{1,0:T(8,128)S(1)}, u32[]{:S(2)}, u32[]{:S(2)}) collective-permute-start(f32[96,128]{1,0:T(8,128)S(1)} %constant_dynamic-update-slice_fusion.column), channel_id=1, source_target_pairs={{0,1},{1,2},{2,3},{3,4},{4,5},{5,6},{6,7},{7,0},{8,9},{9,10},{10,1... | collective-permute-start | bytes 147464 | tf_op jit(solution)/shard_map/ppermute | solution.py:303
  18.6 2.2 %copy-start = (f32[32,64,512]{2,1,0:T(8,128)S(1)}, f32[32,64,512]{2,1,0:T(8,128)}, u32[]{:S(2)}) copy-start(f32[32,64,512]{2,1,0:T(8,128)} %features.9) | copy-start | bytes 12582916
  27.3 5.9 %collective-permute-start.4 = (f32[32,128]{1,0:T(8,128)S(1)}, f32[32,128]{1,0:T(8,128)S(1)}, u32[]{:S(2)}, u32[]{:S(2)}) collective-permute-start(f32[32,128]{1,0:T(8,128)S(1)} %get-tuple-element.21), channel_id=1, source_target_pairs={{0,8},{8,16},{16,24},{24,32},{32,40},{40,48},{48,56},{56,64},{64,7... | collective-permute-start | bytes 49160 | tf_op jit(solution)/shard_map/ppermute | solution.py:300
  27.4 5.9 %collective-permute-start.5 = (f32[32,128]{1,0:T(8,128)S(1)}, f32[32,128]{1,0:T(8,128)S(1)}, u32[]{:S(2)}, u32[]{:S(2)}) collective-permute-start(f32[32,128]{1,0:T(8,128)S(1)} %get-tuple-element.21), channel_id=1, source_target_pairs={{0,248},{8,0},{16,8},{24,16},{32,24},{40,32},{48,40},{56,48},{64,5... | collective-permute-start | bytes 49160 | tf_op jit(solution)/shard_map/ppermute | solution.py:300
  33.3 3.7 %collective-permute-start.7 = (f32[96,128]{1,0:T(8,128)S(1)}, f32[96,128]{1,0:T(8,128)S(1)}, u32[]{:S(2)}, u32[]{:S(2)}) collective-permute-start(f32[96,128]{1,0:T(8,128)S(1)} %constant_dynamic-update-slice_fusion.3.column), channel_id=1, source_target_pairs={{0,7},{1,0},{2,1},{3,2},{4,3},{5,4},{6,5},{7,6},{8,15},{9,8},{10,9... | collective-permute-start | bytes 147464 | tf_op jit(solution)/shard_map/ppermute | solution.py:305
  36.1 1.3 %collective-permute-start.6 = (f32[96,128]{1,0:T(8,128)S(1)}, f32[96,128]{1,0:T(8,128)S(1)}, u32[]{:S(2)}, u32[]{:S(2)}) collective-permute-start(f32[96,128]{1,0:T(8,128)S(1)} %constant_dynamic-update-slice_fusion.3.column), channel_id=1, source_target_pairs={{0,1},{1,2},{2,3},{3,4},{4,5},{5,6},{6,7},{7,0},{8,9},{9,10},{10,1... | collective-permute-start | bytes 147464 | tf_op jit(solution)/shard_map/ppermute | solution.py:303
  37.4 45.9 %copy-start.3 = (f32[64,1024]{1,0:T(8,128)S(1)}, f32[64,1024]{1,0:T(8,128)}, u32[]{:S(2)}) copy-start(f32[64,1024]{1,0:T(8,128)} %vertex_features.1) | copy-start | bytes 786436
  37.4 45.9 %copy-start.4 = (s32[1024]{0:T(1024)S(1)}, s32[1024]{0:T(1024)}, u32[]{:S(2)}) copy-start(s32[1024]{0:T(1024)} %param.11) | copy-start | bytes 12292
  40.6 6.2 %collective-permute-start.8 = (f32[32,128]{1,0:T(8,128)S(1)}, f32[32,128]{1,0:T(8,128)S(1)}, u32[]{:S(2)}, u32[]{:S(2)}) collective-permute-start(f32[32,128]{1,0:T(8,128)S(1)} %get-tuple-element.26), channel_id=1, source_target_pairs={{0,8},{8,16},{16,24},{24,32},{32,40},{40,48},{48,56},{56,64},{64,7... | collective-permute-start | bytes 49160 | tf_op jit(solution)/shard_map/ppermute | solution.py:300
  40.7 6.1 %collective-permute-start.9 = (f32[32,128]{1,0:T(8,128)S(1)}, f32[32,128]{1,0:T(8,128)S(1)}, u32[]{:S(2)}, u32[]{:S(2)}) collective-permute-start(f32[32,128]{1,0:T(8,128)S(1)} %get-tuple-element.26), channel_id=1, source_target_pairs={{0,248},{8,0},{16,8},{24,16},{32,24},{40,32},{48,40},{56,48},{64,5... | collective-permute-start | bytes 49160 | tf_op jit(solution)/shard_map/ppermute | solution.py:300
  46.8 5.8 %collective-permute-start.11 = (f32[96,128]{1,0:T(8,128)S(1)}, f32[96,128]{1,0:T(8,128)S(1)}, u32[]{:S(2)}, u32[]{:S(2)}) collective-permute-start(f32[96,128]{1,0:T(8,128)S(1)} %constant_dynamic-update-slice_fusion.6.column), channel_id=1, source_target_pairs={{0,7},{1,0},{2,1},{3,2},{4,3},{5,4},{6,5},{7,6},{8,15},{9,8},{10,9... | collective-permute-start | bytes 147464 | tf_op jit(solution)/shard_map/ppermute | solution.py:305
  51.8 1.2 %collective-permute-start.10 = (f32[96,128]{1,0:T(8,128)S(1)}, f32[96,128]{1,0:T(8,128)S(1)}, u32[]{:S(2)}, u32[]{:S(2)}) collective-permute-start(f32[96,128]{1,0:T(8,128)S(1)} %constant_dynamic-update-slice_fusion.6.column), channel_id=1, source_target_pairs={{0,1},{1,2},{2,3},{3,4},{4,5},{5,6},{6,7},{7,0},{8,9},{9,10},{10,1... | collective-permute-start | bytes 147464 | tf_op jit(solution)/shard_map/ppermute | solution.py:303

commit v5 on v3

--- a/solution.py
+++ b/solution.py
@@ -11,7 +11,7 @@
 SHIFT = 1.25
 LANES = 128
 MOMENTS = 2 * ITERS
-CHUNKS = 8
+CHUNKS = 16
 MOMENT_LANE = 96
 FIRST_LIMIT = 60
 VMEM = pl.BlockSpec(memory_space=pltpu.VMEM)
@@ -117,18 +117,33 @@
     return jnp.concatenate([third, jnp.zeros((LANES - third.shape[0], third.shape[1]), third.dtype)])
 
 
-def own_kernel(shape, index, block, features, out):
+def third_of(table, d):
+    return table[:, d * LANES : (d + 1) * LANES]
+
+
+def own_kernel(shape, index, block, features, own, copy):
     nrows, width, slots, across = shape
+    copy[...] = block[...]
     place = positions(block[...], nrows, across, index[0], index[1])
-    out[...] = one_hot(place, 0, 3 * LANES, width, slots)
-
-
-def middle_kernel(shape, index, column, own, out):
+    own[...] = one_hot(place, 0, 3 * LANES, width, slots)
+
+
+def middle_kernel(shape, index, column, own, twice):
     nrows, width, slots, across = shape
     others = jnp.concatenate([column[:nrows, :], column[2 * nrows :, :]], axis=0)
     place = positions(others, nrows, across, index[0], index[1])
     hot = one_hot(place, 0, 3 * LANES, width, slots)
-    out[...] = padded(jnp.concatenate([hot[:nrows], own[...], hot[nrows:]], axis=0))
+    mine = own[...]
+    centre = padded(jnp.concatenate([hot[:nrows], mine, hot[nrows:]], axis=0))
+    known = jnp.dot(third_of(mine, 1), centre, preferred_element_type=F32)
+    extra = [
+        lax.dot_general(
+            third_of(mine, d), third_of(centre, d), (((1,), (1,)), ((), ())), preferred_element_type=F32
+        )
+        for d in (0, 2)
+    ]
+    parts = [third_of(known, 0), third_of(known, 1) + extra[0] + extra[1], third_of(known, 2)]
+    twice[...] = jnp.concatenate(parts, axis=1)
 
 
 def advance(step, nrows, width, weights, around, features, diagonal, before, sums, moments, outs):
@@ -148,16 +163,16 @@
     moved = pltpu.roll(turned, shift, 1) if shift else turned
     sums = jnp.where((lanes >= shift) & (lanes < shift + nrows), moved, sums)
     old = before[...]
-    base = (diagonal[...] - SHIFT) * old
+    images = [
+        jnp.sum(features[b] * turned[:, nrows + b : nrows + b + 1], axis=0, keepdims=True)
+        for b in range(nrows)
+    ]
+    new = (diagonal[...] - SHIFT) * old + jnp.concatenate(images, axis=0)
+    outs[0][...] = new
     columns = jnp.zeros((width, LANES), F32)
-    for b in range(nrows):
-        second = turned[:, nrows + b : nrows + b + 1]
-        image = jnp.sum(features[b] * second, axis=0, keepdims=True)
-        new = base[b : b + 1, :] + image
-        outs[0][b : b + 1, :] = new
-        if not last:
-            columns = project(features[b], new, columns, b)
-    new = outs[0][...]
+    if not last:
+        for b in range(nrows):
+            columns = project(features[b], outs[0][b : b + 1, :], columns, b)
     moments = put(moments, MOMENT_LANE + 2 * step + 1, total(old * new))
     if not last:
         moments = put(moments, MOMENT_LANE + 2 * step + 2, total(new * new))
@@ -165,25 +180,19 @@
 
 
 def second_kernel(
-    shape, index, left, column, right, middle, features, diagonal, before, moments,
+    shape, index, left, column, right, own, known, features, diagonal, before, moments,
     new, block, sums_out, moments_out, weights_out,
 ):
     nrows, width, slots, across = shape
-    own = middle[nrows : 2 * nrows, :]
-    pieces = [own[:, d * LANES : (d + 1) * LANES] for d in range(3)]
-    centre = middle[...]
-    thirds = [jnp.dot(pieces[1], centre[:, d * LANES : (d + 1) * LANES], preferred_element_type=F32) for d in range(3)]
+    mine = own[...]
+    thirds = [third_of(known, d) for d in range(3)]
     for d, side in ((0, left), (2, right)):
         place = positions(side[...], nrows, across, index[0], index[1])
         hot = padded(one_hot(place, d * LANES, LANES, width, slots))
-        thirds[d] = thirds[d] + jnp.dot(pieces[d], hot, preferred_element_type=F32)
-        across_dy = centre[:, d * LANES : (d + 1) * LANES]
-        thirds[1] = thirds[1] + lax.dot_general(
-            pieces[d], across_dy, (((1,), (1,)), ((), ())), preferred_element_type=F32
-        )
+        thirds[d] = thirds[d] + jnp.dot(third_of(mine, d), hot, preferred_element_type=F32)
     twice = jnp.concatenate(thirds, axis=1).astype(BF16)
     pad = jnp.zeros((LANES - 2 * nrows, 3 * LANES), BF16)
-    weights = jnp.concatenate([own, twice, pad], axis=0)
+    weights = jnp.concatenate([mine, twice, pad], axis=0)
     weights_out[...] = weights
     around = jnp.concatenate([padded(side[...]) for side in (left, column, right)], axis=0)
     sums, moment, columns = advance(
@@ -299,10 +308,9 @@
     vertices_out[...] = sum(w * vertices[i : i + 1, :] for i, w in enumerate(field))
 
 
-def neighbourhood(block):
-    column = jnp.concatenate(
-        [lax.ppermute(block, "gx", ring("gx", 1)), block, lax.ppermute(block, "gx", ring("gx", -1))]
-    )
+def neighbourhood(block, copy=None):
+    up, down = lax.ppermute(block, "gx", ring("gx", 1)), lax.ppermute(block, "gx", ring("gx", -1))
+    column = jnp.concatenate([up, block if copy is None else copy, down])
     return (
         lax.ppermute(column, "gy", ring("gy", 1)),
         column,
@@ -330,20 +338,21 @@
             pltpu.SemaphoreType.DMA((CHUNKS + 2,)),
         ],
     )
-    own = call(
-        functools.partial(own_kernel, shape), jax.ShapeDtypeStruct((nrows, 3 * LANES), BF16),
+    own, copy = call(
+        functools.partial(own_kernel, shape),
+        [jax.ShapeDtypeStruct((nrows, 3 * LANES), BF16), block_shape],
         index, block, features, specs=[smem, VMEM, VMEM],
     )
-    left, column, right = neighbourhood(block)
-    middle = call(
-        functools.partial(middle_kernel, shape), jax.ShapeDtypeStruct((LANES, 3 * LANES), BF16),
+    left, column, right = neighbourhood(block, copy)
+    known = call(
+        functools.partial(middle_kernel, shape), f32(nrows, 3 * LANES),
         index, column, own, specs=[smem, VMEM, VMEM],
     )
     v1, block, sums, moments, weights = call(
         functools.partial(second_kernel, shape),
         [power, block_shape, table, row, jax.ShapeDtypeStruct((LANES, 3 * LANES), BF16)],
-        index, left, column, right, middle, features, diagonal, right_side, moments,
-        specs=[smem] + [VMEM] * 8,
+        index, left, column, right, own, known, features, diagonal, right_side, moments,
+        specs=[smem] + [VMEM] * 9,
     )
     left, column, right = neighbourhood(block)
     v2, block, sums, moments = call(

time: 85.9 us -> 81.9 us (0.953)
  Pallas kernels: 17.3 us -> 13.3 us
  local copies, waits for them, and re-layouts: 4.06 us -> 2.95 us
    pallas_call x9, Pallas kernels: 17.3 us -> 13.3 us  [call(): pl.pallas_call(kernel, out_shape=out_shape, in_specs=specs or [VMEM] * le...]
    ppermute x3, starting transfers between devices: 8.14 us -> 10.5 us  [neighbourhood(): lax.ppermute(column, 'gy', ring('gy', -1))]
    ppermute x3, starting transfers between devices: 16.4 us -> 18.6 us  [neighbourhood(): lax.ppermute(block, 'gx', ring('gx', -1))]
    ppermute x3, starting transfers between devices: 2.2 us -> 0.08 us  [neighbourhood(): lax.ppermute(block, 'gx', ring('gx', 1))]
    all_to_all x1, starting transfers between devices: 8.35 us -> 6.71 us  [per_device(): lax.all_to_all(call(fold_kernel, f32(along, LANES), slab), 'gx', 0, 0, ti...]
    unnamed x22, local copies, waits for them, and re-layouts: 4.05 us -> 2.94 us
    ppermute x3, waiting for transfers between devices: 3.41 us -> 4.52 us  [neighbourhood(): lax.ppermute(block, 'gx', ring('gx', 1))]
  transfers between devices with their start and end apart: 13 -> 13, of which waited for: 8 -> 9; matrix products, arithmetic and copies ran while one was open for 1% -> 0% of each run, Pallas kernels for 3% -> 4%
where the time goes in v5:
time: 81.9 us; the launch traced here: 81.6 us
  starting transfers between devices  37.1 us (45%)
  waiting for transfers between devices  14.9 us (18%)
  Pallas kernels  13.3 us (16%)
  blocking collectives  12.4 us (15%)
  local copies, waits for them, and re-layouts  2.95 us (4%)
    ppermute x3, starting transfers between devices, neighbourhood(): lax.ppermute(block, 'gx', ring('gx', -1))  18.6 us
    pallas_call x9, Pallas kernels, call(): pl.pallas_call(kernel, out_shape=out_shape, in_specs=specs or [VMEM] * le...  13.3 us
    all_to_all x1, blocking collectives, per_device(): slab = lax.all_to_all(sums, 'gy', 0, 0, tiled=True)  12.4 us
    ppermute x3, starting transfers between devices, neighbourhood(): lax.ppermute(column, 'gy', ring('gy', -1))  10.5 us
    all_to_all x1, waiting for transfers between devices, per_device(): lax.all_to_all(call(fold_kernel, f32(along, LANES), slab), 'gx', 0, 0, ti...  7.3 us
    all_to_all x1, starting transfers between devices, per_device(): lax.all_to_all(call(fold_kernel, f32(along, LANES), slab), 'gx', 0, 0, ti...  6.71 us
    ppermute x3, waiting for transfers between devices, neighbourhood(): lax.ppermute(block, 'gx', ring('gx', 1))  4.52 us
    unnamed x22, local copies, waits for them, and re-layouts  2.94 us
  transfers between devices with their start and end apart: 13, of which 9 were waited for; matrix products, arithmetic and copies ran while one was open for 0% of the time, Pallas kernels for 4%

profile of v5, /device:TPU:1, one launch (start us, length us, event | category | flops | bytes accessed | tf_op | source)
XLA Modules:
  0.0 81.6 jit_solution(7153213113593255559)
XLA Ops:
  0.7 3.4 %shard_map.85 = (f32[32,128]{1,0:T(8,128)}, f32[1,128]{1,0:T(1,128)}) custom-call(f32[32,64,512]{2,1,0:T(8,128)} %features.9, f32[32,512]{1,0:T(8,128)} %v0.1, s32[32,27]{1,0:T(8,128)} %neighbours.1), custom_call_target="tpu_custom_call" | custom-call | tf_op jit(solution)/shard_map/pallas_call | solution.py:23
  4.1 8.7 %collective-permute-start.1 = (f32[32,128]{1,0:T(8,128)}, f32[32,128]{1,0:T(8,128)S(1)}, u32[]{:S(2)}, u32[]{:S(2)}) collective-permute-start(f32[32,128]{1,0:T(8,128)} %get-tuple-element.21.block), channel_id=1, source_target_pairs={{0,248},{8,0},{16,8},{24,16},{32,24},{40,32},{48,40},{56,48},{64,5... | collective-permute-start | bytes 49160 | tf_op jit(solution)/shard_map/ppermute | solution.py:312
  12.8 0.1 pad_add_fusion.index
  12.9 2.2 %copy-done = f32[32,64,512]{2,1,0:T(8,128)S(1)} copy-done((f32[32,64,512]{2,1,0:T(8,128)S(1)}, f32[32,64,512]{2,1,0:T(8,128)}, u32[]{:S(2)}) %copy-start) | copy-done | bytes 4194328
  15.0 0.7 copy-done.5
  15.8 0.8 shard_map.86
  16.5 2.4 %collective-permute-done = f32[32,128]{1,0:T(8,128)S(1)} collective-permute-done((f32[32,128]{1,0:T(8,128)}, f32[32,128]{1,0:T(8,128)S(1)}, u32[]{:S(2)}, u32[]{:S(2)}) %collective-permute-start) | collective-permute-done | bytes 16416 | tf_op jit(solution)/shard_map/ppermute | solution.py:312
  18.9 2.1 %collective-permute-start.3 = (f32[96,128]{1,0:T(8,128)S(1)}, f32[96,128]{1,0:T(8,128)S(1)}, u32[]{:S(2)}, u32[]{:S(2)}) collective-permute-start(f32[96,128]{1,0:T(8,128)S(1)} %constant_dynamic-update-slice_fusion.column), channel_id=1, source_target_pairs={{0,7},{1,0},{2,1},{3,2},{4,3},{5,4},{6,5},{7,6},{8,15},{9,8},{10,9... | collective-permute-start | bytes 147464 | tf_op jit(solution)/shard_map/ppermute | solution.py:317
  21.0 1.2 %collective-permute-start.2 = (f32[96,128]{1,0:T(8,128)S(1)}, f32[96,128]{1,0:T(8,128)S(1)}, u32[]{:S(2)}, u32[]{:S(2)}) collective-permute-start(f32[96,128]{1,0:T(8,128)S(1)} %constant_dynamic-update-slice_fusion.column), channel_id=1, source_target_pairs={{0,1},{1,2},{2,3},{3,4},{4,5},{5,6},{6,7},{7,0},{8,9},{9,10},{10,1... | collective-permute-start | bytes 147464 | tf_op jit(solution)/shard_map/ppermute | solution.py:315
  22.2 1.1 %shard_map.87.known = f32[32,384]{1,0:T(8,128)S(1)} custom-call(s32[2]{0:T(128)S(1)} %pad_add_fusion.index, f32[96,128]{1,0:T(8,128)S(1)} %constant_dynamic-update-slice_fusion.column, bf16[32,384]{1,0:T(8,128)(2,1)S(1)} %get-tuple-element.23.own), custom_call_target="tpu_custom_call" | custom-call | tf_op jit(solution)/shard_map/pallas_call | solution.py:23
  23.3 0.7 collective-permute-done.3.right
  24.0 2.8 %shard_map.88 = (f32[32,512]{1,0:T(8,128)S(1)}, f32[32,128]{1,0:T(8,128)S(1)}, f32[64,128]{1,0:T(8,128)S(1)}, f32[1,128]{1,0:T(1,128)S(1)}, bf16[128,384]{1,0:T(8,128)(2,1)S(1)}) custom-call(s32[2]{0:T(128)S(1)} %pad_add_fusion.index, f32[96,128]{1,0:T(8,128)S(1)} %collective-permute-done.2.left, f32[96,128]{1,0:T(8,128)S(1)} %constant_dynamic-update-slice_fusion.column, ...), custom_call_target="tpu_custom_call" | custom-call | tf_op jit(solution)/shard_map/pallas_call | solution.py:23
  26.8 0.0 collective-permute-start.4
  26.8 4.8 %collective-permute-start.5 = (f32[32,128]{1,0:T(8,128)S(1)}, f32[32,128]{1,0:T(8,128)S(1)}, u32[]{:S(2)}, u32[]{:S(2)}) collective-permute-start(f32[32,128]{1,0:T(8,128)S(1)} %get-tuple-element.25), channel_id=1, source_target_pairs={{0,248},{8,0},{16,8},{24,16},{32,24},{40,32},{48,40},{56,48},{64,5... | collective-permute-start | bytes 49160 | tf_op jit(solution)/shard_map/ppermute | solution.py:312
  31.6 1.1 %collective-permute-done.4 = f32[32,128]{1,0:T(8,128)S(1)} collective-permute-done((f32[32,128]{1,0:T(8,128)S(1)}, f32[32,128]{1,0:T(8,128)S(1)}, u32[]{:S(2)}, u32[]{:S(2)}) %collective-permute-start.4) | collective-permute-done | bytes 16416 | tf_op jit(solution)/shard_map/ppermute | solution.py:312
  32.8 3.9 %collective-permute-start.7 = (f32[96,128]{1,0:T(8,128)S(1)}, f32[96,128]{1,0:T(8,128)S(1)}, u32[]{:S(2)}, u32[]{:S(2)}) collective-permute-start(f32[96,128]{1,0:T(8,128)S(1)} %constant_dynamic-update-slice_fusion.3.column), channel_id=1, source_target_pairs={{0,7},{1,0},{2,1},{3,2},{4,3},{5,4},{6,5},{7,6},{8,15},{9,8},{10,9... | collective-permute-start | bytes 147464 | tf_op jit(solution)/shard_map/ppermute | solution.py:317
  36.7 0.9 %collective-permute-done.7.right = f32[96,128]{1,0:T(8,128)S(1)} collective-permute-done((f32[96,128]{1,0:T(8,128)S(1)}, f32[96,128]{1,0:T(8,128)S(1)}, u32[]{:S(2)}, u32[]{:S(2)}) %collective-permute-start.7) | collective-permute-done | bytes 49184 | tf_op jit(solution)/shard_map/ppermute | solution.py:317
  37.6 0.3 collective-permute-done.6.left
  37.9 1.5 %shard_map.89 = (f32[32,512]{1,0:T(8,128)S(1)}, f32[32,128]{1,0:T(8,128)S(1)}, f32[64,128]{1,0:T(8,128)S(1)}, f32[1,128]{1,0:T(1,128)S(1)}) custom-call(f32[96,128]{1,0:T(8,128)S(1)} %collective-permute-done.6.left, f32[96,128]{1,0:T(8,128)S(1)} %constant_dynamic-update-slice_fusion.3.column, f32[96,128]{1,0:T(8,128)S(1)} %collective-permute-done.7.right, ...), custom_call_target="tpu_custom_call" | custom-call | tf_op jit(solution)/shard_map/pallas_call | solution.py:23
  39.4 0.0 collective-permute-start.8
  39.4 5.1 %collective-permute-start.9 = (f32[32,128]{1,0:T(8,128)S(1)}, f32[32,128]{1,0:T(8,128)S(1)}, u32[]{:S(2)}, u32[]{:S(2)}) collective-permute-start(f32[32,128]{1,0:T(8,128)S(1)} %get-tuple-element.30), channel_id=1, source_target_pairs={{0,248},{8,0},{16,8},{24,16},{32,24},{40,32},{48,40},{56,48},{64,5... | collective-permute-start | bytes 49160 | tf_op jit(solution)/shard_map/ppermute | solution.py:312
  44.5 1.0 %collective-permute-done.8 = f32[32,128]{1,0:T(8,128)S(1)} collective-permute-done((f32[32,128]{1,0:T(8,128)S(1)}, f32[32,128]{1,0:T(8,128)S(1)}, u32[]{:S(2)}, u32[]{:S(2)}) %collective-permute-start.8) | collective-permute-done | bytes 16416 | tf_op jit(solution)/shard_map/ppermute | solution.py:312
  45.6 4.4 %collective-permute-start.11 = (f32[96,128]{1,0:T(8,128)S(1)}, f32[96,128]{1,0:T(8,128)S(1)}, u32[]{:S(2)}, u32[]{:S(2)}) collective-permute-start(f32[96,128]{1,0:T(8,128)S(1)} %constant_dynamic-update-slice_fusion.6.column), channel_id=1, source_target_pairs={{0,7},{1,0},{2,1},{3,2},{4,3},{5,4},{6,5},{7,6},{8,15},{9,8},{10,9... | collective-permute-start | bytes 147464 | tf_op jit(solution)/shard_map/ppermute | solution.py:317
  50.0 0.9 %collective-permute-done.11.right = f32[96,128]{1,0:T(8,128)S(1)} collective-permute-done((f32[96,128]{1,0:T(8,128)S(1)}, f32[96,128]{1,0:T(8,128)S(1)}, u32[]{:S(2)}, u32[]{:S(2)}) %collective-permute-start.11) | collective-permute-done | bytes 49184 | tf_op jit(solution)/shard_map/ppermute | solution.py:317
  50.9 0.3 collective-permute-done.10.left
  51.3 1.1 %shard_map.90 = (f32[32,512]{1,0:T(8,128)S(1)}, f32[8,64,128]{2,1,0:T(8,128)S(1)}) custom-call(f32[96,128]{1,0:T(8,128)S(1)} %collective-permute-done.10.left, f32[96,128]{1,0:T(8,128)S(1)} %constant_dynamic-update-slice_fusion.6.column, f32[96,128]{1,0:T(8,128)S(1)} %collective-permute-done.11.right, bf16[128,384]{1,0:T(8,128)(2,1)S(1)} %get-tuple-element.26.weights, ...), custom_call_target="tpu_custom_call" | custom-call | tf_op jit(solution)/shard_map/pallas_call | solution.py:23
  52.4 12.4 %all_to_all.16.slab = f32[8,64,128]{2,1,0:T(8,128)S(1)} all-to-all(f32[8,64,128]{2,1,0:T(8,128)S(1)} %get-tuple-element.34), channel_id=1, replica_groups=mesh['gx'=32,'gy'=8] {'gy'}, dimensions={0} | all-to-all | bytes 524288 | tf_op jit(solution)/shard_map/all_to_all | solution.py:367
  64.8 0.6 shard_map.91
  65.4 6.7 %all-to-all-start.1 = ((f32[32,1,128]{2,1,0:T(1,128)}), f32[32,1,128]{2,1,0:T(1,128)S(1)}, u32[]{:S(2)}, u32[]{:S(2)}) async-start(f32[32,1,128]{2,1,0:T(1,128)} %bitcast.3), calls=%async_computation.1 | async-start | bytes 32768 | tf_op jit(solution)/shard_map/all_to_all | solution.py:368
  72.2 1.2 %shard_map.92.vertices = f32[8,1024]{1,0:T(8,128)S(1)} custom-call(s32[2]{0:T(128)S(1)} %pad_add_fusion.index, f32[8,64,128]{2,1,0:T(8,128)S(1)} %all_to_all.16.slab, s32[1,1024]{1,0:T(1,128)S(1)} %bitcast.9, f32[64,1024]{1,0:T(8,128)S(1)} %copy-done.4), custom_call_target="tpu_custom_call" | custom-call | tf_op jit(solution)/shard_map/pallas_call | solution.py:23
  73.3 7.3 %all-to-all-done.1 = f32[32,1,128]{2,1,0:T(1,128)S(1)} async-done(((f32[32,1,128]{2,1,0:T(1,128)}), f32[32,1,128]{2,1,0:T(1,128)S(1)}, u32[]{:S(2)}, u32[]{:S(2)}) %all-to-all-start.1) | async-done | bytes 16416 | tf_op jit(solution)/shard_map/all_to_all | solution.py:368
  80.6 0.9 %shard_map.93 = (f32[32,512]{1,0:T(8,128)}, f32[32,512]{1,0:T(8,128)}, f32[1,1024]{1,0:T(1,128)}) custom-call(f32[32,128]{1,0:T(8,128)S(1)} %bitcast.8, f32[32,512]{1,0:T(8,128)S(1)} %copy-done.3, f32[32,512]{1,0:T(8,128)S(1)} %get-tuple-element.27.before.v1, f32[32,512]{1,0:T(8,128)S(1)} %get-tuple-element.31.before.v2, ...), custom_call_target="tpu_custom_call" | custom-call | tf_op jit(solution)/shard_map/pallas_call | solution.py:23
  (30 shorter events, 0.1 us)
Async XLA Ops:
  0.6 23.4 %copy-start.3 = (f32[32,512]{1,0:T(8,128)S(1)}, f32[32,512]{1,0:T(8,128)}, u32[]{:S(2)}) copy-start(f32[32,512]{1,0:T(8,128)} %v0.1) | copy-start | bytes 196612
  0.6 23.4 %copy-start.2 = (f32[32,512]{1,0:T(8,128)S(1)}, f32[32,512]{1,0:T(8,128)}, u32[]{:S(2)}) copy-start(f32[32,512]{1,0:T(8,128)} %diagonal.5) | copy-start | bytes 196612
  4.1 19.9 %copy-start.7 = (f32[1,128]{1,0:T(1,128)S(1)}, f32[1,128]{1,0:T(1,128)}, u32[]{:S(2)}) copy-start(f32[1,128]{1,0:T(1,128)} %get-tuple-element.24.moments) | copy-start | bytes 1540
  4.1 14.8 %collective-permute-start.1 = (f32[32,128]{1,0:T(8,128)}, f32[32,128]{1,0:T(8,128)S(1)}, u32[]{:S(2)}, u32[]{:S(2)}) collective-permute-start(f32[32,128]{1,0:T(8,128)} %get-tuple-element.21.block), channel_id=1, source_target_pairs={{0,248},{8,0},{16,8},{24,16},{32,24},{40,32},{48,40},{56,48},{64,5... | collective-permute-start | bytes 49160 | tf_op jit(solution)/shard_map/ppermute | solution.py:312
  12.8 6.1 %collective-permute-start = (f32[32,128]{1,0:T(8,128)}, f32[32,128]{1,0:T(8,128)S(1)}, u32[]{:S(2)}, u32[]{:S(2)}) collective-permute-start(f32[32,128]{1,0:T(8,128)} %get-tuple-element.21.block), channel_id=1, source_target_pairs={{0,8},{8,16},{16,24},{24,32},{32,40},{40,48},{48,56},{56,64},{64,7... | collective-permute-start | bytes 49160 | tf_op jit(solution)/shard_map/ppermute | solution.py:312
  12.9 2.2 %copy-start = (f32[32,64,512]{2,1,0:T(8,128)S(1)}, f32[32,64,512]{2,1,0:T(8,128)}, u32[]{:S(2)}) copy-start(f32[32,64,512]{2,1,0:T(8,128)} %features.9) | copy-start | bytes 12582916
  15.0 0.7 copy-start.5
  15.8 8.3 %copy-start.1 = (f32[32,64,512]{2,1,0:T(8,128)S(1)}, f32[32,64,512]{2,1,0:T(8,128)}, u32[]{:S(2)}) copy-start(f32[32,64,512]{2,1,0:T(8,128)} %features.9) | copy-start | bytes 12582916
  18.9 5.1 %collective-permute-start.3 = (f32[96,128]{1,0:T(8,128)S(1)}, f32[96,128]{1,0:T(8,128)S(1)}, u32[]{:S(2)}, u32[]{:S(2)}) collective-permute-start(f32[96,128]{1,0:T(8,128)S(1)} %constant_dynamic-update-slice_fusion.column), channel_id=1, source_target_pairs={{0,7},{1,0},{2,1},{3,2},{4,3},{5,4},{6,5},{7,6},{8,15},{9,8},{10,9... | collective-permute-start | bytes 147464 | tf_op jit(solution)/shard_map/ppermute | solution.py:317
  21.0 3.0 %collective-permute-start.2 = (f32[96,128]{1,0:T(8,128)S(1)}, f32[96,128]{1,0:T(8,128)S(1)}, u32[]{:S(2)}, u32[]{:S(2)}) collective-permute-start(f32[96,128]{1,0:T(8,128)S(1)} %constant_dynamic-update-slice_fusion.column), channel_id=1, source_target_pairs={{0,1},{1,2},{2,3},{3,4},{4,5},{5,6},{6,7},{7,0},{8,9},{9,10},{10,1... | collective-permute-start | bytes 147464 | tf_op jit(solution)/shard_map/ppermute | solution.py:315
  26.8 5.9 %collective-permute-start.4 = (f32[32,128]{1,0:T(8,128)S(1)}, f32[32,128]{1,0:T(8,128)S(1)}, u32[]{:S(2)}, u32[]{:S(2)}) collective-permute-start(f32[32,128]{1,0:T(8,128)S(1)} %get-tuple-element.25), channel_id=1, source_target_pairs={{0,8},{8,16},{16,24},{24,32},{32,40},{40,48},{48,56},{56,64},{64,7... | collective-permute-start | bytes 49160 | tf_op jit(solution)/shard_map/ppermute | solution.py:312
  26.8 5.9 %collective-permute-start.5 = (f32[32,128]{1,0:T(8,128)S(1)}, f32[32,128]{1,0:T(8,128)S(1)}, u32[]{:S(2)}, u32[]{:S(2)}) collective-permute-start(f32[32,128]{1,0:T(8,128)S(1)} %get-tuple-element.25), channel_id=1, source_target_pairs={{0,248},{8,0},{16,8},{24,16},{32,24},{40,32},{48,40},{56,48},{64,5... | collective-permute-start | bytes 49160 | tf_op jit(solution)/shard_map/ppermute | solution.py:312
  32.8 4.8 %collective-permute-start.7 = (f32[96,128]{1,0:T(8,128)S(1)}, f32[96,128]{1,0:T(8,128)S(1)}, u32[]{:S(2)}, u32[]{:S(2)}) collective-permute-start(f32[96,128]{1,0:T(8,128)S(1)} %constant_dynamic-update-slice_fusion.3.column), channel_id=1, source_target_pairs={{0,7},{1,0},{2,1},{3,2},{4,3},{5,4},{6,5},{7,6},{8,15},{9,8},{10,9... | collective-permute-start | bytes 147464 | tf_op jit(solution)/shard_map/ppermute | solution.py:317
  36.7 1.2 %collective-permute-start.6 = (f32[96,128]{1,0:T(8,128)S(1)}, f32[96,128]{1,0:T(8,128)S(1)}, u32[]{:S(2)}, u32[]{:S(2)}) collective-permute-start(f32[96,128]{1,0:T(8,128)S(1)} %constant_dynamic-update-slice_fusion.3.column), channel_id=1, source_target_pairs={{0,1},{1,2},{2,3},{3,4},{4,5},{5,6},{6,7},{7,0},{8,9},{9,10},{10,1... | collective-permute-start | bytes 147464 | tf_op jit(solution)/shard_map/ppermute | solution.py:315
  37.9 34.2 %copy-start.4 = (f32[64,1024]{1,0:T(8,128)S(1)}, f32[64,1024]{1,0:T(8,128)}, u32[]{:S(2)}) copy-start(f32[64,1024]{1,0:T(8,128)} %vertex_features.1) | copy-start | bytes 786436
  37.9 34.2 %copy-start.6 = (s32[1024]{0:T(1024)S(1)}, s32[1024]{0:T(1024)}, u32[]{:S(2)}) copy-start(s32[1024]{0:T(1024)} %param.11) | copy-start | bytes 12292
  39.4 6.2 %collective-permute-start.8 = (f32[32,128]{1,0:T(8,128)S(1)}, f32[32,128]{1,0:T(8,128)S(1)}, u32[]{:S(2)}, u32[]{:S(2)}) collective-permute-start(f32[32,128]{1,0:T(8,128)S(1)} %get-tuple-element.30), channel_id=1, source_target_pairs={{0,8},{8,16},{16,24},{24,32},{32,40},{40,48},{48,56},{56,64},{64,7... | collective-permute-start | bytes 49160 | tf_op jit(solution)/shard_map/ppermute | solution.py:312
  39.4 6.2 %collective-permute-start.9 = (f32[32,128]{1,0:T(8,128)S(1)}, f32[32,128]{1,0:T(8,128)S(1)}, u32[]{:S(2)}, u32[]{:S(2)}) collective-permute-start(f32[32,128]{1,0:T(8,128)S(1)} %get-tuple-element.30), channel_id=1, source_target_pairs={{0,248},{8,0},{16,8},{24,16},{32,24},{40,32},{48,40},{56,48},{64,5... | collective-permute-start | bytes 49160 | tf_op jit(solution)/shard_map/ppermute | solution.py:312
  45.6 5.3 %collective-permute-start.11 = (f32[96,128]{1,0:T(8,128)S(1)}, f32[96,128]{1,0:T(8,128)S(1)}, u32[]{:S(2)}, u32[]{:S(2)}) collective-permute-start(f32[96,128]{1,0:T(8,128)S(1)} %constant_dynamic-update-slice_fusion.6.column), channel_id=1, source_target_pairs={{0,7},{1,0},{2,1},{3,2},{4,3},{5,4},{6,5},{7,6},{8,15},{9,8},{10,9... | collective-permute-start | bytes 147464 | tf_op jit(solution)/shard_map/ppermute | solution.py:317
  50.0 1.2 %collective-permute-start.10 = (f32[96,128]{1,0:T(8,128)S(1)}, f32[96,128]{1,0:T(8,128)S(1)}, u32[]{:S(2)}, u32[]{:S(2)}) collective-permute-start(f32[96,128]{1,0:T(8,128)S(1)} %constant_dynamic-update-slice_fusion.6.column), channel_id=1, source_target_pairs={{0,1},{1,2},{2,3},{3,4},{4,5},{5,6},{6,7},{7,0},{8,9},{9,10},{10,1... | collective-permute-start | bytes 147464 | tf_op jit(solution)/shard_map/ppermute | solution.py:315
  65.4 15.2 %all-to-all-start.1 = ((f32[32,1,128]{2,1,0:T(1,128)}), f32[32,1,128]{2,1,0:T(1,128)S(1)}, u32[]{:S(2)}, u32[]{:S(2)}) async-start(f32[32,1,128]{2,1,0:T(1,128)} %bitcast.3), calls=%async_computation.1 | async-start | bytes 32768 | tf_op jit(solution)/shard_map/all_to_all | solution.py:368

commit v6 on v5

--- a/solution.py
+++ b/solution.py
@@ -18,7 +18,7 @@
 F32, BF16 = jnp.float32, jnp.bfloat16
 
 
-def call(kernel, out_shape, *args, specs=None, scratch=(), limit=24):
+def call(kernel, out_shape, *args, specs=None, scratch=(), limit=12):
     many = isinstance(out_shape, (list, tuple))
     return pl.pallas_call(
         kernel,
@@ -146,42 +146,46 @@
     twice[...] = jnp.concatenate(parts, axis=1)
 
 
-def advance(step, nrows, width, weights, around, features, diagonal, before, sums, moments, outs):
-    last = step + 1 == ITERS
-    parts = []
-    rest = around
+def products(weights, values):
+    result, rest = None, values
     for _ in range(3):
         part = rest.astype(BF16)
         rest = rest - part.astype(F32)
-        parts.append(part)
-    result = jnp.dot(weights, parts[0], preferred_element_type=F32)
-    for part in parts[1:]:
-        result = result + jnp.dot(weights, part, preferred_element_type=F32)
-    turned = result.T[:width]
-    lanes = lane_iota(width)
-    shift = step * nrows
-    moved = pltpu.roll(turned, shift, 1) if shift else turned
-    sums = jnp.where((lanes >= shift) & (lanes < shift + nrows), moved, sums)
-    old = before[...]
+        value = jnp.dot(weights, part, preferred_element_type=F32)
+        result = value if result is None else result + value
+    return result
+
+
+def expand(result, nrows, features, shifted, old):
+    turned = result.T[: features.shape[1]]
     images = [
         jnp.sum(features[b] * turned[:, nrows + b : nrows + b + 1], axis=0, keepdims=True)
         for b in range(nrows)
     ]
-    new = (diagonal[...] - SHIFT) * old + jnp.concatenate(images, axis=0)
-    outs[0][...] = new
+    return shifted * old + jnp.concatenate(images, axis=0)
+
+
+def advance(step, weights, around, features, diagonal, before, moments, new, sums, block):
+    nrows, width, _ = features.shape
+    result = products(weights, around)
+    sums[...] = result[:nrows]
+    old, shifted = before[...], diagonal[...] - SHIFT
+    value = expand(result, nrows, features, shifted, old)
+    new[...] = value
     columns = jnp.zeros((width, LANES), F32)
-    if not last:
-        for b in range(nrows):
-            columns = project(features[b], outs[0][b : b + 1, :], columns, b)
-    moments = put(moments, MOMENT_LANE + 2 * step + 1, total(old * new))
-    if not last:
-        moments = put(moments, MOMENT_LANE + 2 * step + 2, total(new * new))
-    return sums, moments, columns
+    for b in range(nrows):
+        columns = project(features[b], new[b : b + 1, :], columns, b)
+    block[...] = to_rows(columns, nrows)
+    moments = put(moments, MOMENT_LANE + 2 * step + 1, total(old * value))
+    moments = put(moments, MOMENT_LANE + 2 * step + 2, total(value * value))
+    if step + 2 == ITERS:
+        moments = put(moments, MOMENT_LANE + 2 * step + 3, total(value * value * shifted))
+    return moments
 
 
 def second_kernel(
     shape, index, left, column, right, own, known, features, diagonal, before, moments,
-    new, block, sums_out, moments_out, weights_out,
+    new, block, sums, moments_out, weights_out, tables,
 ):
     nrows, width, slots, across = shape
     mine = own[...]
@@ -194,72 +198,88 @@
     pad = jnp.zeros((LANES - 2 * nrows, 3 * LANES), BF16)
     weights = jnp.concatenate([mine, twice, pad], axis=0)
     weights_out[...] = weights
+    tables[...] = jnp.concatenate([side[nrows : 2 * nrows, :] for side in (left, column, right)], axis=0)
     around = jnp.concatenate([padded(side[...]) for side in (left, column, right)], axis=0)
-    sums, moment, columns = advance(
-        0, nrows, width, weights, around, features, diagonal, before,
-        jnp.zeros((width, LANES), F32), moments[...], [new],
-    )
-    block[...] = to_rows(columns, nrows)
-    sums_out[...] = sums
-    moments_out[...] = moment
+    moments_out[...] = advance(
+        0, weights, around, features, diagonal, before, moments[...], new, sums, block
+    )
 
 
 def third_kernel(
-    left, column, right, weights, features, diagonal, before, sums, moments,
-    new, block, sums_out, moments_out,
+    left, column, right, weights, features, diagonal, before, moments, far, ahead,
+    new, block, sums, moments_out,
 ):
-    nrows, width, _ = features.shape
     around = jnp.concatenate([padded(side[...]) for side in (left, column, right)], axis=0)
-    total_sums, moment, columns = advance(
-        1, nrows, width, weights[...], around, features, diagonal, before,
-        sums[...], moments[...], [new],
-    )
-    block[...] = to_rows(columns, nrows)
-    sums_out[...] = total_sums
-    moments_out[...] = moment
-
-
-def fourth_kernel(
-    left, column, right, weights, features, diagonal, before, sums, moments,
-    new, sums_out,
-):
-    nrows, width, _ = features.shape
-    around = jnp.concatenate([padded(side[...]) for side in (left, column, right)], axis=0)
-    total_sums, moment, _ = advance(
-        2, nrows, width, weights[...], around, features, diagonal, before,
-        sums[...], moments[...], [new],
-    )
-    rows = lax.broadcasted_iota(jnp.int32, total_sums.shape, 0)
-    mixed = total_sums + jnp.where(rows == 0, moment, 0.0)
-    sums_out[...] = jnp.broadcast_to(mixed[None], sums_out.shape)
-
-
-def fold_kernel(slab, out):
-    row = slab[0, 0:1, :]
-    for d in range(1, slab.shape[0]):
-        row = row + slab[d, 0:1, :]
+    moments_out[...] = advance(
+        1, weights[...], around, features, diagonal, before, moments[...], new, sums, block
+    )
+
+
+def slab_hot_kernel(shape, index, far, near, ahead, block, out, ids):
+    nrows, width, slots, across = shape
+    for j in range(across):
+        source, part = ((far, j), (near, j - 3), (ahead, j - 6))[j // 3]
+        ids[j] = source[part * nrows : (part + 1) * nrows, :]
+    span = 3 * nrows
+    for a in range(across):
+        table = ids[(a - index[1] + across // 2) & (across - 1)].astype(jnp.int32)
+        owner = lax.shift_right_arithmetic(table, nrows.bit_length() - 1)
+        offset_x = lax.shift_right_arithmetic(owner, across.bit_length() - 1) - index[0] + 1
+        place = (owner & (across - 1)) * span + offset_x * nrows + (table & (nrows - 1))
+        place = jnp.where((table >= 0) & (offset_x >= 0) & (offset_x < 3), place, -1)
+        first = max(a - 1, 0) * span // LANES * LANES
+        last = -(-min(a + 2, across) * span // LANES) * LANES
+        rows = pl.ds(a * nrows, nrows)
+        if first:
+            out[rows, :first] = jnp.zeros((nrows, first), BF16)
+        out[rows, first:last] = one_hot(place, first, last - first, width, slots)
+        if last < out.shape[1]:
+            out[rows, last:] = jnp.zeros((nrows, out.shape[1] - last), BF16)
+
+
+def pack_kernel(up, block, down, first_sums, second_sums, moments, hot, out):
+    nrows = block.shape[0]
+    low = lane_iota(nrows) < LANES // 2
+    top = lax.broadcasted_iota(jnp.int32, (nrows, LANES), 0) == 0
+    parts = [
+        jnp.where(low, up[...], pltpu.roll(first_sums[...], LANES // 2, 1)),
+        jnp.where(low, block[...], pltpu.roll(second_sums[...], LANES // 2, 1)),
+        jnp.where(low, down[...], jnp.where(top, moments[...], 0.0)),
+    ]
+    out[...] = jnp.broadcast_to(jnp.concatenate(parts, axis=0)[None], out.shape)
+
+
+def slab_kernel(hot, slab, sums, out):
+    across, span, _ = slab.shape
+    result = products(hot[...], jnp.concatenate([slab[d] for d in range(across)], axis=0))
+    sums[...] = result
+    start = span // 3 * 2
+    row = slab[0, start : start + 1, :]
+    for d in range(1, across):
+        row = row + slab[d, start : start + 1, :]
+    square = total(jnp.where(lane_iota(result.shape[0]) < LANES // 2, result * result, 0.0))
+    row = jnp.where(lane_iota(1) == MOMENT_LANE + MOMENTS - 1, row + square, row)
     out[...] = jnp.broadcast_to(row, out.shape)
 
 
-def vertex_kernel(nrows, index, slab, bricks, vertex_features, out):
-    across, width, _ = slab.shape
+def fourth_kernel(index, slab, weights, features, diagonal, before, new):
+    across = slab.shape[0]
+    around = [padded(slab[(index[1] + d) & (across - 1)]) for d in (across - 1, 0, 1)]
+    result = products(weights[...], jnp.concatenate(around, axis=0))
+    new[...] = expand(result, features.shape[0], features, diagonal[...] - SHIFT, before[...])
+
+
+def vertex_kernel(nrows, index, slab, sums, bricks, vertex_features, out):
+    across, _, _ = slab.shape
+    width = vertex_features.shape[0]
     local = bricks[...] - index[0] * across * nrows
     hot = lax.broadcasted_iota(jnp.int32, (across * nrows, local.shape[1]), 0) == local
     hot = jnp.where(hot, 1.0, 0.0).astype(BF16)
-    group = LANES // nrows
-    lanes = lane_iota(width)
-    table = []
-    for k in range(ITERS):
-        tiles = []
-        for start in range(0, across, group):
-            tile = jnp.zeros((width, LANES), F32)
-            for d in range(group):
-                shift = (d - k) * nrows % LANES
-                moved = pltpu.roll(slab[start + d], shift, 1) if shift else slab[start + d]
-                tile = jnp.where((lanes >= d * nrows) & (lanes < (d + 1) * nrows), moved, tile)
-            tiles.append(tile)
-        table.append(jnp.concatenate(tiles, axis=1))
-    rest = jnp.concatenate(table, axis=0)
+    table = [
+        jnp.concatenate([slab[d, k * nrows : (k + 1) * nrows, :] for d in range(across)], axis=0).T[width:]
+        for k in range(2)
+    ]
+    rest = jnp.concatenate(table + [sums[...].T[:width]], axis=0)
     picked = None
     for _ in range(3):
         part = rest.astype(BF16)
@@ -326,7 +346,7 @@
     smem, hbm = pl.BlockSpec(memory_space=pltpu.SMEM), pl.BlockSpec(memory_space=pltpu.HBM)
     shape = (nrows, width, slots, across)
     power = f32(nrows, voxels)
-    block_shape, row, table = f32(nrows, LANES), f32(1, LANES), f32(width, LANES)
+    block_shape, row = f32(nrows, LANES), f32(1, LANES)
 
     block, moments = call(
         first_kernel, [block_shape, row], features, right_side, neighbours,
@@ -348,27 +368,41 @@
         functools.partial(middle_kernel, shape), f32(nrows, 3 * LANES),
         index, column, own, specs=[smem, VMEM, VMEM],
     )
-    v1, block, sums, moments, weights = call(
+    tables_shape = f32(3 * nrows, LANES)
+    v1, block, first_sums, moments, weights, tables = call(
         functools.partial(second_kernel, shape),
-        [power, block_shape, table, row, jax.ShapeDtypeStruct((LANES, 3 * LANES), BF16)],
+        [power, block_shape, block_shape, row, jax.ShapeDtypeStruct((LANES, 3 * LANES), BF16), tables_shape],
         index, left, column, right, own, known, features, diagonal, right_side, moments,
         specs=[smem] + [VMEM] * 9,
     )
     left, column, right = neighbourhood(block)
-    v2, block, sums, moments = call(
-        third_kernel, [power, block_shape, table, row],
-        left, column, right, weights, features, diagonal, v1, sums, moments,
-    )
-    left, column, right = neighbourhood(block)
-    v3, sums = call(
-        fourth_kernel, [power, f32(across, width, LANES)],
-        left, column, right, weights, features, diagonal, v2, sums, moments,
-    )
-    slab = lax.all_to_all(sums, "gy", 0, 0, tiled=True)
-    moments = lax.all_to_all(call(fold_kernel, f32(along, LANES), slab), "gx", 0, 0, tiled=True)
+    far = lax.ppermute(tables, "gy", ring("gy", 3))
+    ahead = lax.ppermute(tables, "gy", ring("gy", -3))
+    v2, block, second_sums, moments = call(
+        third_kernel, [power, block_shape, block_shape, row],
+        left, column, right, weights, features, diagonal, v1, moments, far, ahead,
+    )
+    up, down = lax.ppermute(block, "gx", ring("gx", 1)), lax.ppermute(block, "gx", ring("gx", -1))
+    hot = call(
+        functools.partial(slab_hot_kernel, shape),
+        jax.ShapeDtypeStruct((across * nrows, across * 3 * nrows), BF16),
+        index, far, tables, ahead, block, specs=[smem] + [VMEM] * 4,
+        scratch=[pltpu.VMEM((across, nrows, LANES), F32)],
+    )
+    packed = call(
+        pack_kernel, f32(across, 3 * nrows, LANES),
+        up, block, down, first_sums, second_sums, moments, hot,
+    )
+    slab = lax.all_to_all(packed, "gy", 0, 0, tiled=True)
+    sums, moments = call(slab_kernel, [f32(across * nrows, LANES), f32(along, LANES)], hot, slab)
+    moments = lax.all_to_all(moments, "gx", 0, 0, tiled=True)
+    v3 = call(
+        fourth_kernel, power, index, slab, weights, features, diagonal, v2,
+        specs=[smem] + [VMEM] * 5,
+    )
     vertices = call(
         functools.partial(vertex_kernel, nrows), f32(8, vertex_bricks.shape[0]),
-        index, slab, vertex_bricks.reshape(1, -1), vertex_features, specs=[smem] + [VMEM] * 3,
+        index, slab, sums, vertex_bricks.reshape(1, -1), vertex_features, specs=[smem] + [VMEM] * 4,
     )
     field, residual, values = call(
         last_kernel, [power, power, f32(1, vertex_bricks.shape[0])],

time: 81.9 us -> 80.6 us (0.984)
  starting transfers between devices: 37.1 us -> 29.2 us
  Pallas kernels: 13.3 us -> 16.4 us
  blocking collectives: 12.4 us -> 15.4 us
  local copies, waits for them, and re-layouts: 2.95 us -> 5.13 us
  waiting for transfers between devices: 14.9 us -> 13.3 us
    ppermute x3 -> x2, starting transfers between devices: 10.5 us -> 3.28 us  [neighbourhood(): lax.ppermute(column, 'gy', ring('gy', -1))]
    ppermute x0 -> x4, starting transfers between devices: none -> 6.85 us  [the longest x1 3.75 us: per_device(): ahead = lax.ppermute(tables, 'gy', ring('gy', -3))]
    ppermute x0 -> x4, waiting for transfers between devices: none -> 6.57 us  [the longest x1 3.8 us: per_device(): lax.ppermute(block, 'gx', ring('gx', 1))]
    ppermute x3 -> x2, starting transfers between devices: 18.6 us -> 13.4 us  [neighbourhood(): lax.ppermute(block, 'gx', ring('gx', -1))]
    all_to_all x1, waiting for transfers between devices: 7.3 us -> 3.69 us  [per_device(): moments = lax.all_to_all(moments, 'gx', 0, 0, tiled=True)]
    pallas_call x9 -> x11, Pallas kernels: 13.3 us -> 16.4 us  [call(): pl.pallas_call(kernel, out_shape=out_shape, in_specs=specs or [VMEM] * le...]
    all_to_all x1, blocking collectives: 12.4 us -> 15.4 us  [per_device(): slab = lax.all_to_all(packed, 'gy', 0, 0, tiled=True)]
    all_to_all x1, starting transfers between devices: 6.71 us -> 3.83 us  [per_device(): moments = lax.all_to_all(moments, 'gx', 0, 0, tiled=True)]
  transfers between devices with their start and end apart: 13 -> 13, of which waited for: 9 -> 5; matrix products, arithmetic and copies ran while one was open for 0% -> 0% of each run, Pallas kernels for 4% -> 8%
where the time goes in v6:
time: 80.6 us; the launch traced here: 80.3 us
  starting transfers between devices  29.2 us (36%)
  Pallas kernels  16.4 us (20%)
  blocking collectives  15.4 us (19%)
  waiting for transfers between devices  13.3 us (17%)
  local copies, waits for them, and re-layouts  5.13 us (6%)
  between operations  0.81 us (1%)
    pallas_call x11, Pallas kernels, call(): pl.pallas_call(kernel, out_shape=out_shape, in_specs=specs or [VMEM] * le...  16.4 us
    all_to_all x1, blocking collectives, per_device(): slab = lax.all_to_all(packed, 'gy', 0, 0, tiled=True)  15.4 us
    ppermute x2, starting transfers between devices, neighbourhood(): lax.ppermute(block, 'gx', ring('gx', -1))  13.4 us
    unnamed x22, local copies, waits for them, and re-layouts  5.12 us
    all_to_all x1, starting transfers between devices, per_device(): moments = lax.all_to_all(moments, 'gx', 0, 0, tiled=True)  3.83 us
    ppermute x1, waiting for transfers between devices, per_device(): lax.ppermute(block, 'gx', ring('gx', 1))  3.8 us
    ppermute x1, starting transfers between devices, per_device(): ahead = lax.ppermute(tables, 'gy', ring('gy', -3))  3.75 us
    all_to_all x1, waiting for transfers between devices, per_device(): moments = lax.all_to_all(moments, 'gx', 0, 0, tiled=True)  3.69 us
  transfers between devices with their start and end apart: 13, of which 5 were waited for; matrix products, arithmetic and copies ran while one was open for 0% of the time, Pallas kernels for 8%

profile of v6, /device:TPU:1, one launch (start us, length us, event | category | flops | bytes accessed | tf_op | source)
XLA Modules:
  0.0 80.3 jit_solution(11272176997515568728)
XLA Ops:
  0.7 3.4 %shard_map.85 = (f32[32,128]{1,0:T(8,128)}, f32[1,128]{1,0:T(1,128)}) custom-call(f32[32,64,512]{2,1,0:T(8,128)} %features.9, f32[32,512]{1,0:T(8,128)} %v0.1, s32[32,27]{1,0:T(8,128)} %neighbours.1), custom_call_target="tpu_custom_call" | custom-call | tf_op jit(solution)/shard_map/pallas_call | solution.py:23
  4.1 8.7 %collective-permute-start.1 = (f32[32,128]{1,0:T(8,128)}, f32[32,128]{1,0:T(8,128)S(1)}, u32[]{:S(2)}, u32[]{:S(2)}) collective-permute-start(f32[32,128]{1,0:T(8,128)} %get-tuple-element.22.block), channel_id=1, source_target_pairs={{0,248},{8,0},{16,8},{24,16},{32,24},{40,32},{48,40},{56,48},{64,5... | collective-permute-start | bytes 49160 | tf_op jit(solution)/shard_map/ppermute | solution.py:332
  12.8 0.1 pad_add_fusion.index
  12.9 2.2 %copy-done = f32[32,64,512]{2,1,0:T(8,128)S(1)} copy-done((f32[32,64,512]{2,1,0:T(8,128)S(1)}, f32[32,64,512]{2,1,0:T(8,128)}, u32[]{:S(2)}) %copy-start) | copy-done | bytes 4194328
  15.0 0.7 copy-done.6
  15.8 0.8 shard_map.86
  16.5 2.4 %collective-permute-done = f32[32,128]{1,0:T(8,128)S(1)} collective-permute-done((f32[32,128]{1,0:T(8,128)}, f32[32,128]{1,0:T(8,128)S(1)}, u32[]{:S(2)}, u32[]{:S(2)}) %collective-permute-start) | collective-permute-done | bytes 16416 | tf_op jit(solution)/shard_map/ppermute | solution.py:332
  18.9 2.1 %collective-permute-start.3 = (f32[96,128]{1,0:T(8,128)S(1)}, f32[96,128]{1,0:T(8,128)S(1)}, u32[]{:S(2)}, u32[]{:S(2)}) collective-permute-start(f32[96,128]{1,0:T(8,128)S(1)} %constant_dynamic-update-slice_fusion.column), channel_id=1, source_target_pairs={{0,7},{1,0},{2,1},{3,2},{4,3},{5,4},{6,5},{7,6},{8,15},{9,8},{10,9... | collective-permute-start | bytes 147464 | tf_op jit(solution)/shard_map/ppermute | solution.py:337
  21.0 1.2 %collective-permute-start.2 = (f32[96,128]{1,0:T(8,128)S(1)}, f32[96,128]{1,0:T(8,128)S(1)}, u32[]{:S(2)}, u32[]{:S(2)}) collective-permute-start(f32[96,128]{1,0:T(8,128)S(1)} %constant_dynamic-update-slice_fusion.column), channel_id=1, source_target_pairs={{0,1},{1,2},{2,3},{3,4},{4,5},{5,6},{6,7},{7,0},{8,9},{9,10},{10,1... | collective-permute-start | bytes 147464 | tf_op jit(solution)/shard_map/ppermute | solution.py:335
  22.2 1.1 %shard_map.87.known = f32[32,384]{1,0:T(8,128)S(1)} custom-call(s32[2]{0:T(128)S(1)} %pad_add_fusion.index, f32[96,128]{1,0:T(8,128)S(1)} %constant_dynamic-update-slice_fusion.column, bf16[32,384]{1,0:T(8,128)(2,1)S(1)} %get-tuple-element.24.own), custom_call_target="tpu_custom_call" | custom-call | tf_op jit(solution)/shard_map/pallas_call | solution.py:23
  23.3 0.7 collective-permute-done.3.right
  24.0 2.8 %shard_map.88 = (f32[32,512]{1,0:T(8,128)S(1)}, f32[32,128]{1,0:T(8,128)S(1)}, f32[32,128]{1,0:T(8,128)S(1)}, f32[1,128]{1,0:T(1,128)S(1)}, bf16[128,384]{1,0:T(8,128)(2,1)S(1)}, /*index=5*/f32[96,128]{1,0:T(8,128)S(1)}) custom-call(s32[2]{0:T(128)S(1)} %pad_add_fusion.index, f32[96,128]{1,0:T(8,128)S(1)} %collective-permute-done.2.left, ...), custom_call_target="tpu_custom_call" | custom-call | tf_op jit(solution)/shard_map/pallas_call | solution.py:23
  26.8 0.0 collective-permute-start.6
  26.8 4.8 %collective-permute-start.7 = (f32[32,128]{1,0:T(8,128)S(1)}, f32[32,128]{1,0:T(8,128)S(1)}, u32[]{:S(2)}, u32[]{:S(2)}) collective-permute-start(f32[32,128]{1,0:T(8,128)S(1)} %get-tuple-element.27), channel_id=1, source_target_pairs={{0,248},{8,0},{16,8},{24,16},{32,24},{40,32},{48,40},{56,48},{64,5... | collective-permute-start | bytes 49160 | tf_op jit(solution)/shard_map/ppermute | solution.py:332
  31.6 3.8 %collective-permute-start.5 = (f32[96,128]{1,0:T(8,128)S(1)}, f32[96,128]{1,0:T(8,128)S(1)}, u32[]{:S(2)}, u32[]{:S(2)}) collective-permute-start(f32[96,128]{1,0:T(8,128)S(1)} %get-tuple-element.26.near), channel_id=1, source_target_pairs={{0,5},{1,6},{2,7},{3,0},{4,1},{5,2},{6,3},{7,4},{8,13},{9,14},{10,... | collective-permute-start | bytes 147464 | tf_op jit(solution)/shard_map/ppermute | solution.py:380
  35.4 0.2 collective-permute-start.4
  35.6 1.2 %collective-permute-start.9 = (f32[96,128]{1,0:T(8,128)S(1)}, f32[96,128]{1,0:T(8,128)S(1)}, u32[]{:S(2)}, u32[]{:S(2)}) collective-permute-start(f32[96,128]{1,0:T(8,128)S(1)} %constant_dynamic-update-slice_fusion.3.column), channel_id=1, source_target_pairs={{0,7},{1,0},{2,1},{3,2},{4,3},{5,4},{6,5},{7,6},{8,15},{9,8},{10,9... | collective-permute-start | bytes 147464 | tf_op jit(solution)/shard_map/ppermute | solution.py:337
  36.8 0.6 collective-permute-start.8
  37.3 2.8 %collective-permute-done.4.far = f32[96,128]{1,0:T(8,128)S(1)} collective-permute-done((f32[96,128]{1,0:T(8,128)S(1)}, f32[96,128]{1,0:T(8,128)S(1)}, u32[]{:S(2)}, u32[]{:S(2)}) %collective-permute-start.4) | collective-permute-done | bytes 49184 | tf_op jit(solution)/shard_map/ppermute | solution.py:379
  40.1 1.4 %shard_map.89 = (f32[32,512]{1,0:T(8,128)S(1)}, f32[32,128]{1,0:T(8,128)S(1)}, f32[32,128]{1,0:T(8,128)S(1)}, f32[1,128]{1,0:T(1,128)S(1)}) custom-call(f32[96,128]{1,0:T(8,128)S(1)} %collective-permute-done.8.left, f32[96,128]{1,0:T(8,128)S(1)} %constant_dynamic-update-slice_fusion.3.column, f32[96,128]{1,0:T(8,128)S(1)} %collective-permute-done.9.right, ...), custom_call_target="tpu_custom_call" | custom-call | tf_op jit(solution)/shard_map/pallas_call | solution.py:23
  41.6 2.9 %collective-permute-start.11 = (f32[32,128]{1,0:T(8,128)S(1)}, f32[32,128]{1,0:T(8,128)S(1)}, u32[]{:S(2)}, u32[]{:S(2)}) collective-permute-start(f32[32,128]{1,0:T(8,128)S(1)} %get-tuple-element.31.block), channel_id=1, source_target_pairs={{0,248},{8,0},{16,8},{24,16},{32,24},{40,32},{48,40},{56,48},{64,5... | collective-permute-start | bytes 49160 | tf_op jit(solution)/shard_map/ppermute | solution.py:385
  44.5 2.1 %shard_map.90.hot = bf16[256,768]{1,0:T(8,128)(2,1)S(1)} custom-call(s32[2]{0:T(128)S(1)} %pad_add_fusion.index, f32[96,128]{1,0:T(8,128)S(1)} %collective-permute-done.4.far, f32[96,128]{1,0:T(8,128)S(1)} %get-tuple-element.26.near, f32[96,128]{1,0:T(8,128)S(1)} %collective-permute-done.5.ahead, f32[32,128]{1,0:T(8,128)S(1)} %get-tuple-element.31.block), custom_call_target="tpu_custom_call" | custom-call | tf_op jit(solution)/shard_map/pallas_call | solution.py:23
  46.6 3.8 %collective-permute-done.10.up = f32[32,128]{1,0:T(8,128)S(1)} collective-permute-done((f32[32,128]{1,0:T(8,128)S(1)}, f32[32,128]{1,0:T(8,128)S(1)}, u32[]{:S(2)}, u32[]{:S(2)}) %collective-permute-start.10) | collective-permute-done | bytes 16416 | tf_op jit(solution)/shard_map/ppermute | solution.py:385
  50.4 0.1 shard_map.91
  50.5 15.4 %all_to_all.16.slab = f32[8,96,128]{2,1,0:T(8,128)S(1)} all-to-all(f32[8,96,128]{2,1,0:T(8,128)S(1)} %shard_map.91), channel_id=1, replica_groups=mesh['gx'=32,'gy'=8] {'gy'}, dimensions={0} | all-to-all | bytes 786432 | tf_op jit(solution)/shard_map/all_to_all | solution.py:396
  65.9 1.2 %shard_map.92 = (f32[256,128]{1,0:T(8,128)S(1)}, f32[32,128]{1,0:T(8,128)}) custom-call(bf16[256,768]{1,0:T(8,128)(2,1)S(1)} %shard_map.90.hot, f32[8,96,128]{2,1,0:T(8,128)S(1)} %all_to_all.16.slab), custom_call_target="tpu_custom_call" | custom-call | tf_op jit(solution)/shard_map/pallas_call | solution.py:23
  67.0 3.8 %all-to-all-start.1 = ((f32[32,1,128]{2,1,0:T(1,128)}), f32[32,1,128]{2,1,0:T(1,128)S(1)}, u32[]{:S(2)}, u32[]{:S(2)}) async-start(f32[32,1,128]{2,1,0:T(1,128)} %bitcast.3), calls=%async_computation.1 | async-start | bytes 32768 | tf_op jit(solution)/shard_map/all_to_all | solution.py:398
  70.9 2.2 %copy-done.2 = f32[32,64,512]{2,1,0:T(8,128)S(1)} copy-done((f32[32,64,512]{2,1,0:T(8,128)S(1)}, f32[32,64,512]{2,1,0:T(8,128)}, u32[]{:S(2)}) %copy-start.2) | copy-done | bytes 4194328
  73.1 1.5 %shard_map.93.v3 = f32[32,512]{1,0:T(8,128)S(1)} custom-call(s32[2]{0:T(128)S(1)} %pad_add_fusion.index, f32[8,96,128]{2,1,0:T(8,128)S(1)} %all_to_all.16.slab, bf16[128,384]{1,0:T(8,128)(2,1)S(1)} %get-tuple-element.28.weights, f32[32,64,512]{2,1,0:T(8,128)S(1)} %copy-done.2, f32[32,512]{1,0:T(8,128)S(1)} %copy-done.3, ...), custom_call_target="tpu_custom_call" | custom-call | tf_op jit(solution)/shard_map/pallas_call | solution.py:23
  74.6 1.1 %shard_map.94.vertices = f32[8,1024]{1,0:T(8,128)S(1)} custom-call(s32[2]{0:T(128)S(1)} %pad_add_fusion.index, f32[8,96,128]{2,1,0:T(8,128)S(1)} %all_to_all.16.slab, f32[256,128]{1,0:T(8,128)S(1)} %get-tuple-element.37.sums, s32[1,1024]{1,0:T(1,128)S(1)} %bitcast.9, f32[64,1024]{1,0:T(8,128)S(1)} %copy-done.5), custom_call_target="tpu_custom_call" | custom-call | tf_op jit(solution)/shard_map/pallas_call | solution.py:23
  75.7 3.7 %all-to-all-done.1 = f32[32,1,128]{2,1,0:T(1,128)S(1)} async-done(((f32[32,1,128]{2,1,0:T(1,128)}), f32[32,1,128]{2,1,0:T(1,128)S(1)}, u32[]{:S(2)}, u32[]{:S(2)}) %all-to-all-start.1) | async-done | bytes 16416 | tf_op jit(solution)/shard_map/all_to_all | solution.py:398
  79.4 0.9 %shard_map.95 = (f32[32,512]{1,0:T(8,128)}, f32[32,512]{1,0:T(8,128)}, f32[1,1024]{1,0:T(1,128)}) custom-call(f32[32,128]{1,0:T(8,128)S(1)} %bitcast.8, f32[32,512]{1,0:T(8,128)S(1)} %copy-done.4, f32[32,512]{1,0:T(8,128)S(1)} %get-tuple-element.29.before.v1, f32[32,512]{1,0:T(8,128)S(1)} %get-tuple-element.36.before.v2, f32[32,512]{1,0:T(8,128)S(1)} %shard_map.93.v3, ...), custom_call_target="tpu_custom_call" | custom-call | tf_op jit(solution)/shard_map/pallas_call | solution.py:23
  (31 shorter events, 0.1 us)
Async XLA Ops:
  0.6 23.4 %copy-start.4 = (f32[32,512]{1,0:T(8,128)S(1)}, f32[32,512]{1,0:T(8,128)}, u32[]{:S(2)}) copy-start(f32[32,512]{1,0:T(8,128)} %v0.1) | copy-start | bytes 196612
  0.6 23.4 %copy-start.3 = (f32[32,512]{1,0:T(8,128)S(1)}, f32[32,512]{1,0:T(8,128)}, u32[]{:S(2)}) copy-start(f32[32,512]{1,0:T(8,128)} %diagonal.5) | copy-start | bytes 196612
  4.1 19.9 %copy-start.8 = (f32[1,128]{1,0:T(1,128)S(1)}, f32[1,128]{1,0:T(1,128)}, u32[]{:S(2)}) copy-start(f32[1,128]{1,0:T(1,128)} %get-tuple-element.25.moments) | copy-start | bytes 1540
  4.1 14.8 %collective-permute-start.1 = (f32[32,128]{1,0:T(8,128)}, f32[32,128]{1,0:T(8,128)S(1)}, u32[]{:S(2)}, u32[]{:S(2)}) collective-permute-start(f32[32,128]{1,0:T(8,128)} %get-tuple-element.22.block), channel_id=1, source_target_pairs={{0,248},{8,0},{16,8},{24,16},{32,24},{40,32},{48,40},{56,48},{64,5... | collective-permute-start | bytes 49160 | tf_op jit(solution)/shard_map/ppermute | solution.py:332
  12.8 6.1 %collective-permute-start = (f32[32,128]{1,0:T(8,128)}, f32[32,128]{1,0:T(8,128)S(1)}, u32[]{:S(2)}, u32[]{:S(2)}) collective-permute-start(f32[32,128]{1,0:T(8,128)} %get-tuple-element.22.block), channel_id=1, source_target_pairs={{0,8},{8,16},{16,24},{24,32},{32,40},{40,48},{48,56},{56,64},{64,7... | collective-permute-start | bytes 49160 | tf_op jit(solution)/shard_map/ppermute | solution.py:332
  12.9 2.2 %copy-start = (f32[32,64,512]{2,1,0:T(8,128)S(1)}, f32[32,64,512]{2,1,0:T(8,128)}, u32[]{:S(2)}) copy-start(f32[32,64,512]{2,1,0:T(8,128)} %features.9) | copy-start | bytes 12582916
  15.0 0.7 copy-start.6
  15.8 8.3 %copy-start.1 = (f32[32,64,512]{2,1,0:T(8,128)S(1)}, f32[32,64,512]{2,1,0:T(8,128)}, u32[]{:S(2)}) copy-start(f32[32,64,512]{2,1,0:T(8,128)} %features.9) | copy-start | bytes 12582916
  18.9 5.1 %collective-permute-start.3 = (f32[96,128]{1,0:T(8,128)S(1)}, f32[96,128]{1,0:T(8,128)S(1)}, u32[]{:S(2)}, u32[]{:S(2)}) collective-permute-start(f32[96,128]{1,0:T(8,128)S(1)} %constant_dynamic-update-slice_fusion.column), channel_id=1, source_target_pairs={{0,7},{1,0},{2,1},{3,2},{4,3},{5,4},{6,5},{7,6},{8,15},{9,8},{10,9... | collective-permute-start | bytes 147464 | tf_op jit(solution)/shard_map/ppermute | solution.py:337
  21.0 3.0 %collective-permute-start.2 = (f32[96,128]{1,0:T(8,128)S(1)}, f32[96,128]{1,0:T(8,128)S(1)}, u32[]{:S(2)}, u32[]{:S(2)}) collective-permute-start(f32[96,128]{1,0:T(8,128)S(1)} %constant_dynamic-update-slice_fusion.column), channel_id=1, source_target_pairs={{0,1},{1,2},{2,3},{3,4},{4,5},{5,6},{6,7},{7,0},{8,9},{9,10},{10,1... | collective-permute-start | bytes 147464 | tf_op jit(solution)/shard_map/ppermute | solution.py:335
  26.8 8.8 %collective-permute-start.6 = (f32[32,128]{1,0:T(8,128)S(1)}, f32[32,128]{1,0:T(8,128)S(1)}, u32[]{:S(2)}, u32[]{:S(2)}) collective-permute-start(f32[32,128]{1,0:T(8,128)S(1)} %get-tuple-element.27), channel_id=1, source_target_pairs={{0,8},{8,16},{16,24},{24,32},{32,40},{40,48},{48,56},{56,64},{64,7... | collective-permute-start | bytes 49160 | tf_op jit(solution)/shard_map/ppermute | solution.py:332
  26.8 8.7 %collective-permute-start.7 = (f32[32,128]{1,0:T(8,128)S(1)}, f32[32,128]{1,0:T(8,128)S(1)}, u32[]{:S(2)}, u32[]{:S(2)}) collective-permute-start(f32[32,128]{1,0:T(8,128)S(1)} %get-tuple-element.27), channel_id=1, source_target_pairs={{0,248},{8,0},{16,8},{24,16},{32,24},{40,32},{48,40},{56,48},{64,5... | collective-permute-start | bytes 49160 | tf_op jit(solution)/shard_map/ppermute | solution.py:332
  31.6 5.7 %collective-permute-start.5 = (f32[96,128]{1,0:T(8,128)S(1)}, f32[96,128]{1,0:T(8,128)S(1)}, u32[]{:S(2)}, u32[]{:S(2)}) collective-permute-start(f32[96,128]{1,0:T(8,128)S(1)} %get-tuple-element.26.near), channel_id=1, source_target_pairs={{0,5},{1,6},{2,7},{3,0},{4,1},{5,2},{6,3},{7,4},{8,13},{9,14},{10,... | collective-permute-start | bytes 147464 | tf_op jit(solution)/shard_map/ppermute | solution.py:380
  35.4 4.7 %collective-permute-start.4 = (f32[96,128]{1,0:T(8,128)S(1)}, f32[96,128]{1,0:T(8,128)S(1)}, u32[]{:S(2)}, u32[]{:S(2)}) collective-permute-start(f32[96,128]{1,0:T(8,128)S(1)} %get-tuple-element.26.near), channel_id=1, source_target_pairs={{0,3},{1,4},{2,5},{3,6},{4,7},{5,0},{6,1},{7,2},{8,11},{9,12},{10,... | collective-permute-start | bytes 147464 | tf_op jit(solution)/shard_map/ppermute | solution.py:379
  35.6 4.5 %collective-permute-start.9 = (f32[96,128]{1,0:T(8,128)S(1)}, f32[96,128]{1,0:T(8,128)S(1)}, u32[]{:S(2)}, u32[]{:S(2)}) collective-permute-start(f32[96,128]{1,0:T(8,128)S(1)} %constant_dynamic-update-slice_fusion.3.column), channel_id=1, source_target_pairs={{0,7},{1,0},{2,1},{3,2},{4,3},{5,4},{6,5},{7,6},{8,15},{9,8},{10,9... | collective-permute-start | bytes 147464 | tf_op jit(solution)/shard_map/ppermute | solution.py:337
  36.8 3.4 %collective-permute-start.8 = (f32[96,128]{1,0:T(8,128)S(1)}, f32[96,128]{1,0:T(8,128)S(1)}, u32[]{:S(2)}, u32[]{:S(2)}) collective-permute-start(f32[96,128]{1,0:T(8,128)S(1)} %constant_dynamic-update-slice_fusion.3.column), channel_id=1, source_target_pairs={{0,1},{1,2},{2,3},{3,4},{4,5},{5,6},{6,7},{7,0},{8,9},{9,10},{10,1... | collective-permute-start | bytes 147464 | tf_op jit(solution)/shard_map/ppermute | solution.py:335
  41.6 33.0 %copy-start.5 = (f32[64,1024]{1,0:T(8,128)S(1)}, f32[64,1024]{1,0:T(8,128)}, u32[]{:S(2)}) copy-start(f32[64,1024]{1,0:T(8,128)} %vertex_features.1) | copy-start | bytes 786436
  41.6 33.0 %copy-start.7 = (s32[1024]{0:T(1024)S(1)}, s32[1024]{0:T(1024)}, u32[]{:S(2)}) copy-start(s32[1024]{0:T(1024)} %param.11) | copy-start | bytes 12292
  41.6 5.0 %collective-permute-start.11 = (f32[32,128]{1,0:T(8,128)S(1)}, f32[32,128]{1,0:T(8,128)S(1)}, u32[]{:S(2)}, u32[]{:S(2)}) collective-permute-start(f32[32,128]{1,0:T(8,128)S(1)} %get-tuple-element.31.block), channel_id=1, source_target_pairs={{0,248},{8,0},{16,8},{24,16},{32,24},{40,32},{48,40},{56,48},{64,5... | collective-permute-start | bytes 49160 | tf_op jit(solution)/shard_map/ppermute | solution.py:385
  44.5 5.9 %collective-permute-start.10 = (f32[32,128]{1,0:T(8,128)S(1)}, f32[32,128]{1,0:T(8,128)S(1)}, u32[]{:S(2)}, u32[]{:S(2)}) collective-permute-start(f32[32,128]{1,0:T(8,128)S(1)} %get-tuple-element.31.block), channel_id=1, source_target_pairs={{0,8},{8,16},{16,24},{24,32},{32,40},{40,48},{48,56},{56,64},{64,7... | collective-permute-start | bytes 49160 | tf_op jit(solution)/shard_map/ppermute | solution.py:385
  67.0 12.4 %all-to-all-start.1 = ((f32[32,1,128]{2,1,0:T(1,128)}), f32[32,1,128]{2,1,0:T(1,128)S(1)}, u32[]{:S(2)}, u32[]{:S(2)}) async-start(f32[32,1,128]{2,1,0:T(1,128)} %bitcast.3), calls=%async_computation.1 | async-start | bytes 32768 | tf_op jit(solution)/shard_map/all_to_all | solution.py:398
  70.9 2.2 %copy-start.2 = (f32[32,64,512]{2,1,0:T(8,128)S(1)}, f32[32,64,512]{2,1,0:T(8,128)}, u32[]{:S(2)}) copy-start(f32[32,64,512]{2,1,0:T(8,128)} %features.9) | copy-start | bytes 12582916

commit v7 on v6

--- a/solution.py
+++ b/solution.py
@@ -198,28 +198,38 @@
     pad = jnp.zeros((LANES - 2 * nrows, 3 * LANES), BF16)
     weights = jnp.concatenate([mine, twice, pad], axis=0)
     weights_out[...] = weights
-    tables[...] = jnp.concatenate([side[nrows : 2 * nrows, :] for side in (left, column, right)], axis=0)
+    low, middle_ids, high = [side[nrows : 2 * nrows, :] for side in (left, column, right)]
+    lanes = lane_iota(nrows)
+    half, quarter = LANES // 2, LANES // 4
+    sides = jnp.where(lanes < half, 0.0, jnp.where(lanes < half + quarter, low, pltpu.roll(high, quarter, 1)))
+    tables[...] = jnp.where(lanes < half, pltpu.roll(middle_ids, half, 1), sides)
     around = jnp.concatenate([padded(side[...]) for side in (left, column, right)], axis=0)
     moments_out[...] = advance(
         0, weights, around, features, diagonal, before, moments[...], new, sums, block
     )
+    block[...] = block[...] + sides
 
 
 def third_kernel(
-    left, column, right, weights, features, diagonal, before, moments, far, ahead,
-    new, block, sums, moments_out,
+    left, column, right, weights, features, diagonal, before, moments, far,
+    new, block, sums, moments_out, tables,
 ):
+    nrows = before.shape[0]
+    low, high = left[nrows : 2 * nrows, :], right[nrows : 2 * nrows, :]
+    lanes = lane_iota(nrows)
+    tables[...] = jnp.where(lanes < LANES * 3 // 4, low, high)
     around = jnp.concatenate([padded(side[...]) for side in (left, column, right)], axis=0)
     moments_out[...] = advance(
         1, weights[...], around, features, diagonal, before, moments[...], new, sums, block
     )
 
 
-def slab_hot_kernel(shape, index, far, near, ahead, block, out, ids):
+def slab_hot_kernel(shape, index, near, two, far, block, out, ids):
     nrows, width, slots, across = shape
-    for j in range(across):
-        source, part = ((far, j), (near, j - 3), (ahead, j - 6))[j // 3]
-        ids[j] = source[part * nrows : (part + 1) * nrows, :]
+    before, after = LANES // 2, LANES * 3 // 4
+    places = ((far, 0), (far, after), (two, before), (near, before), (near, 0), (near, after), (two, after), (far, before))
+    for j, (source, lane) in enumerate(places):
+        ids[j] = pltpu.roll(source[...], (width - lane) % LANES, 1) if lane != width else source[...]
     span = 3 * nrows
     for a in range(across):
         table = ids[(a - index[1] + across // 2) & (across - 1)].astype(jnp.int32)
@@ -249,7 +259,7 @@
     out[...] = jnp.broadcast_to(jnp.concatenate(parts, axis=0)[None], out.shape)
 
 
-def slab_kernel(hot, slab, sums, out):
+def slab_kernel(index, hot, slab, weights, features, diagonal, before, sums, out, new):
     across, span, _ = slab.shape
     result = products(hot[...], jnp.concatenate([slab[d] for d in range(across)], axis=0))
     sums[...] = result
@@ -260,10 +270,6 @@
     square = total(jnp.where(lane_iota(result.shape[0]) < LANES // 2, result * result, 0.0))
     row = jnp.where(lane_iota(1) == MOMENT_LANE + MOMENTS - 1, row + square, row)
     out[...] = jnp.broadcast_to(row, out.shape)
-
-
-def fourth_kernel(index, slab, weights, features, diagonal, before, new):
-    across = slab.shape[0]
     around = [padded(slab[(index[1] + d) & (across - 1)]) for d in (across - 1, 0, 1)]
     result = products(weights[...], jnp.concatenate(around, axis=0))
     new[...] = expand(result, features.shape[0], features, diagonal[...] - SHIFT, before[...])
@@ -368,25 +374,23 @@
         functools.partial(middle_kernel, shape), f32(nrows, 3 * LANES),
         index, column, own, specs=[smem, VMEM, VMEM],
     )
-    tables_shape = f32(3 * nrows, LANES)
-    v1, block, first_sums, moments, weights, tables = call(
+    v1, block, first_sums, moments, weights, near = call(
         functools.partial(second_kernel, shape),
-        [power, block_shape, block_shape, row, jax.ShapeDtypeStruct((LANES, 3 * LANES), BF16), tables_shape],
+        [power, block_shape, block_shape, row, jax.ShapeDtypeStruct((LANES, 3 * LANES), BF16), block_shape],
         index, left, column, right, own, known, features, diagonal, right_side, moments,
         specs=[smem] + [VMEM] * 9,
     )
     left, column, right = neighbourhood(block)
-    far = lax.ppermute(tables, "gy", ring("gy", 3))
-    ahead = lax.ppermute(tables, "gy", ring("gy", -3))
-    v2, block, second_sums, moments = call(
-        third_kernel, [power, block_shape, block_shape, row],
-        left, column, right, weights, features, diagonal, v1, moments, far, ahead,
+    far = lax.ppermute(near, "gy", ring("gy", across // 2))
+    v2, block, second_sums, moments, two = call(
+        third_kernel, [power, block_shape, block_shape, row, block_shape],
+        left, column, right, weights, features, diagonal, v1, moments, far,
     )
     up, down = lax.ppermute(block, "gx", ring("gx", 1)), lax.ppermute(block, "gx", ring("gx", -1))
     hot = call(
         functools.partial(slab_hot_kernel, shape),
         jax.ShapeDtypeStruct((across * nrows, across * 3 * nrows), BF16),
-        index, far, tables, ahead, block, specs=[smem] + [VMEM] * 4,
+        index, near, two, far, block, specs=[smem] + [VMEM] * 4,
         scratch=[pltpu.VMEM((across, nrows, LANES), F32)],
     )
     packed = call(
@@ -394,12 +398,11 @@
         up, block, down, first_sums, second_sums, moments, hot,
     )
     slab = lax.all_to_all(packed, "gy", 0, 0, tiled=True)
-    sums, moments = call(slab_kernel, [f32(across * nrows, LANES), f32(along, LANES)], hot, slab)
+    sums, moments, v3 = call(
+        slab_kernel, [f32(across * nrows, LANES), f32(along, LANES), power],
+        index, hot, slab, weights, features, diagonal, v2, specs=[smem] + [VMEM] * 6,
+    )
     moments = lax.all_to_all(moments, "gx", 0, 0, tiled=True)
-    v3 = call(
-        fourth_kernel, power, index, slab, weights, features, diagonal, v2,
-        specs=[smem] + [VMEM] * 5,
-    )
     vertices = call(
         functools.partial(vertex_kernel, nrows), f32(8, vertex_bricks.shape[0]),
         index, slab, sums, vertex_bricks.reshape(1, -1), vertex_features, specs=[smem] + [VMEM] * 4,

time: 80.6 us -> 82.4 us (1.022)
  waiting for transfers between devices: 13.3 us -> 17.8 us
  local copies, waits for them, and re-layouts: 5.13 us -> 2.94 us
  starting transfers between devices: 29.2 us -> 31.3 us
  blocking collectives: 15.4 us -> 13.4 us
    all_to_all x1, waiting for transfers between devices: 3.69 us -> 7.37 us  [per_device(): moments = lax.all_to_all(moments, 'gx', 0, 0, tiled=True)]
    ppermute x2, starting transfers between devices: 3.28 us -> 6.06 us  [neighbourhood(): lax.ppermute(column, 'gy', ring('gy', -1))]
    ppermute x2 -> x1, starting transfers between devices: 3.94 us -> 1.62 us  [per_device(): far = lax.ppermute(near, 'gy', ring('gy', across // 2))]
    ppermute x1, starting transfers between devices: 2.91 us -> 5.1 us  [per_device(): lax.ppermute(block, 'gx', ring('gx', -1))]
    unnamed x22 -> x20, local copies, waits for them, and re-layouts: 5.12 us -> 2.94 us
    all_to_all x1, blocking collectives: 15.4 us -> 13.4 us  [per_device(): slab = lax.all_to_all(packed, 'gy', 0, 0, tiled=True)]
    ppermute x2, waiting for transfers between devices: 2.36 us -> 3.48 us  [neighbourhood(): lax.ppermute(block, 'gx', ring('gx', 1))]
    pallas_call x11 -> x10, Pallas kernels: 16.4 us -> 15.8 us  [call(): pl.pallas_call(kernel, out_shape=out_shape, in_specs=specs or [VMEM] * le...]
  transfers between devices with their start and end apart: 13 -> 12, of which waited for: 5 -> 6; matrix products, arithmetic and copies ran while one was open for 0% -> 0% of each run, Pallas kernels for 8% -> 6%
where the time goes in v7:
time: 82.4 us; the launch traced here: 82.2 us
  starting transfers between devices  31.3 us (38%)
  waiting for transfers between devices  17.8 us (22%)
  Pallas kernels  15.8 us (19%)
  blocking collectives  13.4 us (16%)
  local copies, waits for them, and re-layouts  2.94 us (4%)
    pallas_call x10, Pallas kernels, call(): pl.pallas_call(kernel, out_shape=out_shape, in_specs=specs or [VMEM] * le...  15.8 us
    ppermute x2, starting transfers between devices, neighbourhood(): lax.ppermute(block, 'gx', ring('gx', -1))  13.4 us
    all_to_all x1, blocking collectives, per_device(): slab = lax.all_to_all(packed, 'gy', 0, 0, tiled=True)  13.4 us
    all_to_all x1, waiting for transfers between devices, per_device(): moments = lax.all_to_all(moments, 'gx', 0, 0, tiled=True)  7.37 us
    ppermute x2, starting transfers between devices, neighbourhood(): lax.ppermute(column, 'gy', ring('gy', -1))  6.06 us
    ppermute x1, starting transfers between devices, per_device(): lax.ppermute(block, 'gx', ring('gx', -1))  5.1 us
    all_to_all x1, starting transfers between devices, per_device(): moments = lax.all_to_all(moments, 'gx', 0, 0, tiled=True)  3.84 us
    ppermute x1, waiting for transfers between devices, per_device(): lax.ppermute(block, 'gx', ring('gx', 1))  3.72 us
  transfers between devices with their start and end apart: 12, of which 6 were waited for; matrix products, arithmetic and copies ran while one was open for 0% of the time, Pallas kernels for 6%

profile of v7, /device:TPU:1, one launch (start us, length us, event | category | flops | bytes accessed | tf_op | source)
XLA Modules:
  0.0 82.2 jit_solution(7130815022634386899)
XLA Ops:
  0.7 3.4 %shard_map.85 = (f32[32,128]{1,0:T(8,128)}, f32[1,128]{1,0:T(1,128)}) custom-call(f32[32,64,512]{2,1,0:T(8,128)} %features.9, f32[32,512]{1,0:T(8,128)} %v0.1, s32[32,27]{1,0:T(8,128)} %neighbours.1), custom_call_target="tpu_custom_call" | custom-call | tf_op jit(solution)/shard_map/pallas_call | solution.py:23
  4.1 8.7 %collective-permute-start.1 = (f32[32,128]{1,0:T(8,128)}, f32[32,128]{1,0:T(8,128)S(1)}, u32[]{:S(2)}, u32[]{:S(2)}) collective-permute-start(f32[32,128]{1,0:T(8,128)} %get-tuple-element.24.block), channel_id=1, source_target_pairs={{0,248},{8,0},{16,8},{24,16},{32,24},{40,32},{48,40},{56,48},{64,5... | collective-permute-start | bytes 49160 | tf_op jit(solution)/shard_map/ppermute | solution.py:338
  12.8 0.1 pad_add_fusion.index
  12.9 2.2 %copy-done = f32[32,64,512]{2,1,0:T(8,128)S(1)} copy-done((f32[32,64,512]{2,1,0:T(8,128)S(1)}, f32[32,64,512]{2,1,0:T(8,128)}, u32[]{:S(2)}) %copy-start) | copy-done | bytes 4194328
  15.0 0.7 copy-done.5
  15.8 0.8 shard_map.86
  16.5 2.4 %collective-permute-done = f32[32,128]{1,0:T(8,128)S(1)} collective-permute-done((f32[32,128]{1,0:T(8,128)}, f32[32,128]{1,0:T(8,128)S(1)}, u32[]{:S(2)}, u32[]{:S(2)}) %collective-permute-start) | collective-permute-done | bytes 16416 | tf_op jit(solution)/shard_map/ppermute | solution.py:338
  18.9 0.0 collective-permute-done.1
  18.9 2.1 %collective-permute-start.3 = (f32[96,128]{1,0:T(8,128)S(1)}, f32[96,128]{1,0:T(8,128)S(1)}, u32[]{:S(2)}, u32[]{:S(2)}) collective-permute-start(f32[96,128]{1,0:T(8,128)S(1)} %constant_dynamic-update-slice_fusion.column), channel_id=1, source_target_pairs={{0,7},{1,0},{2,1},{3,2},{4,3},{5,4},{6,5},{7,6},{8,15},{9,8},{10,9... | collective-permute-start | bytes 147464 | tf_op jit(solution)/shard_map/ppermute | solution.py:343
  21.0 1.2 %collective-permute-start.2 = (f32[96,128]{1,0:T(8,128)S(1)}, f32[96,128]{1,0:T(8,128)S(1)}, u32[]{:S(2)}, u32[]{:S(2)}) collective-permute-start(f32[96,128]{1,0:T(8,128)S(1)} %constant_dynamic-update-slice_fusion.column), channel_id=1, source_target_pairs={{0,1},{1,2},{2,3},{3,4},{4,5},{5,6},{6,7},{7,0},{8,9},{9,10},{10,1... | collective-permute-start | bytes 147464 | tf_op jit(solution)/shard_map/ppermute | solution.py:341
  22.2 1.1 %shard_map.87.known = f32[32,384]{1,0:T(8,128)S(1)} custom-call(s32[2]{0:T(128)S(1)} %pad_add_fusion.index, f32[96,128]{1,0:T(8,128)S(1)} %constant_dynamic-update-slice_fusion.column, bf16[32,384]{1,0:T(8,128)(2,1)S(1)} %get-tuple-element.26.own), custom_call_target="tpu_custom_call" | custom-call | tf_op jit(solution)/shard_map/pallas_call | solution.py:23
  23.3 0.7 collective-permute-done.3.right
  24.0 0.0 collective-permute-done.2.left
  24.0 2.8 %shard_map.88 = (f32[32,512]{1,0:T(8,128)S(1)}, f32[32,128]{1,0:T(8,128)S(1)}, f32[32,128]{1,0:T(8,128)S(1)}, f32[1,128]{1,0:T(1,128)S(1)}, bf16[128,384]{1,0:T(8,128)(2,1)S(1)}, /*index=5*/f32[32,128]{1,0:T(8,128)S(1)}) custom-call(s32[2]{0:T(128)S(1)} %pad_add_fusion.index, f32[96,128]{1,0:T(8,128)S(1)} %collective-permute-done.2.left, ...), custom_call_target="tpu_custom_call" | custom-call | tf_op jit(solution)/shard_map/pallas_call | solution.py:23
  26.8 0.0 collective-permute-start.4
  26.8 4.8 %collective-permute-start.5 = (f32[32,128]{1,0:T(8,128)S(1)}, f32[32,128]{1,0:T(8,128)S(1)}, u32[]{:S(2)}, u32[]{:S(2)}) collective-permute-start(f32[32,128]{1,0:T(8,128)S(1)} %get-tuple-element.29), channel_id=1, source_target_pairs={{0,248},{8,0},{16,8},{24,16},{32,24},{40,32},{48,40},{56,48},{64,5... | collective-permute-start | bytes 49160 | tf_op jit(solution)/shard_map/ppermute | solution.py:338
  31.6 1.1 %collective-permute-done.4 = f32[32,128]{1,0:T(8,128)S(1)} collective-permute-done((f32[32,128]{1,0:T(8,128)S(1)}, f32[32,128]{1,0:T(8,128)S(1)}, u32[]{:S(2)}, u32[]{:S(2)}) %collective-permute-start.4) | collective-permute-done | bytes 16416 | tf_op jit(solution)/shard_map/ppermute | solution.py:338
  32.7 0.0 collective-permute-done.5
  32.8 3.9 %collective-permute-start.7 = (f32[96,128]{1,0:T(8,128)S(1)}, f32[96,128]{1,0:T(8,128)S(1)}, u32[]{:S(2)}, u32[]{:S(2)}) collective-permute-start(f32[96,128]{1,0:T(8,128)S(1)} %constant_dynamic-update-slice_fusion.3.column), channel_id=1, source_target_pairs={{0,7},{1,0},{2,1},{3,2},{4,3},{5,4},{6,5},{7,6},{8,15},{9,8},{10,9... | collective-permute-start | bytes 147464 | tf_op jit(solution)/shard_map/ppermute | solution.py:343
  36.7 1.6 %collective-permute-start.8 = (f32[32,128]{1,0:T(8,128)S(1)}, f32[32,128]{1,0:T(8,128)S(1)}, u32[]{:S(2)}, u32[]{:S(2)}) collective-permute-start(f32[32,128]{1,0:T(8,128)S(1)} %get-tuple-element.28.near), channel_id=1, source_target_pairs={{0,4},{1,5},{2,6},{3,7},{4,0},{5,1},{6,2},{7,3},{8,12},{9,13},{10,... | collective-permute-start | bytes 49160 | tf_op jit(solution)/shard_map/ppermute | solution.py:384
  38.3 2.6 %collective-permute-done.8.far = f32[32,128]{1,0:T(8,128)S(1)} collective-permute-done((f32[32,128]{1,0:T(8,128)S(1)}, f32[32,128]{1,0:T(8,128)S(1)}, u32[]{:S(2)}, u32[]{:S(2)}) %collective-permute-start.8) | collective-permute-done | bytes 16416 | tf_op jit(solution)/shard_map/ppermute | solution.py:384
  40.9 1.4 %shard_map.89 = (f32[32,512]{1,0:T(8,128)S(1)}, f32[32,128]{1,0:T(8,128)S(1)}, f32[32,128]{1,0:T(8,128)S(1)}, f32[1,128]{1,0:T(1,128)S(1)}, f32[32,128]{1,0:T(8,128)S(1)}) custom-call(f32[96,128]{1,0:T(8,128)S(1)} %collective-permute-done.6.left, f32[96,128]{1,0:T(8,128)S(1)} %constant_dynamic-update-slice_fusion.3.column, ...), custom_call_target="tpu_custom_call" | custom-call | tf_op jit(solution)/shard_map/pallas_call | solution.py:23
  42.4 5.1 %collective-permute-start.10 = (f32[32,128]{1,0:T(8,128)S(1)}, f32[32,128]{1,0:T(8,128)S(1)}, u32[]{:S(2)}, u32[]{:S(2)}) collective-permute-start(f32[32,128]{1,0:T(8,128)S(1)} %get-tuple-element.34.block), channel_id=1, source_target_pairs={{0,248},{8,0},{16,8},{24,16},{32,24},{40,32},{48,40},{56,48},{64,5... | collective-permute-start | bytes 49160 | tf_op jit(solution)/shard_map/ppermute | solution.py:389
  47.5 2.2 %shard_map.90.hot = bf16[256,768]{1,0:T(8,128)(2,1)S(1)} custom-call(s32[2]{0:T(128)S(1)} %pad_add_fusion.index, f32[32,128]{1,0:T(8,128)S(1)} %get-tuple-element.28.near, f32[32,128]{1,0:T(8,128)S(1)} %get-tuple-element.33.two, f32[32,128]{1,0:T(8,128)S(1)} %collective-permute-done.8.far, f32[32,128]{1,0:T(8,128)S(1)} %get-tuple-element.34.block), custom_call_target="tpu_custom_call" | custom-call | tf_op jit(solution)/shard_map/pallas_call | solution.py:23
  49.7 3.7 %collective-permute-done.9.up = f32[32,128]{1,0:T(8,128)S(1)} collective-permute-done((f32[32,128]{1,0:T(8,128)S(1)}, f32[32,128]{1,0:T(8,128)S(1)}, u32[]{:S(2)}, u32[]{:S(2)}) %collective-permute-start.9) | collective-permute-done | bytes 16416 | tf_op jit(solution)/shard_map/ppermute | solution.py:389
  53.4 0.1 shard_map.91
  53.5 13.4 %all_to_all.16.slab = f32[8,96,128]{2,1,0:T(8,128)S(1)} all-to-all(f32[8,96,128]{2,1,0:T(8,128)S(1)} %shard_map.91), channel_id=1, replica_groups=mesh['gx'=32,'gy'=8] {'gy'}, dimensions={0} | all-to-all | bytes 786432 | tf_op jit(solution)/shard_map/all_to_all | solution.py:400
  66.9 1.9 %shard_map.92 = (f32[256,128]{1,0:T(8,128)S(1)}, f32[32,128]{1,0:T(8,128)}, f32[32,512]{1,0:T(8,128)S(1)}) custom-call(s32[2]{0:T(128)S(1)} %pad_add_fusion.index, bf16[256,768]{1,0:T(8,128)(2,1)S(1)} %shard_map.90.hot, f32[8,96,128]{2,1,0:T(8,128)S(1)} %all_to_all.16.slab, bf16[128,384]{1,0:T(8,128)(2,1)S(1)} %get-tuple-element.30.weights, ...), custom_call_target="tpu_custom_call" | custom-call | tf_op jit(solution)/shard_map/pallas_call | solution.py:23
  68.9 3.8 %all-to-all-start.1 = ((f32[32,1,128]{2,1,0:T(1,128)}), f32[32,1,128]{2,1,0:T(1,128)S(1)}, u32[]{:S(2)}, u32[]{:S(2)}) async-start(f32[32,1,128]{2,1,0:T(1,128)} %bitcast.3), calls=%async_computation.1 | async-start | bytes 32768 | tf_op jit(solution)/shard_map/all_to_all | solution.py:405
  72.7 1.1 %shard_map.93.vertices = f32[8,1024]{1,0:T(8,128)S(1)} custom-call(s32[2]{0:T(128)S(1)} %pad_add_fusion.index, f32[8,96,128]{2,1,0:T(8,128)S(1)} %all_to_all.16.slab, f32[256,128]{1,0:T(8,128)S(1)} %get-tuple-element.41.sums, s32[1,1024]{1,0:T(1,128)S(1)} %bitcast.9, f32[64,1024]{1,0:T(8,128)S(1)} %copy-done.4), custom_call_target="tpu_custom_call" | custom-call | tf_op jit(solution)/shard_map/pallas_call | solution.py:23
  73.9 7.4 %all-to-all-done.1 = f32[32,1,128]{2,1,0:T(1,128)S(1)} async-done(((f32[32,1,128]{2,1,0:T(1,128)}), f32[32,1,128]{2,1,0:T(1,128)S(1)}, u32[]{:S(2)}, u32[]{:S(2)}) %all-to-all-start.1) | async-done | bytes 16416 | tf_op jit(solution)/shard_map/all_to_all | solution.py:405
  81.2 0.9 %shard_map.94 = (f32[32,512]{1,0:T(8,128)}, f32[32,512]{1,0:T(8,128)}, f32[1,1024]{1,0:T(1,128)}) custom-call(f32[32,128]{1,0:T(8,128)S(1)} %bitcast.8, f32[32,512]{1,0:T(8,128)S(1)} %copy-done.3, f32[32,512]{1,0:T(8,128)S(1)} %get-tuple-element.31.before.v1, f32[32,512]{1,0:T(8,128)S(1)} %get-tuple-element.38.before.v2, ...), custom_call_target="tpu_custom_call" | custom-call | tf_op jit(solution)/shard_map/pallas_call | solution.py:23
  (26 shorter events, 0.1 us)
Async XLA Ops:
  0.6 23.4 %copy-start.3 = (f32[32,512]{1,0:T(8,128)S(1)}, f32[32,512]{1,0:T(8,128)}, u32[]{:S(2)}) copy-start(f32[32,512]{1,0:T(8,128)} %v0.1) | copy-start | bytes 196612
  0.6 23.4 %copy-start.2 = (f32[32,512]{1,0:T(8,128)S(1)}, f32[32,512]{1,0:T(8,128)}, u32[]{:S(2)}) copy-start(f32[32,512]{1,0:T(8,128)} %diagonal.5) | copy-start | bytes 196612
  4.1 19.9 %copy-start.7 = (f32[1,128]{1,0:T(1,128)S(1)}, f32[1,128]{1,0:T(1,128)}, u32[]{:S(2)}) copy-start(f32[1,128]{1,0:T(1,128)} %get-tuple-element.27.moments) | copy-start | bytes 1540
  4.1 14.8 %collective-permute-start.1 = (f32[32,128]{1,0:T(8,128)}, f32[32,128]{1,0:T(8,128)S(1)}, u32[]{:S(2)}, u32[]{:S(2)}) collective-permute-start(f32[32,128]{1,0:T(8,128)} %get-tuple-element.24.block), channel_id=1, source_target_pairs={{0,248},{8,0},{16,8},{24,16},{32,24},{40,32},{48,40},{56,48},{64,5... | collective-permute-start | bytes 49160 | tf_op jit(solution)/shard_map/ppermute | solution.py:338
  12.8 6.1 %collective-permute-start = (f32[32,128]{1,0:T(8,128)}, f32[32,128]{1,0:T(8,128)S(1)}, u32[]{:S(2)}, u32[]{:S(2)}) collective-permute-start(f32[32,128]{1,0:T(8,128)} %get-tuple-element.24.block), channel_id=1, source_target_pairs={{0,8},{8,16},{16,24},{24,32},{32,40},{40,48},{48,56},{56,64},{64,7... | collective-permute-start | bytes 49160 | tf_op jit(solution)/shard_map/ppermute | solution.py:338
  12.9 2.2 %copy-start = (f32[32,64,512]{2,1,0:T(8,128)S(1)}, f32[32,64,512]{2,1,0:T(8,128)}, u32[]{:S(2)}) copy-start(f32[32,64,512]{2,1,0:T(8,128)} %features.9) | copy-start | bytes 12582916
  15.0 0.7 copy-start.5
  15.8 8.3 %copy-start.1 = (f32[32,64,512]{2,1,0:T(8,128)S(1)}, f32[32,64,512]{2,1,0:T(8,128)}, u32[]{:S(2)}) copy-start(f32[32,64,512]{2,1,0:T(8,128)} %features.9) | copy-start | bytes 12582916
  18.9 5.1 %collective-permute-start.3 = (f32[96,128]{1,0:T(8,128)S(1)}, f32[96,128]{1,0:T(8,128)S(1)}, u32[]{:S(2)}, u32[]{:S(2)}) collective-permute-start(f32[96,128]{1,0:T(8,128)S(1)} %constant_dynamic-update-slice_fusion.column), channel_id=1, source_target_pairs={{0,7},{1,0},{2,1},{3,2},{4,3},{5,4},{6,5},{7,6},{8,15},{9,8},{10,9... | collective-permute-start | bytes 147464 | tf_op jit(solution)/shard_map/ppermute | solution.py:343
  21.0 3.0 %collective-permute-start.2 = (f32[96,128]{1,0:T(8,128)S(1)}, f32[96,128]{1,0:T(8,128)S(1)}, u32[]{:S(2)}, u32[]{:S(2)}) collective-permute-start(f32[96,128]{1,0:T(8,128)S(1)} %constant_dynamic-update-slice_fusion.column), channel_id=1, source_target_pairs={{0,1},{1,2},{2,3},{3,4},{4,5},{5,6},{6,7},{7,0},{8,9},{9,10},{10,1... | collective-permute-start | bytes 147464 | tf_op jit(solution)/shard_map/ppermute | solution.py:341
  26.8 5.9 %collective-permute-start.4 = (f32[32,128]{1,0:T(8,128)S(1)}, f32[32,128]{1,0:T(8,128)S(1)}, u32[]{:S(2)}, u32[]{:S(2)}) collective-permute-start(f32[32,128]{1,0:T(8,128)S(1)} %get-tuple-element.29), channel_id=1, source_target_pairs={{0,8},{8,16},{16,24},{24,32},{32,40},{40,48},{48,56},{56,64},{64,7... | collective-permute-start | bytes 49160 | tf_op jit(solution)/shard_map/ppermute | solution.py:338
  26.8 5.9 %collective-permute-start.5 = (f32[32,128]{1,0:T(8,128)S(1)}, f32[32,128]{1,0:T(8,128)S(1)}, u32[]{:S(2)}, u32[]{:S(2)}) collective-permute-start(f32[32,128]{1,0:T(8,128)S(1)} %get-tuple-element.29), channel_id=1, source_target_pairs={{0,248},{8,0},{16,8},{24,16},{32,24},{40,32},{48,40},{56,48},{64,5... | collective-permute-start | bytes 49160 | tf_op jit(solution)/shard_map/ppermute | solution.py:338
  32.8 8.2 %collective-permute-start.7 = (f32[96,128]{1,0:T(8,128)S(1)}, f32[96,128]{1,0:T(8,128)S(1)}, u32[]{:S(2)}, u32[]{:S(2)}) collective-permute-start(f32[96,128]{1,0:T(8,128)S(1)} %constant_dynamic-update-slice_fusion.3.column), channel_id=1, source_target_pairs={{0,7},{1,0},{2,1},{3,2},{4,3},{5,4},{6,5},{7,6},{8,15},{9,8},{10,9... | collective-permute-start | bytes 147464 | tf_op jit(solution)/shard_map/ppermute | solution.py:343
  36.7 4.2 %collective-permute-start.6 = (f32[96,128]{1,0:T(8,128)S(1)}, f32[96,128]{1,0:T(8,128)S(1)}, u32[]{:S(2)}, u32[]{:S(2)}) collective-permute-start(f32[96,128]{1,0:T(8,128)S(1)} %constant_dynamic-update-slice_fusion.3.column), channel_id=1, source_target_pairs={{0,1},{1,2},{2,3},{3,4},{4,5},{5,6},{6,7},{7,0},{8,9},{9,10},{10,1... | collective-permute-start | bytes 147464 | tf_op jit(solution)/shard_map/ppermute | solution.py:341
  36.7 4.2 %collective-permute-start.8 = (f32[32,128]{1,0:T(8,128)S(1)}, f32[32,128]{1,0:T(8,128)S(1)}, u32[]{:S(2)}, u32[]{:S(2)}) collective-permute-start(f32[32,128]{1,0:T(8,128)S(1)} %get-tuple-element.28.near), channel_id=1, source_target_pairs={{0,4},{1,5},{2,6},{3,7},{4,0},{5,1},{6,2},{7,3},{8,12},{9,13},{10,... | collective-permute-start | bytes 49160 | tf_op jit(solution)/shard_map/ppermute | solution.py:384
  42.4 30.3 %copy-start.4 = (f32[64,1024]{1,0:T(8,128)S(1)}, f32[64,1024]{1,0:T(8,128)}, u32[]{:S(2)}) copy-start(f32[64,1024]{1,0:T(8,128)} %vertex_features.1) | copy-start | bytes 786436
  42.4 30.4 %copy-start.6 = (s32[1024]{0:T(1024)S(1)}, s32[1024]{0:T(1024)}, u32[]{:S(2)}) copy-start(s32[1024]{0:T(1024)} %param.11) | copy-start | bytes 12292
  42.4 7.3 %collective-permute-start.10 = (f32[32,128]{1,0:T(8,128)S(1)}, f32[32,128]{1,0:T(8,128)S(1)}, u32[]{:S(2)}, u32[]{:S(2)}) collective-permute-start(f32[32,128]{1,0:T(8,128)S(1)} %get-tuple-element.34.block), channel_id=1, source_target_pairs={{0,248},{8,0},{16,8},{24,16},{32,24},{40,32},{48,40},{56,48},{64,5... | collective-permute-start | bytes 49160 | tf_op jit(solution)/shard_map/ppermute | solution.py:389
  47.5 5.9 %collective-permute-start.9 = (f32[32,128]{1,0:T(8,128)S(1)}, f32[32,128]{1,0:T(8,128)S(1)}, u32[]{:S(2)}, u32[]{:S(2)}) collective-permute-start(f32[32,128]{1,0:T(8,128)S(1)} %get-tuple-element.34.block), channel_id=1, source_target_pairs={{0,8},{8,16},{16,24},{24,32},{32,40},{40,48},{48,56},{56,64},{64,7... | collective-permute-start | bytes 49160 | tf_op jit(solution)/shard_map/ppermute | solution.py:389
  68.9 12.4 %all-to-all-start.1 = ((f32[32,1,128]{2,1,0:T(1,128)}), f32[32,1,128]{2,1,0:T(1,128)S(1)}, u32[]{:S(2)}, u32[]{:S(2)}) async-start(f32[32,1,128]{2,1,0:T(1,128)} %bitcast.3), calls=%async_computation.1 | async-start | bytes 32768 | tf_op jit(solution)/shard_map/all_to_all | solution.py:405

commit v8 on v5

--- a/solution.py
+++ b/solution.py
@@ -34,9 +34,10 @@
     return jax.ShapeDtypeStruct(shape, F32)
 
 
-def ring(axis, step):
+def swaps(axis, first):
     count = lax.axis_size(axis)
-    return [(i, (i + step) % count) for i in range(count)]
+    pairs = [(i, (i + 1) % count) for i in range(first, count, 2)]
+    return pairs + [(b, a) for a, b in pairs]
 
 
 def lane_iota(rows, lanes=LANES):
@@ -102,7 +103,9 @@
     offset_x = lax.shift_right_arithmetic(owner, across.bit_length() - 1) - row_index + 1
     offset_y = (owner & (across - 1)) - col_index + 1
     inside = (ids >= 0) & (offset_x >= 0) & (offset_x < 3) & (offset_y >= 0) & (offset_y < 3)
-    return jnp.where(inside, offset_y * LANES + offset_x * nrows + (ids & (nrows - 1)), -1)
+    slot_x = jnp.where((row_index & 1) == 0, 2 - offset_x, offset_x)
+    slot_y = jnp.where((col_index & 1) == 0, 2 - offset_y, offset_y)
+    return jnp.where(inside, slot_y * LANES + slot_x * nrows + (ids & (nrows - 1)), -1)
 
 
 def one_hot(position, first, lanes, width, slots):
@@ -309,13 +312,10 @@
 
 
 def neighbourhood(block, copy=None):
-    up, down = lax.ppermute(block, "gx", ring("gx", 1)), lax.ppermute(block, "gx", ring("gx", -1))
-    column = jnp.concatenate([up, block if copy is None else copy, down])
-    return (
-        lax.ppermute(column, "gy", ring("gy", 1)),
-        column,
-        lax.ppermute(column, "gy", ring("gy", -1)),
-    )
+    second, first = lax.ppermute(block, "gx", swaps("gx", 1)), lax.ppermute(block, "gx", swaps("gx", 0))
+    column = jnp.concatenate([first, block if copy is None else copy, second])
+    after, before = lax.ppermute(column, "gy", swaps("gy", 1)), lax.ppermute(column, "gy", swaps("gy", 0))
+    return before, column, after
 
 
 def per_device(right_side, diagonal, features, neighbours, vertex_features, vertex_bricks):

time: 81.9 us -> 76.6 us (0.935)
  starting transfers between devices: 37.1 us -> 27.6 us
  waiting for transfers between devices: 14.9 us -> 18.8 us
    ppermute x12, starting transfers between devices: 30.3 us -> 23.8 us  [the longest x3 11.3 us: neighbourhood(): lax.ppermute(block, 'gx', swaps('gx', 1))]
    ppermute x12, waiting for transfers between devices: 7.64 us -> 11.5 us  [the longest x3 7.96 us: neighbourhood(): lax.ppermute(block, 'gx', swaps('gx', 1))]
    all_to_all x1, starting transfers between devices: 6.71 us -> 3.83 us  [per_device(): lax.all_to_all(call(fold_kernel, f32(along, LANES), slab), 'gx', 0, 0, ti...]
  transfers between devices with their start and end apart: 13 -> 13, of which waited for: 9 -> 7; matrix products, arithmetic and copies ran while one was open for 0% -> 0% of each run, Pallas kernels for 4% -> 4%
where the time goes in v8:
time: 76.6 us; the launch traced here: 76.3 us
  starting transfers between devices  27.6 us (36%)
  waiting for transfers between devices  18.8 us (25%)
  Pallas kernels  13.4 us (17%)
  blocking collectives  12.7 us (17%)
  local copies, waits for them, and re-layouts  2.95 us (4%)
  between operations  0.82 us (1%)
    pallas_call x9, Pallas kernels, call(): pl.pallas_call(kernel, out_shape=out_shape, in_specs=specs or [VMEM] * le...  13.4 us
    all_to_all x1, blocking collectives, per_device(): slab = lax.all_to_all(sums, 'gy', 0, 0, tiled=True)  12.7 us
    ppermute x3, starting transfers between devices, neighbourhood(): lax.ppermute(block, 'gx', swaps('gx', 1))  11.3 us
    ppermute x3, starting transfers between devices, neighbourhood(): lax.ppermute(column, 'gy', swaps('gy', 1))  8.36 us
    ppermute x3, waiting for transfers between devices, neighbourhood(): lax.ppermute(block, 'gx', swaps('gx', 1))  7.96 us
    all_to_all x1, waiting for transfers between devices, per_device(): lax.all_to_all(call(fold_kernel, f32(along, LANES), slab), 'gx', 0, 0, ti...  7.31 us
    all_to_all x1, starting transfers between devices, per_device(): lax.all_to_all(call(fold_kernel, f32(along, LANES), slab), 'gx', 0, 0, ti...  3.83 us
    unnamed x22, local copies, waits for them, and re-layouts  2.94 us
  transfers between devices with their start and end apart: 13, of which 7 were waited for; matrix products, arithmetic and copies ran while one was open for 0% of the time, Pallas kernels for 4%

profile of v8, /device:TPU:1, one launch (start us, length us, event | category | flops | bytes accessed | tf_op | source)
XLA Modules:
  0.0 76.3 jit_solution(11678407772038196459)
XLA Ops:
  0.7 3.4 %shard_map.85 = (f32[32,128]{1,0:T(8,128)}, f32[1,128]{1,0:T(1,128)}) custom-call(f32[32,64,512]{2,1,0:T(8,128)} %features.9, f32[32,512]{1,0:T(8,128)} %v0.1, s32[32,27]{1,0:T(8,128)} %neighbours.1), custom_call_target="tpu_custom_call" | custom-call | tf_op jit(solution)/shard_map/pallas_call | solution.py:23
  4.1 8.7 %collective-permute-start.1 = (f32[32,128]{1,0:T(8,128)}, f32[32,128]{1,0:T(8,128)S(1)}, u32[]{:S(2)}, u32[]{:S(2)}) collective-permute-start(f32[32,128]{1,0:T(8,128)} %get-tuple-element.21.block), channel_id=1, source_target_pairs={{8,16},{24,32},{40,48},{56,64},{72,80},{88,96},{104,112},{120,128}... | collective-permute-start | bytes 49160 | tf_op jit(solution)/shard_map/ppermute | solution.py:315
  12.8 0.1 pad_add_fusion.index
  12.9 2.2 %copy-done = f32[32,64,512]{2,1,0:T(8,128)S(1)} copy-done((f32[32,64,512]{2,1,0:T(8,128)S(1)}, f32[32,64,512]{2,1,0:T(8,128)}, u32[]{:S(2)}) %copy-start) | copy-done | bytes 4194328
  15.1 0.7 copy-done.5
  15.8 0.8 %shard_map.86 = (bf16[32,384]{1,0:T(8,128)(2,1)S(1)}, f32[32,128]{1,0:T(8,128)S(1)}) custom-call(s32[2]{0:T(128)S(1)} %pad_add_fusion.index, f32[32,128]{1,0:T(8,128)S(1)} %copy-done.5, f32[32,64,512]{2,1,0:T(8,128)S(1)} %copy-done), custom_call_target="tpu_custom_call" | custom-call | tf_op jit(solution)/shard_map/pallas_call | solution.py:23
  16.6 2.4 %collective-permute-start.3 = (f32[96,128]{1,0:T(8,128)S(1)}, f32[96,128]{1,0:T(8,128)S(1)}, u32[]{:S(2)}, u32[]{:S(2)}) collective-permute-start(f32[96,128]{1,0:T(8,128)S(1)} %constant_dynamic-update-slice_fusion.column), channel_id=1, source_target_pairs={{1,2},{3,4},{5,6},{7,0},{2,1},{4,3},{6,5},{0,7},{9,10},{11,12},{13... | collective-permute-start | bytes 147464 | tf_op jit(solution)/shard_map/ppermute | solution.py:317
  19.0 0.8 %collective-permute-start.2 = (f32[96,128]{1,0:T(8,128)S(1)}, f32[96,128]{1,0:T(8,128)S(1)}, u32[]{:S(2)}, u32[]{:S(2)}) collective-permute-start(f32[96,128]{1,0:T(8,128)S(1)} %constant_dynamic-update-slice_fusion.column), channel_id=1, source_target_pairs={{0,1},{2,3},{4,5},{6,7},{1,0},{3,2},{5,4},{7,6},{8,9},{10,11},{12,... | collective-permute-start | bytes 147464 | tf_op jit(solution)/shard_map/ppermute | solution.py:317
  19.8 1.1 %shard_map.87.known = f32[32,384]{1,0:T(8,128)S(1)} custom-call(s32[2]{0:T(128)S(1)} %pad_add_fusion.index, f32[96,128]{1,0:T(8,128)S(1)} %constant_dynamic-update-slice_fusion.column, bf16[32,384]{1,0:T(8,128)(2,1)S(1)} %get-tuple-element.23.own), custom_call_target="tpu_custom_call" | custom-call | tf_op jit(solution)/shard_map/pallas_call | solution.py:23
  21.0 2.8 %shard_map.88 = (f32[32,512]{1,0:T(8,128)S(1)}, f32[32,128]{1,0:T(8,128)S(1)}, f32[64,128]{1,0:T(8,128)S(1)}, f32[1,128]{1,0:T(1,128)S(1)}, bf16[128,384]{1,0:T(8,128)(2,1)S(1)}) custom-call(s32[2]{0:T(128)S(1)} %pad_add_fusion.index, f32[96,128]{1,0:T(8,128)S(1)} %collective-permute-done.2.left, f32[96,128]{1,0:T(8,128)S(1)} %constant_dynamic-update-slice_fusion.column, ...), custom_call_target="tpu_custom_call" | custom-call | tf_op jit(solution)/shard_map/pallas_call | solution.py:23
  23.8 1.5 %collective-permute-start.4 = (f32[32,128]{1,0:T(8,128)S(1)}, f32[32,128]{1,0:T(8,128)S(1)}, u32[]{:S(2)}, u32[]{:S(2)}) collective-permute-start(f32[32,128]{1,0:T(8,128)S(1)} %get-tuple-element.25), channel_id=1, source_target_pairs={{0,8},{16,24},{32,40},{48,56},{64,72},{80,88},{96,104},{112,120},{... | collective-permute-start | bytes 49160 | tf_op jit(solution)/shard_map/ppermute | solution.py:315
  25.3 1.4 %collective-permute-start.5 = (f32[32,128]{1,0:T(8,128)S(1)}, f32[32,128]{1,0:T(8,128)S(1)}, u32[]{:S(2)}, u32[]{:S(2)}) collective-permute-start(f32[32,128]{1,0:T(8,128)S(1)} %get-tuple-element.25), channel_id=1, source_target_pairs={{8,16},{24,32},{40,48},{56,64},{72,80},{88,96},{104,112},{120,128}... | collective-permute-start | bytes 49160 | tf_op jit(solution)/shard_map/ppermute | solution.py:315
  26.6 4.5 %collective-permute-done.5 = f32[32,128]{1,0:T(8,128)S(1)} collective-permute-done((f32[32,128]{1,0:T(8,128)S(1)}, f32[32,128]{1,0:T(8,128)S(1)}, u32[]{:S(2)}, u32[]{:S(2)}) %collective-permute-start.5) | collective-permute-done | bytes 16416 | tf_op jit(solution)/shard_map/ppermute | solution.py:315
  31.2 3.1 %collective-permute-start.7 = (f32[96,128]{1,0:T(8,128)S(1)}, f32[96,128]{1,0:T(8,128)S(1)}, u32[]{:S(2)}, u32[]{:S(2)}) collective-permute-start(f32[96,128]{1,0:T(8,128)S(1)} %constant_dynamic-update-slice_fusion.3.column), channel_id=1, source_target_pairs={{1,2},{3,4},{5,6},{7,0},{2,1},{4,3},{6,5},{0,7},{9,10},{11,12},{13... | collective-permute-start | bytes 147464 | tf_op jit(solution)/shard_map/ppermute | solution.py:317
  34.3 0.5 collective-permute-start.6
  34.8 1.3 %collective-permute-done.7.right = f32[96,128]{1,0:T(8,128)S(1)} collective-permute-done((f32[96,128]{1,0:T(8,128)S(1)}, f32[96,128]{1,0:T(8,128)S(1)}, u32[]{:S(2)}, u32[]{:S(2)}) %collective-permute-start.7) | collective-permute-done | bytes 49184 | tf_op jit(solution)/shard_map/ppermute | solution.py:317
  36.1 1.5 %shard_map.89 = (f32[32,512]{1,0:T(8,128)S(1)}, f32[32,128]{1,0:T(8,128)S(1)}, f32[64,128]{1,0:T(8,128)S(1)}, f32[1,128]{1,0:T(1,128)S(1)}) custom-call(f32[96,128]{1,0:T(8,128)S(1)} %collective-permute-done.6.left, f32[96,128]{1,0:T(8,128)S(1)} %constant_dynamic-update-slice_fusion.3.column, f32[96,128]{1,0:T(8,128)S(1)} %collective-permute-done.7.right, ...), custom_call_target="tpu_custom_call" | custom-call | tf_op jit(solution)/shard_map/pallas_call | solution.py:23
  37.5 0.0 collective-permute-start.8
  37.6 1.2 %collective-permute-start.9 = (f32[32,128]{1,0:T(8,128)S(1)}, f32[32,128]{1,0:T(8,128)S(1)}, u32[]{:S(2)}, u32[]{:S(2)}) collective-permute-start(f32[32,128]{1,0:T(8,128)S(1)} %get-tuple-element.30), channel_id=1, source_target_pairs={{8,16},{24,32},{40,48},{56,64},{72,80},{88,96},{104,112},{120,128}... | collective-permute-start | bytes 49160 | tf_op jit(solution)/shard_map/ppermute | solution.py:315
  38.8 1.3 %collective-permute-done.8 = f32[32,128]{1,0:T(8,128)S(1)} collective-permute-done((f32[32,128]{1,0:T(8,128)S(1)}, f32[32,128]{1,0:T(8,128)S(1)}, u32[]{:S(2)}, u32[]{:S(2)}) %collective-permute-start.8) | collective-permute-done | bytes 16416 | tf_op jit(solution)/shard_map/ppermute | solution.py:315
  40.2 3.4 %collective-permute-done.9 = f32[32,128]{1,0:T(8,128)S(1)} collective-permute-done((f32[32,128]{1,0:T(8,128)S(1)}, f32[32,128]{1,0:T(8,128)S(1)}, u32[]{:S(2)}, u32[]{:S(2)}) %collective-permute-start.9) | collective-permute-done | bytes 16416 | tf_op jit(solution)/shard_map/ppermute | solution.py:315
  43.6 2.9 %collective-permute-start.11 = (f32[96,128]{1,0:T(8,128)S(1)}, f32[96,128]{1,0:T(8,128)S(1)}, u32[]{:S(2)}, u32[]{:S(2)}) collective-permute-start(f32[96,128]{1,0:T(8,128)S(1)} %constant_dynamic-update-slice_fusion.6.column), channel_id=1, source_target_pairs={{1,2},{3,4},{5,6},{7,0},{2,1},{4,3},{6,5},{0,7},{9,10},{11,12},{13... | collective-permute-start | bytes 147464 | tf_op jit(solution)/shard_map/ppermute | solution.py:317
  46.5 1.2 %collective-permute-start.10 = (f32[96,128]{1,0:T(8,128)S(1)}, f32[96,128]{1,0:T(8,128)S(1)}, u32[]{:S(2)}, u32[]{:S(2)}) collective-permute-start(f32[96,128]{1,0:T(8,128)S(1)} %constant_dynamic-update-slice_fusion.6.column), channel_id=1, source_target_pairs={{0,1},{2,3},{4,5},{6,7},{1,0},{3,2},{5,4},{7,6},{8,9},{10,11},{12,... | collective-permute-start | bytes 147464 | tf_op jit(solution)/shard_map/ppermute | solution.py:317
  47.7 0.5 collective-permute-done.11.right
  48.2 0.4 collective-permute-done.10.left
  48.6 1.1 %shard_map.90 = (f32[32,512]{1,0:T(8,128)S(1)}, f32[8,64,128]{2,1,0:T(8,128)S(1)}) custom-call(f32[96,128]{1,0:T(8,128)S(1)} %collective-permute-done.10.left, f32[96,128]{1,0:T(8,128)S(1)} %constant_dynamic-update-slice_fusion.6.column, f32[96,128]{1,0:T(8,128)S(1)} %collective-permute-done.11.right, bf16[128,384]{1,0:T(8,128)(2,1)S(1)} %get-tuple-element.26.weights, ...), custom_call_target="tpu_custom_call" | custom-call | tf_op jit(solution)/shard_map/pallas_call | solution.py:23
  49.7 12.7 %all_to_all.16.slab = f32[8,64,128]{2,1,0:T(8,128)S(1)} all-to-all(f32[8,64,128]{2,1,0:T(8,128)S(1)} %get-tuple-element.34), channel_id=1, replica_groups=mesh['gx'=32,'gy'=8] {'gy'}, dimensions={0} | all-to-all | bytes 524288 | tf_op jit(solution)/shard_map/all_to_all | solution.py:367
  62.4 0.6 shard_map.91
  63.1 3.8 %all-to-all-start.1 = ((f32[32,1,128]{2,1,0:T(1,128)}), f32[32,1,128]{2,1,0:T(1,128)S(1)}, u32[]{:S(2)}, u32[]{:S(2)}) async-start(f32[32,1,128]{2,1,0:T(1,128)} %bitcast.3), calls=%async_computation.1 | async-start | bytes 32768 | tf_op jit(solution)/shard_map/all_to_all | solution.py:368
  66.9 1.2 %shard_map.92.vertices = f32[8,1024]{1,0:T(8,128)S(1)} custom-call(s32[2]{0:T(128)S(1)} %pad_add_fusion.index, f32[8,64,128]{2,1,0:T(8,128)S(1)} %all_to_all.16.slab, s32[1,1024]{1,0:T(1,128)S(1)} %bitcast.9, f32[64,1024]{1,0:T(8,128)S(1)} %copy-done.4), custom_call_target="tpu_custom_call" | custom-call | tf_op jit(solution)/shard_map/pallas_call | solution.py:23
  68.1 7.3 %all-to-all-done.1 = f32[32,1,128]{2,1,0:T(1,128)S(1)} async-done(((f32[32,1,128]{2,1,0:T(1,128)}), f32[32,1,128]{2,1,0:T(1,128)S(1)}, u32[]{:S(2)}, u32[]{:S(2)}) %all-to-all-start.1) | async-done | bytes 16416 | tf_op jit(solution)/shard_map/all_to_all | solution.py:368
  75.4 0.9 %shard_map.93 = (f32[32,512]{1,0:T(8,128)}, f32[32,512]{1,0:T(8,128)}, f32[1,1024]{1,0:T(1,128)}) custom-call(f32[32,128]{1,0:T(8,128)S(1)} %bitcast.8, f32[32,512]{1,0:T(8,128)S(1)} %copy-done.3, f32[32,512]{1,0:T(8,128)S(1)} %get-tuple-element.27.before.v1, f32[32,512]{1,0:T(8,128)S(1)} %get-tuple-element.31.before.v2, ...), custom_call_target="tpu_custom_call" | custom-call | tf_op jit(solution)/shard_map/pallas_call | solution.py:23
  (30 shorter events, 0.1 us)
Async XLA Ops:
  0.6 20.3 %copy-start.3 = (f32[32,512]{1,0:T(8,128)S(1)}, f32[32,512]{1,0:T(8,128)}, u32[]{:S(2)}) copy-start(f32[32,512]{1,0:T(8,128)} %v0.1) | copy-start | bytes 196612
  0.6 20.3 %copy-start.2 = (f32[32,512]{1,0:T(8,128)S(1)}, f32[32,512]{1,0:T(8,128)}, u32[]{:S(2)}) copy-start(f32[32,512]{1,0:T(8,128)} %diagonal.5) | copy-start | bytes 196612
  4.1 16.9 %copy-start.7 = (f32[1,128]{1,0:T(1,128)S(1)}, f32[1,128]{1,0:T(1,128)}, u32[]{:S(2)}) copy-start(f32[1,128]{1,0:T(1,128)} %get-tuple-element.24.moments) | copy-start | bytes 1540
  4.1 12.5 %collective-permute-start.1 = (f32[32,128]{1,0:T(8,128)}, f32[32,128]{1,0:T(8,128)S(1)}, u32[]{:S(2)}, u32[]{:S(2)}) collective-permute-start(f32[32,128]{1,0:T(8,128)} %get-tuple-element.21.block), channel_id=1, source_target_pairs={{8,16},{24,32},{40,48},{56,64},{72,80},{88,96},{104,112},{120,128}... | collective-permute-start | bytes 49160 | tf_op jit(solution)/shard_map/ppermute | solution.py:315
  12.8 3.8 %collective-permute-start = (f32[32,128]{1,0:T(8,128)}, f32[32,128]{1,0:T(8,128)S(1)}, u32[]{:S(2)}, u32[]{:S(2)}) collective-permute-start(f32[32,128]{1,0:T(8,128)} %get-tuple-element.21.block), channel_id=1, source_target_pairs={{0,8},{16,24},{32,40},{48,56},{64,72},{80,88},{96,104},{112,120},{... | collective-permute-start | bytes 49160 | tf_op jit(solution)/shard_map/ppermute | solution.py:315
  12.9 2.2 %copy-start = (f32[32,64,512]{2,1,0:T(8,128)S(1)}, f32[32,64,512]{2,1,0:T(8,128)}, u32[]{:S(2)}) copy-start(f32[32,64,512]{2,1,0:T(8,128)} %features.9) | copy-start | bytes 12582916
  15.1 0.7 copy-start.5
  15.8 5.2 %copy-start.1 = (f32[32,64,512]{2,1,0:T(8,128)S(1)}, f32[32,64,512]{2,1,0:T(8,128)}, u32[]{:S(2)}) copy-start(f32[32,64,512]{2,1,0:T(8,128)} %features.9) | copy-start | bytes 12582916
  16.6 4.3 %collective-permute-start.3 = (f32[96,128]{1,0:T(8,128)S(1)}, f32[96,128]{1,0:T(8,128)S(1)}, u32[]{:S(2)}, u32[]{:S(2)}) collective-permute-start(f32[96,128]{1,0:T(8,128)S(1)} %constant_dynamic-update-slice_fusion.column), channel_id=1, source_target_pairs={{1,2},{3,4},{5,6},{7,0},{2,1},{4,3},{6,5},{0,7},{9,10},{11,12},{13... | collective-permute-start | bytes 147464 | tf_op jit(solution)/shard_map/ppermute | solution.py:317
  19.0 2.0 %collective-permute-start.2 = (f32[96,128]{1,0:T(8,128)S(1)}, f32[96,128]{1,0:T(8,128)S(1)}, u32[]{:S(2)}, u32[]{:S(2)}) collective-permute-start(f32[96,128]{1,0:T(8,128)S(1)} %constant_dynamic-update-slice_fusion.column), channel_id=1, source_target_pairs={{0,1},{2,3},{4,5},{6,7},{1,0},{3,2},{5,4},{7,6},{8,9},{10,11},{12,... | collective-permute-start | bytes 147464 | tf_op jit(solution)/shard_map/ppermute | solution.py:317
  23.8 2.9 %collective-permute-start.4 = (f32[32,128]{1,0:T(8,128)S(1)}, f32[32,128]{1,0:T(8,128)S(1)}, u32[]{:S(2)}, u32[]{:S(2)}) collective-permute-start(f32[32,128]{1,0:T(8,128)S(1)} %get-tuple-element.25), channel_id=1, source_target_pairs={{0,8},{16,24},{32,40},{48,56},{64,72},{80,88},{96,104},{112,120},{... | collective-permute-start | bytes 49160 | tf_op jit(solution)/shard_map/ppermute | solution.py:315
  25.3 5.9 %collective-permute-start.5 = (f32[32,128]{1,0:T(8,128)S(1)}, f32[32,128]{1,0:T(8,128)S(1)}, u32[]{:S(2)}, u32[]{:S(2)}) collective-permute-start(f32[32,128]{1,0:T(8,128)S(1)} %get-tuple-element.25), channel_id=1, source_target_pairs={{8,16},{24,32},{40,48},{56,64},{72,80},{88,96},{104,112},{120,128}... | collective-permute-start | bytes 49160 | tf_op jit(solution)/shard_map/ppermute | solution.py:315
  31.2 4.9 %collective-permute-start.7 = (f32[96,128]{1,0:T(8,128)S(1)}, f32[96,128]{1,0:T(8,128)S(1)}, u32[]{:S(2)}, u32[]{:S(2)}) collective-permute-start(f32[96,128]{1,0:T(8,128)S(1)} %constant_dynamic-update-slice_fusion.3.column), channel_id=1, source_target_pairs={{1,2},{3,4},{5,6},{7,0},{2,1},{4,3},{6,5},{0,7},{9,10},{11,12},{13... | collective-permute-start | bytes 147464 | tf_op jit(solution)/shard_map/ppermute | solution.py:317
  34.3 1.8 %collective-permute-start.6 = (f32[96,128]{1,0:T(8,128)S(1)}, f32[96,128]{1,0:T(8,128)S(1)}, u32[]{:S(2)}, u32[]{:S(2)}) collective-permute-start(f32[96,128]{1,0:T(8,128)S(1)} %constant_dynamic-update-slice_fusion.3.column), channel_id=1, source_target_pairs={{0,1},{2,3},{4,5},{6,7},{1,0},{3,2},{5,4},{7,6},{8,9},{10,11},{12,... | collective-permute-start | bytes 147464 | tf_op jit(solution)/shard_map/ppermute | solution.py:317
  36.1 30.8 %copy-start.4 = (f32[64,1024]{1,0:T(8,128)S(1)}, f32[64,1024]{1,0:T(8,128)}, u32[]{:S(2)}) copy-start(f32[64,1024]{1,0:T(8,128)} %vertex_features.1) | copy-start | bytes 786436
  36.1 30.9 %copy-start.6 = (s32[1024]{0:T(1024)S(1)}, s32[1024]{0:T(1024)}, u32[]{:S(2)}) copy-start(s32[1024]{0:T(1024)} %param.11) | copy-start | bytes 12292
  37.5 2.6 %collective-permute-start.8 = (f32[32,128]{1,0:T(8,128)S(1)}, f32[32,128]{1,0:T(8,128)S(1)}, u32[]{:S(2)}, u32[]{:S(2)}) collective-permute-start(f32[32,128]{1,0:T(8,128)S(1)} %get-tuple-element.30), channel_id=1, source_target_pairs={{0,8},{16,24},{32,40},{48,56},{64,72},{80,88},{96,104},{112,120},{... | collective-permute-start | bytes 49160 | tf_op jit(solution)/shard_map/ppermute | solution.py:315
  37.6 6.0 %collective-permute-start.9 = (f32[32,128]{1,0:T(8,128)S(1)}, f32[32,128]{1,0:T(8,128)S(1)}, u32[]{:S(2)}, u32[]{:S(2)}) collective-permute-start(f32[32,128]{1,0:T(8,128)S(1)} %get-tuple-element.30), channel_id=1, source_target_pairs={{8,16},{24,32},{40,48},{56,64},{72,80},{88,96},{104,112},{120,128}... | collective-permute-start | bytes 49160 | tf_op jit(solution)/shard_map/ppermute | solution.py:315
  43.6 4.7 %collective-permute-start.11 = (f32[96,128]{1,0:T(8,128)S(1)}, f32[96,128]{1,0:T(8,128)S(1)}, u32[]{:S(2)}, u32[]{:S(2)}) collective-permute-start(f32[96,128]{1,0:T(8,128)S(1)} %constant_dynamic-update-slice_fusion.6.column), channel_id=1, source_target_pairs={{1,2},{3,4},{5,6},{7,0},{2,1},{4,3},{6,5},{0,7},{9,10},{11,12},{13... | collective-permute-start | bytes 147464 | tf_op jit(solution)/shard_map/ppermute | solution.py:317
  46.5 2.1 %collective-permute-start.10 = (f32[96,128]{1,0:T(8,128)S(1)}, f32[96,128]{1,0:T(8,128)S(1)}, u32[]{:S(2)}, u32[]{:S(2)}) collective-permute-start(f32[96,128]{1,0:T(8,128)S(1)} %constant_dynamic-update-slice_fusion.6.column), channel_id=1, source_target_pairs={{0,1},{2,3},{4,5},{6,7},{1,0},{3,2},{5,4},{7,6},{8,9},{10,11},{12,... | collective-permute-start | bytes 147464 | tf_op jit(solution)/shard_map/ppermute | solution.py:317
  63.1 12.4 %all-to-all-start.1 = ((f32[32,1,128]{2,1,0:T(1,128)}), f32[32,1,128]{2,1,0:T(1,128)S(1)}, u32[]{:S(2)}, u32[]{:S(2)}) async-start(f32[32,1,128]{2,1,0:T(1,128)} %bitcast.3), calls=%async_computation.1 | async-start | bytes 32768 | tf_op jit(solution)/shard_map/all_to_all | solution.py:368

commit v9 on v8

--- a/solution.py
+++ b/solution.py
@@ -103,7 +103,7 @@
     offset_x = lax.shift_right_arithmetic(owner, across.bit_length() - 1) - row_index + 1
     offset_y = (owner & (across - 1)) - col_index + 1
     inside = (ids >= 0) & (offset_x >= 0) & (offset_x < 3) & (offset_y >= 0) & (offset_y < 3)
-    slot_x = jnp.where((row_index & 1) == 0, 2 - offset_x, offset_x)
+    slot_x = jnp.where((row_index & 1) == 1, 2 - offset_x, offset_x)
     slot_y = jnp.where((col_index & 1) == 0, 2 - offset_y, offset_y)
     return jnp.where(inside, slot_y * LANES + slot_x * nrows + (ids & (nrows - 1)), -1)
 
@@ -124,16 +124,16 @@
     return table[:, d * LANES : (d + 1) * LANES]
 
 
-def own_kernel(shape, index, block, features, own, copy):
+def own_kernel(shape, index, block, own, copy):
     nrows, width, slots, across = shape
     copy[...] = block[...]
     place = positions(block[...], nrows, across, index[0], index[1])
     own[...] = one_hot(place, 0, 3 * LANES, width, slots)
 
 
-def middle_kernel(shape, index, column, own, twice):
+def middle_kernel(shape, index, column, own, features, twice):
     nrows, width, slots, across = shape
-    others = jnp.concatenate([column[:nrows, :], column[2 * nrows :, :]], axis=0)
+    others = jnp.concatenate([column[2 * nrows :, :], column[:nrows, :]], axis=0)
     place = positions(others, nrows, across, index[0], index[1])
     hot = one_hot(place, 0, 3 * LANES, width, slots)
     mine = own[...]
@@ -188,16 +188,17 @@
 ):
     nrows, width, slots, across = shape
     mine = own[...]
+    left, column, right = (turned_slots(side) for side in (left, column, right))
     thirds = [third_of(known, d) for d in range(3)]
     for d, side in ((0, left), (2, right)):
-        place = positions(side[...], nrows, across, index[0], index[1])
+        place = positions(side, nrows, across, index[0], index[1])
         hot = padded(one_hot(place, d * LANES, LANES, width, slots))
         thirds[d] = thirds[d] + jnp.dot(third_of(mine, d), hot, preferred_element_type=F32)
     twice = jnp.concatenate(thirds, axis=1).astype(BF16)
     pad = jnp.zeros((LANES - 2 * nrows, 3 * LANES), BF16)
     weights = jnp.concatenate([mine, twice, pad], axis=0)
     weights_out[...] = weights
-    around = jnp.concatenate([padded(side[...]) for side in (left, column, right)], axis=0)
+    around = jnp.concatenate([padded(side) for side in (left, column, right)], axis=0)
     sums, moment, columns = advance(
         0, nrows, width, weights, around, features, diagonal, before,
         jnp.zeros((width, LANES), F32), moments[...], [new],
@@ -311,9 +312,14 @@
     vertices_out[...] = sum(w * vertices[i : i + 1, :] for i, w in enumerate(field))
 
 
+def turned_slots(side):
+    nrows = side.shape[0] // 3
+    return jnp.concatenate([side[2 * nrows :, :], side[nrows : 2 * nrows, :], side[:nrows, :]], axis=0)
+
+
 def neighbourhood(block, copy=None):
     second, first = lax.ppermute(block, "gx", swaps("gx", 1)), lax.ppermute(block, "gx", swaps("gx", 0))
-    column = jnp.concatenate([first, block if copy is None else copy, second])
+    column = jnp.concatenate([second, block, first] if copy is None else [first, copy, second])
     after, before = lax.ppermute(column, "gy", swaps("gy", 1)), lax.ppermute(column, "gy", swaps("gy", 0))
     return before, column, after
 
@@ -341,12 +347,12 @@
     own, copy = call(
         functools.partial(own_kernel, shape),
         [jax.ShapeDtypeStruct((nrows, 3 * LANES), BF16), block_shape],
-        index, block, features, specs=[smem, VMEM, VMEM],
+        index, block, specs=[smem, VMEM],
     )
     left, column, right = neighbourhood(block, copy)
     known = call(
         functools.partial(middle_kernel, shape), f32(nrows, 3 * LANES),
-        index, column, own, specs=[smem, VMEM, VMEM],
+        index, column, own, features, specs=[smem, VMEM, VMEM, VMEM],
     )
     v1, block, sums, moments, weights = call(
         functools.partial(second_kernel, shape),

time: 76.6 us -> 75.7 us (0.988)
  starting transfers between devices: 27.6 us -> 28.8 us
  waiting for transfers between devices: 18.8 us -> 17.8 us
  blocking collectives: 12.7 us -> 11.9 us
    ppermute x3, starting transfers between devices: 11.3 us -> 14.8 us  [neighbourhood(): lax.ppermute(block, 'gx', swaps('gx', 1))]
    ppermute x3, starting transfers between devices: 2.58 us -> 0.13 us  [neighbourhood(): lax.ppermute(column, 'gy', swaps('gy', 0))]
    ppermute x3, waiting for transfers between devices: 7.96 us -> 5.83 us  [neighbourhood(): lax.ppermute(block, 'gx', swaps('gx', 1))]
    ppermute x3, waiting for transfers between devices: 1.81 us -> 3.42 us  [neighbourhood(): lax.ppermute(column, 'gy', swaps('gy', 1))]
    ppermute x3, starting transfers between devices: 1.55 us -> 0.01 us  [neighbourhood(): lax.ppermute(block, 'gx', swaps('gx', 0))]
    ppermute x3, starting transfers between devices: 8.36 us -> 9.27 us  [neighbourhood(): lax.ppermute(column, 'gy', swaps('gy', 1))]
    all_to_all x1, blocking collectives: 12.7 us -> 11.9 us  [per_device(): slab = lax.all_to_all(sums, 'gy', 0, 0, tiled=True)]
    all_to_all x1, starting transfers between devices: 3.83 us -> 4.6 us  [per_device(): lax.all_to_all(call(fold_kernel, f32(along, LANES), slab), 'gx', 0, 0, ti...]
  transfers between devices with their start and end apart: 13 -> 13, of which waited for: 7 -> 6; matrix products, arithmetic and copies ran while one was open for 0% -> 0% of each run, Pallas kernels for 4% -> 4%
where the time goes in v9:
time: 75.7 us; the launch traced here: 75.4 us
  starting transfers between devices  28.8 us (38%)
  waiting for transfers between devices  17.8 us (24%)
  Pallas kernels  13.1 us (17%)
  blocking collectives  11.9 us (16%)
  local copies, waits for them, and re-layouts  2.98 us (4%)
  between operations  0.79 us (1%)
    ppermute x3, starting transfers between devices, neighbourhood(): lax.ppermute(block, 'gx', swaps('gx', 1))  14.8 us
    pallas_call x9, Pallas kernels, call(): pl.pallas_call(kernel, out_shape=out_shape, in_specs=specs or [VMEM] * le...  13.1 us
    all_to_all x1, blocking collectives, per_device(): slab = lax.all_to_all(sums, 'gy', 0, 0, tiled=True)  11.9 us
    ppermute x3, starting transfers between devices, neighbourhood(): lax.ppermute(column, 'gy', swaps('gy', 1))  9.27 us
    all_to_all x1, waiting for transfers between devices, per_device(): lax.all_to_all(call(fold_kernel, f32(along, LANES), slab), 'gx', 0, 0, ti...  7.3 us
    ppermute x3, waiting for transfers between devices, neighbourhood(): lax.ppermute(block, 'gx', swaps('gx', 1))  5.83 us
    all_to_all x1, starting transfers between devices, per_device(): lax.all_to_all(call(fold_kernel, f32(along, LANES), slab), 'gx', 0, 0, ti...  4.6 us
    ppermute x3, waiting for transfers between devices, neighbourhood(): lax.ppermute(column, 'gy', swaps('gy', 1))  3.42 us
  transfers between devices with their start and end apart: 13, of which 6 were waited for; matrix products, arithmetic and copies ran while one was open for 0% of the time, Pallas kernels for 4%

profile of v9, /device:TPU:1, one launch (start us, length us, event | category | flops | bytes accessed | tf_op | source)
XLA Modules:
  0.0 75.4 jit_solution(12463386971198528550)
XLA Ops:
  0.7 3.4 %shard_map.85 = (f32[32,128]{1,0:T(8,128)}, f32[1,128]{1,0:T(1,128)}) custom-call(f32[32,64,512]{2,1,0:T(8,128)} %features.9, f32[32,512]{1,0:T(8,128)} %v0.1, s32[32,27]{1,0:T(8,128)} %neighbours.1), custom_call_target="tpu_custom_call" | custom-call | tf_op jit(solution)/shard_map/pallas_call | solution.py:23
  4.1 8.7 %collective-permute-start.1 = (f32[32,128]{1,0:T(8,128)}, f32[32,128]{1,0:T(8,128)S(1)}, u32[]{:S(2)}, u32[]{:S(2)}) collective-permute-start(f32[32,128]{1,0:T(8,128)} %get-tuple-element.21.block), channel_id=1, source_target_pairs={{8,16},{24,32},{40,48},{56,64},{72,80},{88,96},{104,112},{120,128}... | collective-permute-start | bytes 49160 | tf_op jit(solution)/shard_map/ppermute | solution.py:321
  12.8 0.1 pad_add_fusion.index
  12.9 0.7 copy-done.4
  13.6 0.8 %shard_map.86 = (bf16[32,384]{1,0:T(8,128)(2,1)S(1)}, f32[32,128]{1,0:T(8,128)S(1)}) custom-call(s32[2]{0:T(128)S(1)} %pad_add_fusion.index, f32[32,128]{1,0:T(8,128)S(1)} %copy-done.4), custom_call_target="tpu_custom_call" | custom-call | tf_op jit(solution)/shard_map/pallas_call | solution.py:23
  14.4 1.2 %collective-permute-done = f32[32,128]{1,0:T(8,128)S(1)} collective-permute-done((f32[32,128]{1,0:T(8,128)}, f32[32,128]{1,0:T(8,128)S(1)}, u32[]{:S(2)}, u32[]{:S(2)}) %collective-permute-start) | collective-permute-done | bytes 16416 | tf_op jit(solution)/shard_map/ppermute | solution.py:321
  15.6 0.0 collective-permute-done.1
  15.6 3.4 %collective-permute-start.3 = (f32[96,128]{1,0:T(8,128)S(1)}, f32[96,128]{1,0:T(8,128)S(1)}, u32[]{:S(2)}, u32[]{:S(2)}) collective-permute-start(f32[96,128]{1,0:T(8,128)S(1)} %constant_dynamic-update-slice_fusion.column), channel_id=1, source_target_pairs={{1,2},{3,4},{5,6},{7,0},{2,1},{4,3},{6,5},{0,7},{9,10},{11,12},{13... | collective-permute-start | bytes 147464 | tf_op jit(solution)/shard_map/ppermute | solution.py:323
  19.0 2.2 %copy-done = f32[32,64,512]{2,1,0:T(8,128)S(1)} copy-done((f32[32,64,512]{2,1,0:T(8,128)S(1)}, f32[32,64,512]{2,1,0:T(8,128)}, u32[]{:S(2)}) %copy-start) | copy-done | bytes 4194328
  21.2 1.1 %shard_map.87.known = f32[32,384]{1,0:T(8,128)S(1)} custom-call(s32[2]{0:T(128)S(1)} %pad_add_fusion.index, f32[96,128]{1,0:T(8,128)S(1)} %constant_dynamic-update-slice_fusion.column, bf16[32,384]{1,0:T(8,128)(2,1)S(1)} %get-tuple-element.23.own, f32[32,64,512]{2,1,0:T(8,128)S(1)} %copy-done), custom_call_target="tpu_custom_call" | custom-call | tf_op jit(solution)/shard_map/pallas_call | solution.py:23
  22.3 0.0 collective-permute-done.3.right
  22.3 0.0 collective-permute-done.2.left
  22.3 2.7 %shard_map.88 = (f32[32,512]{1,0:T(8,128)S(1)}, f32[32,128]{1,0:T(8,128)S(1)}, f32[64,128]{1,0:T(8,128)S(1)}, f32[1,128]{1,0:T(1,128)S(1)}, bf16[128,384]{1,0:T(8,128)(2,1)S(1)}) custom-call(s32[2]{0:T(128)S(1)} %pad_add_fusion.index, f32[96,128]{1,0:T(8,128)S(1)} %collective-permute-done.2.left, f32[96,128]{1,0:T(8,128)S(1)} %constant_dynamic-update-slice_fusion.column, ...), custom_call_target="tpu_custom_call" | custom-call | tf_op jit(solution)/shard_map/pallas_call | solution.py:23
  25.1 3.1 %collective-permute-start.4 = (f32[32,128]{1,0:T(8,128)S(1)}, f32[32,128]{1,0:T(8,128)S(1)}, u32[]{:S(2)}, u32[]{:S(2)}) collective-permute-start(f32[32,128]{1,0:T(8,128)S(1)} %get-tuple-element.25), channel_id=1, source_target_pairs={{8,16},{24,32},{40,48},{56,64},{72,80},{88,96},{104,112},{120,128}... | collective-permute-start | bytes 49160 | tf_op jit(solution)/shard_map/ppermute | solution.py:321
  28.2 0.0 collective-permute-start.5
  28.2 2.9 %collective-permute-done.4 = f32[32,128]{1,0:T(8,128)S(1)} collective-permute-done((f32[32,128]{1,0:T(8,128)S(1)}, f32[32,128]{1,0:T(8,128)S(1)}, u32[]{:S(2)}, u32[]{:S(2)}) %collective-permute-start.4) | collective-permute-done | bytes 16416 | tf_op jit(solution)/shard_map/ppermute | solution.py:321
  31.0 0.0 collective-permute-done.5
  31.0 2.9 %collective-permute-start.7 = (f32[96,128]{1,0:T(8,128)S(1)}, f32[96,128]{1,0:T(8,128)S(1)}, u32[]{:S(2)}, u32[]{:S(2)}) collective-permute-start(f32[96,128]{1,0:T(8,128)S(1)} %constant_dynamic-update-slice_fusion.3.column), channel_id=1, source_target_pairs={{1,2},{3,4},{5,6},{7,0},{2,1},{4,3},{6,5},{0,7},{9,10},{11,12},{13... | collective-permute-start | bytes 147464 | tf_op jit(solution)/shard_map/ppermute | solution.py:323
  34.0 1.8 %collective-permute-done.7.right = f32[96,128]{1,0:T(8,128)S(1)} collective-permute-done((f32[96,128]{1,0:T(8,128)S(1)}, f32[96,128]{1,0:T(8,128)S(1)}, u32[]{:S(2)}, u32[]{:S(2)}) %collective-permute-start.7) | collective-permute-done | bytes 49184 | tf_op jit(solution)/shard_map/ppermute | solution.py:323
  35.7 1.3 %shard_map.89 = (f32[32,512]{1,0:T(8,128)S(1)}, f32[32,128]{1,0:T(8,128)S(1)}, f32[64,128]{1,0:T(8,128)S(1)}, f32[1,128]{1,0:T(1,128)S(1)}) custom-call(f32[96,128]{1,0:T(8,128)S(1)} %collective-permute-done.6.left, f32[96,128]{1,0:T(8,128)S(1)} %constant_dynamic-update-slice_fusion.3.column, f32[96,128]{1,0:T(8,128)S(1)} %collective-permute-done.7.right, ...), custom_call_target="tpu_custom_call" | custom-call | tf_op jit(solution)/shard_map/pallas_call | solution.py:23
  37.1 3.0 %collective-permute-start.8 = (f32[32,128]{1,0:T(8,128)S(1)}, f32[32,128]{1,0:T(8,128)S(1)}, u32[]{:S(2)}, u32[]{:S(2)}) collective-permute-start(f32[32,128]{1,0:T(8,128)S(1)} %get-tuple-element.30), channel_id=1, source_target_pairs={{8,16},{24,32},{40,48},{56,64},{72,80},{88,96},{104,112},{120,128}... | collective-permute-start | bytes 49160 | tf_op jit(solution)/shard_map/ppermute | solution.py:321
  40.1 3.0 %collective-permute-done.8 = f32[32,128]{1,0:T(8,128)S(1)} collective-permute-done((f32[32,128]{1,0:T(8,128)S(1)}, f32[32,128]{1,0:T(8,128)S(1)}, u32[]{:S(2)}, u32[]{:S(2)}) %collective-permute-start.8) | collective-permute-done | bytes 16416 | tf_op jit(solution)/shard_map/ppermute | solution.py:321
  43.1 3.0 %collective-permute-start.11 = (f32[96,128]{1,0:T(8,128)S(1)}, f32[96,128]{1,0:T(8,128)S(1)}, u32[]{:S(2)}, u32[]{:S(2)}) collective-permute-start(f32[96,128]{1,0:T(8,128)S(1)} %constant_dynamic-update-slice_fusion.6.column), channel_id=1, source_target_pairs={{1,2},{3,4},{5,6},{7,0},{2,1},{4,3},{6,5},{0,7},{9,10},{11,12},{13... | collective-permute-start | bytes 147464 | tf_op jit(solution)/shard_map/ppermute | solution.py:323
  46.0 0.1 collective-permute-start.10
  46.2 1.6 %collective-permute-done.11.right = f32[96,128]{1,0:T(8,128)S(1)} collective-permute-done((f32[96,128]{1,0:T(8,128)S(1)}, f32[96,128]{1,0:T(8,128)S(1)}, u32[]{:S(2)}, u32[]{:S(2)}) %collective-permute-start.11) | collective-permute-done | bytes 49184 | tf_op jit(solution)/shard_map/ppermute | solution.py:323
  47.8 1.0 %shard_map.90 = (f32[32,512]{1,0:T(8,128)S(1)}, f32[8,64,128]{2,1,0:T(8,128)S(1)}) custom-call(f32[96,128]{1,0:T(8,128)S(1)} %collective-permute-done.10.left, f32[96,128]{1,0:T(8,128)S(1)} %constant_dynamic-update-slice_fusion.6.column, f32[96,128]{1,0:T(8,128)S(1)} %collective-permute-done.11.right, bf16[128,384]{1,0:T(8,128)(2,1)S(1)} %get-tuple-element.26.weights, ...), custom_call_target="tpu_custom_call" | custom-call | tf_op jit(solution)/shard_map/pallas_call | solution.py:23
  48.8 11.9 %all_to_all.16.slab = f32[8,64,128]{2,1,0:T(8,128)S(1)} all-to-all(f32[8,64,128]{2,1,0:T(8,128)S(1)} %get-tuple-element.34), channel_id=1, replica_groups=mesh['gx'=32,'gy'=8] {'gy'}, dimensions={0} | all-to-all | bytes 524288 | tf_op jit(solution)/shard_map/all_to_all | solution.py:373
  60.7 0.6 shard_map.91
  61.3 4.6 %all-to-all-start.1 = ((f32[32,1,128]{2,1,0:T(1,128)}), f32[32,1,128]{2,1,0:T(1,128)S(1)}, u32[]{:S(2)}, u32[]{:S(2)}) async-start(f32[32,1,128]{2,1,0:T(1,128)} %bitcast.3), calls=%async_computation.1 | async-start | bytes 32768 | tf_op jit(solution)/shard_map/all_to_all | solution.py:374
  66.0 1.2 %shard_map.92.vertices = f32[8,1024]{1,0:T(8,128)S(1)} custom-call(s32[2]{0:T(128)S(1)} %pad_add_fusion.index, f32[8,64,128]{2,1,0:T(8,128)S(1)} %all_to_all.16.slab, s32[1,1024]{1,0:T(1,128)S(1)} %bitcast.9, f32[64,1024]{1,0:T(8,128)S(1)} %copy-done.3), custom_call_target="tpu_custom_call" | custom-call | tf_op jit(solution)/shard_map/pallas_call | solution.py:23
  67.1 7.3 %all-to-all-done.1 = f32[32,1,128]{2,1,0:T(1,128)S(1)} async-done(((f32[32,1,128]{2,1,0:T(1,128)}), f32[32,1,128]{2,1,0:T(1,128)S(1)}, u32[]{:S(2)}, u32[]{:S(2)}) %all-to-all-start.1) | async-done | bytes 16416 | tf_op jit(solution)/shard_map/all_to_all | solution.py:374
  74.5 0.9 %shard_map.93 = (f32[32,512]{1,0:T(8,128)}, f32[32,512]{1,0:T(8,128)}, f32[1,1024]{1,0:T(1,128)}) custom-call(f32[32,128]{1,0:T(8,128)S(1)} %bitcast.8, f32[32,512]{1,0:T(8,128)S(1)} %copy-done.2, f32[32,512]{1,0:T(8,128)S(1)} %get-tuple-element.27.before.v1, f32[32,512]{1,0:T(8,128)S(1)} %get-tuple-element.31.before.v2, ...), custom_call_target="tpu_custom_call" | custom-call | tf_op jit(solution)/shard_map/pallas_call | solution.py:23
  (28 shorter events, 0.1 us)
Async XLA Ops:
  0.6 21.7 %copy-start.2 = (f32[32,512]{1,0:T(8,128)S(1)}, f32[32,512]{1,0:T(8,128)}, u32[]{:S(2)}) copy-start(f32[32,512]{1,0:T(8,128)} %v0.1) | copy-start | bytes 196612
  0.6 21.7 %copy-start.1 = (f32[32,512]{1,0:T(8,128)S(1)}, f32[32,512]{1,0:T(8,128)}, u32[]{:S(2)}) copy-start(f32[32,512]{1,0:T(8,128)} %diagonal.5) | copy-start | bytes 196612
  4.1 18.2 %copy-start.6 = (f32[1,128]{1,0:T(1,128)S(1)}, f32[1,128]{1,0:T(1,128)}, u32[]{:S(2)}) copy-start(f32[1,128]{1,0:T(1,128)} %get-tuple-element.24.moments) | copy-start | bytes 1540
  4.1 11.5 %collective-permute-start.1 = (f32[32,128]{1,0:T(8,128)}, f32[32,128]{1,0:T(8,128)S(1)}, u32[]{:S(2)}, u32[]{:S(2)}) collective-permute-start(f32[32,128]{1,0:T(8,128)} %get-tuple-element.21.block), channel_id=1, source_target_pairs={{8,16},{24,32},{40,48},{56,64},{72,80},{88,96},{104,112},{120,128}... | collective-permute-start | bytes 49160 | tf_op jit(solution)/shard_map/ppermute | solution.py:321
  12.8 2.8 %collective-permute-start = (f32[32,128]{1,0:T(8,128)}, f32[32,128]{1,0:T(8,128)S(1)}, u32[]{:S(2)}, u32[]{:S(2)}) collective-permute-start(f32[32,128]{1,0:T(8,128)} %get-tuple-element.21.block), channel_id=1, source_target_pairs={{0,8},{16,24},{32,40},{48,56},{64,72},{80,88},{96,104},{112,120},{... | collective-permute-start | bytes 49160 | tf_op jit(solution)/shard_map/ppermute | solution.py:321
  12.9 0.7 copy-start.4
  15.6 6.7 %collective-permute-start.3 = (f32[96,128]{1,0:T(8,128)S(1)}, f32[96,128]{1,0:T(8,128)S(1)}, u32[]{:S(2)}, u32[]{:S(2)}) collective-permute-start(f32[96,128]{1,0:T(8,128)S(1)} %constant_dynamic-update-slice_fusion.column), channel_id=1, source_target_pairs={{1,2},{3,4},{5,6},{7,0},{2,1},{4,3},{6,5},{0,7},{9,10},{11,12},{13... | collective-permute-start | bytes 147464 | tf_op jit(solution)/shard_map/ppermute | solution.py:323
  19.0 3.3 %collective-permute-start.2 = (f32[96,128]{1,0:T(8,128)S(1)}, f32[96,128]{1,0:T(8,128)S(1)}, u32[]{:S(2)}, u32[]{:S(2)}) collective-permute-start(f32[96,128]{1,0:T(8,128)S(1)} %constant_dynamic-update-slice_fusion.column), channel_id=1, source_target_pairs={{0,1},{2,3},{4,5},{6,7},{1,0},{3,2},{5,4},{7,6},{8,9},{10,11},{12,... | collective-permute-start | bytes 147464 | tf_op jit(solution)/shard_map/ppermute | solution.py:323
  19.0 2.2 %copy-start = (f32[32,64,512]{2,1,0:T(8,128)S(1)}, f32[32,64,512]{2,1,0:T(8,128)}, u32[]{:S(2)}) copy-start(f32[32,64,512]{2,1,0:T(8,128)} %features.9) | copy-start | bytes 12582916
  25.1 6.0 %collective-permute-start.4 = (f32[32,128]{1,0:T(8,128)S(1)}, f32[32,128]{1,0:T(8,128)S(1)}, u32[]{:S(2)}, u32[]{:S(2)}) collective-permute-start(f32[32,128]{1,0:T(8,128)S(1)} %get-tuple-element.25), channel_id=1, source_target_pairs={{8,16},{24,32},{40,48},{56,64},{72,80},{88,96},{104,112},{120,128}... | collective-permute-start | bytes 49160 | tf_op jit(solution)/shard_map/ppermute | solution.py:321
  28.2 2.9 %collective-permute-start.5 = (f32[32,128]{1,0:T(8,128)S(1)}, f32[32,128]{1,0:T(8,128)S(1)}, u32[]{:S(2)}, u32[]{:S(2)}) collective-permute-start(f32[32,128]{1,0:T(8,128)S(1)} %get-tuple-element.25), channel_id=1, source_target_pairs={{0,8},{16,24},{32,40},{48,56},{64,72},{80,88},{96,104},{112,120},{... | collective-permute-start | bytes 49160 | tf_op jit(solution)/shard_map/ppermute | solution.py:321
  31.0 4.7 %collective-permute-start.7 = (f32[96,128]{1,0:T(8,128)S(1)}, f32[96,128]{1,0:T(8,128)S(1)}, u32[]{:S(2)}, u32[]{:S(2)}) collective-permute-start(f32[96,128]{1,0:T(8,128)S(1)} %constant_dynamic-update-slice_fusion.3.column), channel_id=1, source_target_pairs={{1,2},{3,4},{5,6},{7,0},{2,1},{4,3},{6,5},{0,7},{9,10},{11,12},{13... | collective-permute-start | bytes 147464 | tf_op jit(solution)/shard_map/ppermute | solution.py:323
  34.0 1.8 %collective-permute-start.6 = (f32[96,128]{1,0:T(8,128)S(1)}, f32[96,128]{1,0:T(8,128)S(1)}, u32[]{:S(2)}, u32[]{:S(2)}) collective-permute-start(f32[96,128]{1,0:T(8,128)S(1)} %constant_dynamic-update-slice_fusion.3.column), channel_id=1, source_target_pairs={{0,1},{2,3},{4,5},{6,7},{1,0},{3,2},{5,4},{7,6},{8,9},{10,11},{12,... | collective-permute-start | bytes 147464 | tf_op jit(solution)/shard_map/ppermute | solution.py:323
  35.7 30.2 %copy-start.3 = (f32[64,1024]{1,0:T(8,128)S(1)}, f32[64,1024]{1,0:T(8,128)}, u32[]{:S(2)}) copy-start(f32[64,1024]{1,0:T(8,128)} %vertex_features.1) | copy-start | bytes 786436
  35.7 30.2 %copy-start.5 = (s32[1024]{0:T(1024)S(1)}, s32[1024]{0:T(1024)}, u32[]{:S(2)}) copy-start(s32[1024]{0:T(1024)} %param.11) | copy-start | bytes 12292
  37.1 6.0 %collective-permute-start.8 = (f32[32,128]{1,0:T(8,128)S(1)}, f32[32,128]{1,0:T(8,128)S(1)}, u32[]{:S(2)}, u32[]{:S(2)}) collective-permute-start(f32[32,128]{1,0:T(8,128)S(1)} %get-tuple-element.30), channel_id=1, source_target_pairs={{8,16},{24,32},{40,48},{56,64},{72,80},{88,96},{104,112},{120,128}... | collective-permute-start | bytes 49160 | tf_op jit(solution)/shard_map/ppermute | solution.py:321
  40.1 3.0 %collective-permute-start.9 = (f32[32,128]{1,0:T(8,128)S(1)}, f32[32,128]{1,0:T(8,128)S(1)}, u32[]{:S(2)}, u32[]{:S(2)}) collective-permute-start(f32[32,128]{1,0:T(8,128)S(1)} %get-tuple-element.30), channel_id=1, source_target_pairs={{0,8},{16,24},{32,40},{48,56},{64,72},{80,88},{96,104},{112,120},{... | collective-permute-start | bytes 49160 | tf_op jit(solution)/shard_map/ppermute | solution.py:321
  43.1 4.8 %collective-permute-start.11 = (f32[96,128]{1,0:T(8,128)S(1)}, f32[96,128]{1,0:T(8,128)S(1)}, u32[]{:S(2)}, u32[]{:S(2)}) collective-permute-start(f32[96,128]{1,0:T(8,128)S(1)} %constant_dynamic-update-slice_fusion.6.column), channel_id=1, source_target_pairs={{1,2},{3,4},{5,6},{7,0},{2,1},{4,3},{6,5},{0,7},{9,10},{11,12},{13... | collective-permute-start | bytes 147464 | tf_op jit(solution)/shard_map/ppermute | solution.py:323
  46.0 1.8 %collective-permute-start.10 = (f32[96,128]{1,0:T(8,128)S(1)}, f32[96,128]{1,0:T(8,128)S(1)}, u32[]{:S(2)}, u32[]{:S(2)}) collective-permute-start(f32[96,128]{1,0:T(8,128)S(1)} %constant_dynamic-update-slice_fusion.6.column), channel_id=1, source_target_pairs={{0,1},{2,3},{4,5},{6,7},{1,0},{3,2},{5,4},{7,6},{8,9},{10,11},{12,... | collective-permute-start | bytes 147464 | tf_op jit(solution)/shard_map/ppermute | solution.py:323
  61.3 13.1 %all-to-all-start.1 = ((f32[32,1,128]{2,1,0:T(1,128)}), f32[32,1,128]{2,1,0:T(1,128)S(1)}, u32[]{:S(2)}, u32[]{:S(2)}) async-start(f32[32,1,128]{2,1,0:T(1,128)} %bitcast.3), calls=%async_computation.1 | async-start | bytes 32768 | tf_op jit(solution)/shard_map/all_to_all | solution.py:374

commit v10 on v9

--- a/solution.py
+++ b/solution.py
@@ -11,9 +11,10 @@
 SHIFT = 1.25
 LANES = 128
 MOMENTS = 2 * ITERS
-CHUNKS = 16
+CHUNKS = 8
 MOMENT_LANE = 96
 FIRST_LIMIT = 60
+LIMIT = 47
 VMEM = pl.BlockSpec(memory_space=pltpu.VMEM)
 F32, BF16 = jnp.float32, jnp.bfloat16
 
@@ -69,7 +70,7 @@
     return square.T[:nrows]
 
 
-def first_kernel(features, field, neighbours, block, moments, values, ids, buffer, sems):
+def first_kernel(features, field, neighbours, block, values, ids, buffer, sems):
     nrows, width, _ = features.shape
     each = nrows // CHUNKS
     copies = [
@@ -86,8 +87,6 @@
         copy.start()
     for copy in small:
         copy.wait()
-    value = values[...]
-    moments[...] = put(jnp.zeros((1, LANES), F32), MOMENT_LANE, total(value * value))
     columns = jnp.zeros((width, LANES), F32)
     for i, copy in enumerate(copies):
         copy.wait()
@@ -131,7 +130,7 @@
     own[...] = one_hot(place, 0, 3 * LANES, width, slots)
 
 
-def middle_kernel(shape, index, column, own, features, twice):
+def middle_kernel(shape, index, column, own, twice):
     nrows, width, slots, across = shape
     others = jnp.concatenate([column[2 * nrows :, :], column[:nrows, :]], axis=0)
     place = positions(others, nrows, across, index[0], index[1])
@@ -149,7 +148,7 @@
     twice[...] = jnp.concatenate(parts, axis=1)
 
 
-def advance(step, nrows, width, weights, around, features, diagonal, before, sums, moments, outs):
+def advance(step, nrows, width, weights, around, features, diagonal, before, sums, moments, outs, copies=()):
     last = step + 1 == ITERS
     parts = []
     rest = around
@@ -166,10 +165,11 @@
     moved = pltpu.roll(turned, shift, 1) if shift else turned
     sums = jnp.where((lanes >= shift) & (lanes < shift + nrows), moved, sums)
     old = before[...]
-    images = [
-        jnp.sum(features[b] * turned[:, nrows + b : nrows + b + 1], axis=0, keepdims=True)
-        for b in range(nrows)
-    ]
+    images = []
+    for b in range(nrows):
+        if copies and b % (nrows // len(copies)) == 0:
+            copies[b * len(copies) // nrows].wait()
+        images.append(jnp.sum(features[b] * turned[:, nrows + b : nrows + b + 1], axis=0, keepdims=True))
     new = (diagonal[...] - SHIFT) * old + jnp.concatenate(images, axis=0)
     outs[0][...] = new
     columns = jnp.zeros((width, LANES), F32)
@@ -183,10 +183,19 @@
 
 
 def second_kernel(
-    shape, index, left, column, right, own, known, features, diagonal, before, moments,
-    new, block, sums_out, moments_out, weights_out,
+    shape, index, left, column, right, own, known, far_features, diagonal, before,
+    new, block, sums_out, moments_out, weights_out, features, sems,
 ):
     nrows, width, slots, across = shape
+    each = nrows // CHUNKS
+    copies = [
+        pltpu.make_async_copy(
+            far_features.at[pl.ds(i * each, each)], features.at[pl.ds(i * each, each)], sems.at[i]
+        )
+        for i in range(CHUNKS)
+    ]
+    for copy in copies:
+        copy.start()
     mine = own[...]
     left, column, right = (turned_slots(side) for side in (left, column, right))
     thirds = [third_of(known, d) for d in range(3)]
@@ -199,9 +208,10 @@
     weights = jnp.concatenate([mine, twice, pad], axis=0)
     weights_out[...] = weights
     around = jnp.concatenate([padded(side) for side in (left, column, right)], axis=0)
+    first = put(jnp.zeros((1, LANES), F32), MOMENT_LANE, total(before[...] * before[...]))
     sums, moment, columns = advance(
         0, nrows, width, weights, around, features, diagonal, before,
-        jnp.zeros((width, LANES), F32), moments[...], [new],
+        jnp.zeros((width, LANES), F32), first, [new], copies,
     )
     block[...] = to_rows(columns, nrows)
     sums_out[...] = sums
@@ -334,8 +344,8 @@
     power = f32(nrows, voxels)
     block_shape, row, table = f32(nrows, LANES), f32(1, LANES), f32(width, LANES)
 
-    block, moments = call(
-        first_kernel, [block_shape, row], features, right_side, neighbours,
+    block = call(
+        first_kernel, block_shape, features, right_side, neighbours,
         specs=[hbm] * 3, limit=FIRST_LIMIT,
         scratch=[
             pltpu.VMEM(right_side.shape, F32),
@@ -352,13 +362,17 @@
     left, column, right = neighbourhood(block, copy)
     known = call(
         functools.partial(middle_kernel, shape), f32(nrows, 3 * LANES),
-        index, column, own, features, specs=[smem, VMEM, VMEM, VMEM],
-    )
-    v1, block, sums, moments, weights = call(
+        index, column, own, specs=[smem, VMEM, VMEM],
+    )
+    v1, block, sums, moments, weights, features = call(
         functools.partial(second_kernel, shape),
-        [power, block_shape, table, row, jax.ShapeDtypeStruct((LANES, 3 * LANES), BF16)],
-        index, left, column, right, own, known, features, diagonal, right_side, moments,
-        specs=[smem] + [VMEM] * 9,
+        [
+            power, block_shape, table, row, jax.ShapeDtypeStruct((LANES, 3 * LANES), BF16),
+            f32(*features.shape),
+        ],
+        index, left, column, right, own, known, features, diagonal, right_side,
+        specs=[smem] + [VMEM] * 5 + [hbm] + [VMEM] * 2, limit=LIMIT,
+        scratch=[pltpu.SemaphoreType.DMA((CHUNKS,))],
     )
     left, column, right = neighbourhood(block)
     v2, block, sums, moments = call(

time: 75.7 us -> 76.5 us (1.011)
  local copies, waits for them, and re-layouts: 2.98 us -> 0.79 us
  starting transfers between devices: 28.8 us -> 30.1 us
  Pallas kernels: 13.1 us -> 14.2 us
    unnamed x20 -> x16, local copies, waits for them, and re-layouts: 2.97 us -> 0.77 us
    ppermute x3, starting transfers between devices: 0.13 us -> 1.47 us  [neighbourhood(): lax.ppermute(column, 'gy', swaps('gy', 0))]
    pallas_call x9, Pallas kernels: 13.1 us -> 14.2 us  [call(): pl.pallas_call(kernel, out_shape=out_shape, in_specs=specs or [VMEM] * le...]
    all_to_all x1, blocking collectives: 11.9 us -> 12.6 us  [per_device(): slab = lax.all_to_all(sums, 'gy', 0, 0, tiled=True)]
  transfers between devices with their start and end apart: 13 -> 13, of which waited for: 6 -> 8; matrix products, arithmetic and copies ran while one was open for 0% -> 0% of each run, Pallas kernels for 4% -> 4%
where the time goes in v10:
time: 76.5 us; the launch traced here: 76.2 us
  starting transfers between devices  30.1 us (39%)
  waiting for transfers between devices  17.7 us (23%)
  Pallas kernels  14.2 us (19%)
  blocking collectives  12.6 us (16%)
  local copies, waits for them, and re-layouts  0.79 us (1%)
    ppermute x3, starting transfers between devices, neighbourhood(): lax.ppermute(block, 'gx', swaps('gx', 1))  14.7 us
    pallas_call x9, Pallas kernels, call(): pl.pallas_call(kernel, out_shape=out_shape, in_specs=specs or [VMEM] * le...  14.2 us
    all_to_all x1, blocking collectives, per_device(): slab = lax.all_to_all(sums, 'gy', 0, 0, tiled=True)  12.6 us
    ppermute x3, starting transfers between devices, neighbourhood(): lax.ppermute(column, 'gy', swaps('gy', 1))  9.33 us
    all_to_all x1, waiting for transfers between devices, per_device(): lax.all_to_all(call(fold_kernel, f32(along, LANES), slab), 'gx', 0, 0, ti...  7.3 us
    ppermute x3, waiting for transfers between devices, neighbourhood(): lax.ppermute(block, 'gx', swaps('gx', 1))  5.95 us
    all_to_all x1, starting transfers between devices, per_device(): lax.all_to_all(call(fold_kernel, f32(along, LANES), slab), 'gx', 0, 0, ti...  4.6 us
    ppermute x3, waiting for transfers between devices, neighbourhood(): lax.ppermute(column, 'gy', swaps('gy', 1))  2.76 us
  transfers between devices with their start and end apart: 13, of which 8 were waited for; matrix products, arithmetic and copies ran while one was open for 0% of the time, Pallas kernels for 4%

profile of v10, /device:TPU:1, one launch (start us, length us, event | category | flops | bytes accessed | tf_op | source)
XLA Modules:
  0.0 76.2 jit_solution(6846406237409855864)
XLA Ops:
  0.7 3.1 %shard_map.85.block = f32[32,128]{1,0:T(8,128)} custom-call(f32[32,64,512]{2,1,0:T(8,128)} %far_features.1, f32[32,512]{1,0:T(8,128)} %v0.1, s32[32,27]{1,0:T(8,128)} %neighbours.1), custom_call_target="tpu_custom_call" | custom-call | tf_op jit(solution)/shard_map/pallas_call | solution.py:24
  3.8 8.7 %collective-permute-start.1 = (f32[32,128]{1,0:T(8,128)}, f32[32,128]{1,0:T(8,128)S(1)}, u32[]{:S(2)}, u32[]{:S(2)}) collective-permute-start(f32[32,128]{1,0:T(8,128)} %shard_map.85.block), channel_id=1, source_target_pairs={{8,16},{24,32},{40,48},{56,64},{72,80},{88,96},{104,112},{120,128}... | collective-permute-start | bytes 49160 | tf_op jit(solution)/shard_map/ppermute | solution.py:331
  12.5 0.1 pad_add_fusion.index
  12.5 0.7 copy-done.3
  13.3 0.8 %shard_map.86 = (bf16[32,384]{1,0:T(8,128)(2,1)S(1)}, f32[32,128]{1,0:T(8,128)S(1)}) custom-call(s32[2]{0:T(128)S(1)} %pad_add_fusion.index, f32[32,128]{1,0:T(8,128)S(1)} %copy-done.3), custom_call_target="tpu_custom_call" | custom-call | tf_op jit(solution)/shard_map/pallas_call | solution.py:24
  14.1 1.2 %collective-permute-done = f32[32,128]{1,0:T(8,128)S(1)} collective-permute-done((f32[32,128]{1,0:T(8,128)}, f32[32,128]{1,0:T(8,128)S(1)}, u32[]{:S(2)}, u32[]{:S(2)}) %collective-permute-start) | collective-permute-done | bytes 16416 | tf_op jit(solution)/shard_map/ppermute | solution.py:331
  15.3 0.0 collective-permute-done.1
  15.3 3.4 %collective-permute-start.3 = (f32[96,128]{1,0:T(8,128)S(1)}, f32[96,128]{1,0:T(8,128)S(1)}, u32[]{:S(2)}, u32[]{:S(2)}) collective-permute-start(f32[96,128]{1,0:T(8,128)S(1)} %constant_dynamic-update-slice_fusion.column), channel_id=1, source_target_pairs={{1,2},{3,4},{5,6},{7,0},{2,1},{4,3},{6,5},{0,7},{9,10},{11,12},{13... | collective-permute-start | bytes 147464 | tf_op jit(solution)/shard_map/ppermute | solution.py:333
  18.7 0.0 collective-permute-start.2
  18.7 1.1 %shard_map.87.known = f32[32,384]{1,0:T(8,128)S(1)} custom-call(s32[2]{0:T(128)S(1)} %pad_add_fusion.index, f32[96,128]{1,0:T(8,128)S(1)} %constant_dynamic-update-slice_fusion.column, bf16[32,384]{1,0:T(8,128)(2,1)S(1)} %get-tuple-element.21.own), custom_call_target="tpu_custom_call" | custom-call | tf_op jit(solution)/shard_map/pallas_call | solution.py:24
  19.8 0.7 collective-permute-done.3.right
  20.4 0.0 collective-permute-done.2.left
  20.4 4.2 %shard_map.88 = (f32[32,512]{1,0:T(8,128)S(1)}, f32[32,128]{1,0:T(8,128)S(1)}, f32[64,128]{1,0:T(8,128)S(1)}, f32[1,128]{1,0:T(1,128)S(1)}, bf16[128,384]{1,0:T(8,128)(2,1)S(1)}, /*index=5*/f32[32,64,512]{2,1,0:T(8,128)S(1)}) custom-call(s32[2]{0:T(128)S(1)} %pad_add_fusion.index, f32[96,128]{1,0:T(8,128)S(1)} %collective-permute-done.2.left, ...), custom_call_target="tpu_custom_call" | custom-call | tf_op jit(solution)/shard_map/pallas_call | solution.py:24
  24.6 3.0 %collective-permute-start.4 = (f32[32,128]{1,0:T(8,128)S(1)}, f32[32,128]{1,0:T(8,128)S(1)}, u32[]{:S(2)}, u32[]{:S(2)}) collective-permute-start(f32[32,128]{1,0:T(8,128)S(1)} %get-tuple-element.22), channel_id=1, source_target_pairs={{8,16},{24,32},{40,48},{56,64},{72,80},{88,96},{104,112},{120,128}... | collective-permute-start | bytes 49160 | tf_op jit(solution)/shard_map/ppermute | solution.py:331
  27.6 3.0 %collective-permute-done.4 = f32[32,128]{1,0:T(8,128)S(1)} collective-permute-done((f32[32,128]{1,0:T(8,128)S(1)}, f32[32,128]{1,0:T(8,128)S(1)}, u32[]{:S(2)}, u32[]{:S(2)}) %collective-permute-start.4) | collective-permute-done | bytes 16416 | tf_op jit(solution)/shard_map/ppermute | solution.py:331
  30.6 3.0 %collective-permute-start.7 = (f32[96,128]{1,0:T(8,128)S(1)}, f32[96,128]{1,0:T(8,128)S(1)}, u32[]{:S(2)}, u32[]{:S(2)}) collective-permute-start(f32[96,128]{1,0:T(8,128)S(1)} %constant_dynamic-update-slice_fusion.3.column), channel_id=1, source_target_pairs={{1,2},{3,4},{5,6},{7,0},{2,1},{4,3},{6,5},{0,7},{9,10},{11,12},{13... | collective-permute-start | bytes 147464 | tf_op jit(solution)/shard_map/ppermute | solution.py:333
  33.6 0.1 collective-permute-start.6
  33.7 1.6 %collective-permute-done.7.right = f32[96,128]{1,0:T(8,128)S(1)} collective-permute-done((f32[96,128]{1,0:T(8,128)S(1)}, f32[96,128]{1,0:T(8,128)S(1)}, u32[]{:S(2)}, u32[]{:S(2)}) %collective-permute-start.7) | collective-permute-done | bytes 49184 | tf_op jit(solution)/shard_map/ppermute | solution.py:333
  35.4 1.3 %shard_map.89 = (f32[32,512]{1,0:T(8,128)S(1)}, f32[32,128]{1,0:T(8,128)S(1)}, f32[64,128]{1,0:T(8,128)S(1)}, f32[1,128]{1,0:T(1,128)S(1)}) custom-call(f32[96,128]{1,0:T(8,128)S(1)} %collective-permute-done.6.left, f32[96,128]{1,0:T(8,128)S(1)} %constant_dynamic-update-slice_fusion.3.column, f32[96,128]{1,0:T(8,128)S(1)} %collective-permute-done.7.right, ...), custom_call_target="tpu_custom_call" | custom-call | tf_op jit(solution)/shard_map/pallas_call | solution.py:24
  36.7 3.0 %collective-permute-start.8 = (f32[32,128]{1,0:T(8,128)S(1)}, f32[32,128]{1,0:T(8,128)S(1)}, u32[]{:S(2)}, u32[]{:S(2)}) collective-permute-start(f32[32,128]{1,0:T(8,128)S(1)} %get-tuple-element.28), channel_id=1, source_target_pairs={{8,16},{24,32},{40,48},{56,64},{72,80},{88,96},{104,112},{120,128}... | collective-permute-start | bytes 49160 | tf_op jit(solution)/shard_map/ppermute | solution.py:331
  39.7 3.0 %collective-permute-done.8 = f32[32,128]{1,0:T(8,128)S(1)} collective-permute-done((f32[32,128]{1,0:T(8,128)S(1)}, f32[32,128]{1,0:T(8,128)S(1)}, u32[]{:S(2)}, u32[]{:S(2)}) %collective-permute-start.8) | collective-permute-done | bytes 16416 | tf_op jit(solution)/shard_map/ppermute | solution.py:331
  42.7 3.0 %collective-permute-start.11 = (f32[96,128]{1,0:T(8,128)S(1)}, f32[96,128]{1,0:T(8,128)S(1)}, u32[]{:S(2)}, u32[]{:S(2)}) collective-permute-start(f32[96,128]{1,0:T(8,128)S(1)} %constant_dynamic-update-slice_fusion.6.column), channel_id=1, source_target_pairs={{1,2},{3,4},{5,6},{7,0},{2,1},{4,3},{6,5},{0,7},{9,10},{11,12},{13... | collective-permute-start | bytes 147464 | tf_op jit(solution)/shard_map/ppermute | solution.py:333
  45.7 1.3 %collective-permute-start.10 = (f32[96,128]{1,0:T(8,128)S(1)}, f32[96,128]{1,0:T(8,128)S(1)}, u32[]{:S(2)}, u32[]{:S(2)}) collective-permute-start(f32[96,128]{1,0:T(8,128)S(1)} %constant_dynamic-update-slice_fusion.6.column), channel_id=1, source_target_pairs={{0,1},{2,3},{4,5},{6,7},{1,0},{3,2},{5,4},{7,6},{8,9},{10,11},{12,... | collective-permute-start | bytes 147464 | tf_op jit(solution)/shard_map/ppermute | solution.py:333
  47.0 0.4 collective-permute-done.11.right
  47.5 0.4 collective-permute-done.10.left
  47.9 1.0 %shard_map.90 = (f32[32,512]{1,0:T(8,128)S(1)}, f32[8,64,128]{2,1,0:T(8,128)S(1)}) custom-call(f32[96,128]{1,0:T(8,128)S(1)} %collective-permute-done.10.left, f32[96,128]{1,0:T(8,128)S(1)} %constant_dynamic-update-slice_fusion.6.column, f32[96,128]{1,0:T(8,128)S(1)} %collective-permute-done.11.right, bf16[128,384]{1,0:T(8,128)(2,1)S(1)} %get-tuple-element.23.weights, ...), custom_call_target="tpu_custom_call" | custom-call | tf_op jit(solution)/shard_map/pallas_call | solution.py:24
  48.9 12.6 %all_to_all.16.slab = f32[8,64,128]{2,1,0:T(8,128)S(1)} all-to-all(f32[8,64,128]{2,1,0:T(8,128)S(1)} %get-tuple-element.32), channel_id=1, replica_groups=mesh['gx'=32,'gy'=8] {'gy'}, dimensions={0} | all-to-all | bytes 524288 | tf_op jit(solution)/shard_map/all_to_all | solution.py:387
  61.6 0.6 shard_map.91
  62.2 4.6 %all-to-all-start.1 = ((f32[32,1,128]{2,1,0:T(1,128)}), f32[32,1,128]{2,1,0:T(1,128)S(1)}, u32[]{:S(2)}, u32[]{:S(2)}) async-start(f32[32,1,128]{2,1,0:T(1,128)} %bitcast.3), calls=%async_computation.1 | async-start | bytes 32768 | tf_op jit(solution)/shard_map/all_to_all | solution.py:388
  66.8 1.2 %shard_map.92.vertices = f32[8,1024]{1,0:T(8,128)S(1)} custom-call(s32[2]{0:T(128)S(1)} %pad_add_fusion.index, f32[8,64,128]{2,1,0:T(8,128)S(1)} %all_to_all.16.slab, s32[1,1024]{1,0:T(1,128)S(1)} %bitcast.9, f32[64,1024]{1,0:T(8,128)S(1)} %copy-done.2), custom_call_target="tpu_custom_call" | custom-call | tf_op jit(solution)/shard_map/pallas_call | solution.py:24
  68.0 7.3 %all-to-all-done.1 = f32[32,1,128]{2,1,0:T(1,128)S(1)} async-done(((f32[32,1,128]{2,1,0:T(1,128)}), f32[32,1,128]{2,1,0:T(1,128)S(1)}, u32[]{:S(2)}, u32[]{:S(2)}) %all-to-all-start.1) | async-done | bytes 16416 | tf_op jit(solution)/shard_map/all_to_all | solution.py:388
  75.3 0.9 %shard_map.93 = (f32[32,512]{1,0:T(8,128)}, f32[32,512]{1,0:T(8,128)}, f32[1,1024]{1,0:T(1,128)}) custom-call(f32[32,128]{1,0:T(8,128)S(1)} %bitcast.8, f32[32,512]{1,0:T(8,128)S(1)} %copy-done.1, f32[32,512]{1,0:T(8,128)S(1)} %get-tuple-element.25.before.v1, f32[32,512]{1,0:T(8,128)S(1)} %get-tuple-element.29.before.v2, ...), custom_call_target="tpu_custom_call" | custom-call | tf_op jit(solution)/shard_map/pallas_call | solution.py:24
  (24 shorter events, 0.1 us)
Async XLA Ops:
  0.6 19.8 %copy-start.1 = (f32[32,512]{1,0:T(8,128)S(1)}, f32[32,512]{1,0:T(8,128)}, u32[]{:S(2)}) copy-start(f32[32,512]{1,0:T(8,128)} %v0.1) | copy-start | bytes 196612
  0.6 19.8 %copy-start = (f32[32,512]{1,0:T(8,128)S(1)}, f32[32,512]{1,0:T(8,128)}, u32[]{:S(2)}) copy-start(f32[32,512]{1,0:T(8,128)} %diagonal.5) | copy-start | bytes 196612
  3.8 11.5 %collective-permute-start.1 = (f32[32,128]{1,0:T(8,128)}, f32[32,128]{1,0:T(8,128)S(1)}, u32[]{:S(2)}, u32[]{:S(2)}) collective-permute-start(f32[32,128]{1,0:T(8,128)} %shard_map.85.block), channel_id=1, source_target_pairs={{8,16},{24,32},{40,48},{56,64},{72,80},{88,96},{104,112},{120,128}... | collective-permute-start | bytes 49160 | tf_op jit(solution)/shard_map/ppermute | solution.py:331
  12.5 2.8 %collective-permute-start = (f32[32,128]{1,0:T(8,128)}, f32[32,128]{1,0:T(8,128)S(1)}, u32[]{:S(2)}, u32[]{:S(2)}) collective-permute-start(f32[32,128]{1,0:T(8,128)} %shard_map.85.block), channel_id=1, source_target_pairs={{0,8},{16,24},{32,40},{48,56},{64,72},{80,88},{96,104},{112,120},{... | collective-permute-start | bytes 49160 | tf_op jit(solution)/shard_map/ppermute | solution.py:331
  12.5 0.7 copy-start.3
  15.3 5.1 %collective-permute-start.3 = (f32[96,128]{1,0:T(8,128)S(1)}, f32[96,128]{1,0:T(8,128)S(1)}, u32[]{:S(2)}, u32[]{:S(2)}) collective-permute-start(f32[96,128]{1,0:T(8,128)S(1)} %constant_dynamic-update-slice_fusion.column), channel_id=1, source_target_pairs={{1,2},{3,4},{5,6},{7,0},{2,1},{4,3},{6,5},{0,7},{9,10},{11,12},{13... | collective-permute-start | bytes 147464 | tf_op jit(solution)/shard_map/ppermute | solution.py:333
  18.7 1.8 %collective-permute-start.2 = (f32[96,128]{1,0:T(8,128)S(1)}, f32[96,128]{1,0:T(8,128)S(1)}, u32[]{:S(2)}, u32[]{:S(2)}) collective-permute-start(f32[96,128]{1,0:T(8,128)S(1)} %constant_dynamic-update-slice_fusion.column), channel_id=1, source_target_pairs={{0,1},{2,3},{4,5},{6,7},{1,0},{3,2},{5,4},{7,6},{8,9},{10,11},{12,... | collective-permute-start | bytes 147464 | tf_op jit(solution)/shard_map/ppermute | solution.py:333
  24.6 6.0 %collective-permute-start.4 = (f32[32,128]{1,0:T(8,128)S(1)}, f32[32,128]{1,0:T(8,128)S(1)}, u32[]{:S(2)}, u32[]{:S(2)}) collective-permute-start(f32[32,128]{1,0:T(8,128)S(1)} %get-tuple-element.22), channel_id=1, source_target_pairs={{8,16},{24,32},{40,48},{56,64},{72,80},{88,96},{104,112},{120,128}... | collective-permute-start | bytes 49160 | tf_op jit(solution)/shard_map/ppermute | solution.py:331
  27.6 3.0 %collective-permute-start.5 = (f32[32,128]{1,0:T(8,128)S(1)}, f32[32,128]{1,0:T(8,128)S(1)}, u32[]{:S(2)}, u32[]{:S(2)}) collective-permute-start(f32[32,128]{1,0:T(8,128)S(1)} %get-tuple-element.22), channel_id=1, source_target_pairs={{0,8},{16,24},{32,40},{48,56},{64,72},{80,88},{96,104},{112,120},{... | collective-permute-start | bytes 49160 | tf_op jit(solution)/shard_map/ppermute | solution.py:331
  30.6 4.8 %collective-permute-start.7 = (f32[96,128]{1,0:T(8,128)S(1)}, f32[96,128]{1,0:T(8,128)S(1)}, u32[]{:S(2)}, u32[]{:S(2)}) collective-permute-start(f32[96,128]{1,0:T(8,128)S(1)} %constant_dynamic-update-slice_fusion.3.column), channel_id=1, source_target_pairs={{1,2},{3,4},{5,6},{7,0},{2,1},{4,3},{6,5},{0,7},{9,10},{11,12},{13... | collective-permute-start | bytes 147464 | tf_op jit(solution)/shard_map/ppermute | solution.py:333
  33.6 1.8 %collective-permute-start.6 = (f32[96,128]{1,0:T(8,128)S(1)}, f32[96,128]{1,0:T(8,128)S(1)}, u32[]{:S(2)}, u32[]{:S(2)}) collective-permute-start(f32[96,128]{1,0:T(8,128)S(1)} %constant_dynamic-update-slice_fusion.3.column), channel_id=1, source_target_pairs={{0,1},{2,3},{4,5},{6,7},{1,0},{3,2},{5,4},{7,6},{8,9},{10,11},{12,... | collective-permute-start | bytes 147464 | tf_op jit(solution)/shard_map/ppermute | solution.py:333
  35.4 31.4 %copy-start.2 = (f32[64,1024]{1,0:T(8,128)S(1)}, f32[64,1024]{1,0:T(8,128)}, u32[]{:S(2)}) copy-start(f32[64,1024]{1,0:T(8,128)} %vertex_features.1) | copy-start | bytes 786436
  35.4 31.4 %copy-start.4 = (s32[1024]{0:T(1024)S(1)}, s32[1024]{0:T(1024)}, u32[]{:S(2)}) copy-start(s32[1024]{0:T(1024)} %param.11) | copy-start | bytes 12292
  36.7 6.0 %collective-permute-start.8 = (f32[32,128]{1,0:T(8,128)S(1)}, f32[32,128]{1,0:T(8,128)S(1)}, u32[]{:S(2)}, u32[]{:S(2)}) collective-permute-start(f32[32,128]{1,0:T(8,128)S(1)} %get-tuple-element.28), channel_id=1, source_target_pairs={{8,16},{24,32},{40,48},{56,64},{72,80},{88,96},{104,112},{120,128}... | collective-permute-start | bytes 49160 | tf_op jit(solution)/shard_map/ppermute | solution.py:331
  39.7 3.0 %collective-permute-start.9 = (f32[32,128]{1,0:T(8,128)S(1)}, f32[32,128]{1,0:T(8,128)S(1)}, u32[]{:S(2)}, u32[]{:S(2)}) collective-permute-start(f32[32,128]{1,0:T(8,128)S(1)} %get-tuple-element.28), channel_id=1, source_target_pairs={{0,8},{16,24},{32,40},{48,56},{64,72},{80,88},{96,104},{112,120},{... | collective-permute-start | bytes 49160 | tf_op jit(solution)/shard_map/ppermute | solution.py:331
  42.7 4.8 %collective-permute-start.11 = (f32[96,128]{1,0:T(8,128)S(1)}, f32[96,128]{1,0:T(8,128)S(1)}, u32[]{:S(2)}, u32[]{:S(2)}) collective-permute-start(f32[96,128]{1,0:T(8,128)S(1)} %constant_dynamic-update-slice_fusion.6.column), channel_id=1, source_target_pairs={{1,2},{3,4},{5,6},{7,0},{2,1},{4,3},{6,5},{0,7},{9,10},{11,12},{13... | collective-permute-start | bytes 147464 | tf_op jit(solution)/shard_map/ppermute | solution.py:333
  45.7 2.2 %collective-permute-start.10 = (f32[96,128]{1,0:T(8,128)S(1)}, f32[96,128]{1,0:T(8,128)S(1)}, u32[]{:S(2)}, u32[]{:S(2)}) collective-permute-start(f32[96,128]{1,0:T(8,128)S(1)} %constant_dynamic-update-slice_fusion.6.column), channel_id=1, source_target_pairs={{0,1},{2,3},{4,5},{6,7},{1,0},{3,2},{5,4},{7,6},{8,9},{10,11},{12,... | collective-permute-start | bytes 147464 | tf_op jit(solution)/shard_map/ppermute | solution.py:333
  62.2 13.1 %all-to-all-start.1 = ((f32[32,1,128]{2,1,0:T(1,128)}), f32[32,1,128]{2,1,0:T(1,128)S(1)}, u32[]{:S(2)}, u32[]{:S(2)}) async-start(f32[32,1,128]{2,1,0:T(1,128)} %bitcast.3), calls=%async_computation.1 | async-start | bytes 32768 | tf_op jit(solution)/shard_map/all_to_all | solution.py:388

commit v11 on v9

--- a/solution.py
+++ b/solution.py
@@ -11,7 +11,7 @@
 SHIFT = 1.25
 LANES = 128
 MOMENTS = 2 * ITERS
-CHUNKS = 16
+CHUNKS = 8
 MOMENT_LANE = 96
 FIRST_LIMIT = 60
 VMEM = pl.BlockSpec(memory_space=pltpu.VMEM)

time: 75.7 us -> 75.4 us (level)
  no operation moved by 1% of the time
where the time goes in v11:
time: 75.4 us; the launch traced here: 75.1 us
  starting transfers between devices  28.8 us (38%)
  waiting for transfers between devices  17.8 us (24%)
  Pallas kernels  12.8 us (17%)
  blocking collectives  11.9 us (16%)
  local copies, waits for them, and re-layouts  2.98 us (4%)
  between operations  0.79 us (1%)
    ppermute x3, starting transfers between devices, neighbourhood(): lax.ppermute(block, 'gx', swaps('gx', 1))  14.8 us
    pallas_call x9, Pallas kernels, call(): pl.pallas_call(kernel, out_shape=out_shape, in_specs=specs or [VMEM] * le...  12.8 us
    all_to_all x1, blocking collectives, per_device(): slab = lax.all_to_all(sums, 'gy', 0, 0, tiled=True)  11.9 us
    ppermute x3, starting transfers between devices, neighbourhood(): lax.ppermute(column, 'gy', swaps('gy', 1))  9.27 us
    all_to_all x1, waiting for transfers between devices, per_device(): lax.all_to_all(call(fold_kernel, f32(along, LANES), slab), 'gx', 0, 0, ti...  7.3 us
    ppermute x3, waiting for transfers between devices, neighbourhood(): lax.ppermute(block, 'gx', swaps('gx', 1))  5.83 us
    all_to_all x1, starting transfers between devices, per_device(): lax.all_to_all(call(fold_kernel, f32(along, LANES), slab), 'gx', 0, 0, ti...  4.6 us
    ppermute x3, waiting for transfers between devices, neighbourhood(): lax.ppermute(column, 'gy', swaps('gy', 1))  3.42 us
  transfers between devices with their start and end apart: 13, of which 6 were waited for; matrix products, arithmetic and copies ran while one was open for 0% of the time, Pallas kernels for 4%

profile of v11, /device:TPU:1, one launch (start us, length us, event | category | flops | bytes accessed | tf_op | source)
XLA Modules:
  0.0 75.1 jit_solution(10421154730918075379)
XLA Ops:
  0.7 3.1 %shard_map.85 = (f32[32,128]{1,0:T(8,128)}, f32[1,128]{1,0:T(1,128)}) custom-call(f32[32,64,512]{2,1,0:T(8,128)} %features.9, f32[32,512]{1,0:T(8,128)} %v0.1, s32[32,27]{1,0:T(8,128)} %neighbours.1), custom_call_target="tpu_custom_call" | custom-call | tf_op jit(solution)/shard_map/pallas_call | solution.py:23
  3.8 8.7 %collective-permute-start.1 = (f32[32,128]{1,0:T(8,128)}, f32[32,128]{1,0:T(8,128)S(1)}, u32[]{:S(2)}, u32[]{:S(2)}) collective-permute-start(f32[32,128]{1,0:T(8,128)} %get-tuple-element.21.block), channel_id=1, source_target_pairs={{8,16},{24,32},{40,48},{56,64},{72,80},{88,96},{104,112},{120,128}... | collective-permute-start | bytes 49160 | tf_op jit(solution)/shard_map/ppermute | solution.py:321
  12.5 0.0 collective-permute-start
  12.5 0.1 pad_add_fusion.index
  12.5 0.7 copy-done.4
  13.3 0.8 %shard_map.86 = (bf16[32,384]{1,0:T(8,128)(2,1)S(1)}, f32[32,128]{1,0:T(8,128)S(1)}) custom-call(s32[2]{0:T(128)S(1)} %pad_add_fusion.index, f32[32,128]{1,0:T(8,128)S(1)} %copy-done.4), custom_call_target="tpu_custom_call" | custom-call | tf_op jit(solution)/shard_map/pallas_call | solution.py:23
  14.1 1.2 %collective-permute-done = f32[32,128]{1,0:T(8,128)S(1)} collective-permute-done((f32[32,128]{1,0:T(8,128)}, f32[32,128]{1,0:T(8,128)S(1)}, u32[]{:S(2)}, u32[]{:S(2)}) %collective-permute-start) | collective-permute-done | bytes 16416 | tf_op jit(solution)/shard_map/ppermute | solution.py:321
  15.3 3.4 %collective-permute-start.3 = (f32[96,128]{1,0:T(8,128)S(1)}, f32[96,128]{1,0:T(8,128)S(1)}, u32[]{:S(2)}, u32[]{:S(2)}) collective-permute-start(f32[96,128]{1,0:T(8,128)S(1)} %constant_dynamic-update-slice_fusion.column), channel_id=1, source_target_pairs={{1,2},{3,4},{5,6},{7,0},{2,1},{4,3},{6,5},{0,7},{9,10},{11,12},{13... | collective-permute-start | bytes 147464 | tf_op jit(solution)/shard_map/ppermute | solution.py:323
  18.7 0.0 collective-permute-start.2
  18.7 2.2 %copy-done = f32[32,64,512]{2,1,0:T(8,128)S(1)} copy-done((f32[32,64,512]{2,1,0:T(8,128)S(1)}, f32[32,64,512]{2,1,0:T(8,128)}, u32[]{:S(2)}) %copy-start) | copy-done | bytes 4194328
  20.9 1.1 %shard_map.87.known = f32[32,384]{1,0:T(8,128)S(1)} custom-call(s32[2]{0:T(128)S(1)} %pad_add_fusion.index, f32[96,128]{1,0:T(8,128)S(1)} %constant_dynamic-update-slice_fusion.column, bf16[32,384]{1,0:T(8,128)(2,1)S(1)} %get-tuple-element.23.own, f32[32,64,512]{2,1,0:T(8,128)S(1)} %copy-done), custom_call_target="tpu_custom_call" | custom-call | tf_op jit(solution)/shard_map/pallas_call | solution.py:23
  22.0 0.0 collective-permute-done.2.left
  22.0 2.7 %shard_map.88 = (f32[32,512]{1,0:T(8,128)S(1)}, f32[32,128]{1,0:T(8,128)S(1)}, f32[64,128]{1,0:T(8,128)S(1)}, f32[1,128]{1,0:T(1,128)S(1)}, bf16[128,384]{1,0:T(8,128)(2,1)S(1)}) custom-call(s32[2]{0:T(128)S(1)} %pad_add_fusion.index, f32[96,128]{1,0:T(8,128)S(1)} %collective-permute-done.2.left, f32[96,128]{1,0:T(8,128)S(1)} %constant_dynamic-update-slice_fusion.column, ...), custom_call_target="tpu_custom_call" | custom-call | tf_op jit(solution)/shard_map/pallas_call | solution.py:23
  24.7 3.1 %collective-permute-start.4 = (f32[32,128]{1,0:T(8,128)S(1)}, f32[32,128]{1,0:T(8,128)S(1)}, u32[]{:S(2)}, u32[]{:S(2)}) collective-permute-start(f32[32,128]{1,0:T(8,128)S(1)} %get-tuple-element.25), channel_id=1, source_target_pairs={{8,16},{24,32},{40,48},{56,64},{72,80},{88,96},{104,112},{120,128}... | collective-permute-start | bytes 49160 | tf_op jit(solution)/shard_map/ppermute | solution.py:321
  27.8 0.0 collective-permute-start.5
  27.8 2.9 %collective-permute-done.4 = f32[32,128]{1,0:T(8,128)S(1)} collective-permute-done((f32[32,128]{1,0:T(8,128)S(1)}, f32[32,128]{1,0:T(8,128)S(1)}, u32[]{:S(2)}, u32[]{:S(2)}) %collective-permute-start.4) | collective-permute-done | bytes 16416 | tf_op jit(solution)/shard_map/ppermute | solution.py:321
  30.7 0.0 collective-permute-done.5
  30.7 2.9 %collective-permute-start.7 = (f32[96,128]{1,0:T(8,128)S(1)}, f32[96,128]{1,0:T(8,128)S(1)}, u32[]{:S(2)}, u32[]{:S(2)}) collective-permute-start(f32[96,128]{1,0:T(8,128)S(1)} %constant_dynamic-update-slice_fusion.3.column), channel_id=1, source_target_pairs={{1,2},{3,4},{5,6},{7,0},{2,1},{4,3},{6,5},{0,7},{9,10},{11,12},{13... | collective-permute-start | bytes 147464 | tf_op jit(solution)/shard_map/ppermute | solution.py:323
  33.6 1.8 %collective-permute-done.7.right = f32[96,128]{1,0:T(8,128)S(1)} collective-permute-done((f32[96,128]{1,0:T(8,128)S(1)}, f32[96,128]{1,0:T(8,128)S(1)}, u32[]{:S(2)}, u32[]{:S(2)}) %collective-permute-start.7) | collective-permute-done | bytes 49184 | tf_op jit(solution)/shard_map/ppermute | solution.py:323
  35.4 1.3 %shard_map.89 = (f32[32,512]{1,0:T(8,128)S(1)}, f32[32,128]{1,0:T(8,128)S(1)}, f32[64,128]{1,0:T(8,128)S(1)}, f32[1,128]{1,0:T(1,128)S(1)}) custom-call(f32[96,128]{1,0:T(8,128)S(1)} %collective-permute-done.6.left, f32[96,128]{1,0:T(8,128)S(1)} %constant_dynamic-update-slice_fusion.3.column, f32[96,128]{1,0:T(8,128)S(1)} %collective-permute-done.7.right, ...), custom_call_target="tpu_custom_call" | custom-call | tf_op jit(solution)/shard_map/pallas_call | solution.py:23
  36.8 3.0 %collective-permute-start.8 = (f32[32,128]{1,0:T(8,128)S(1)}, f32[32,128]{1,0:T(8,128)S(1)}, u32[]{:S(2)}, u32[]{:S(2)}) collective-permute-start(f32[32,128]{1,0:T(8,128)S(1)} %get-tuple-element.30), channel_id=1, source_target_pairs={{8,16},{24,32},{40,48},{56,64},{72,80},{88,96},{104,112},{120,128}... | collective-permute-start | bytes 49160 | tf_op jit(solution)/shard_map/ppermute | solution.py:321
  39.7 3.0 %collective-permute-done.8 = f32[32,128]{1,0:T(8,128)S(1)} collective-permute-done((f32[32,128]{1,0:T(8,128)S(1)}, f32[32,128]{1,0:T(8,128)S(1)}, u32[]{:S(2)}, u32[]{:S(2)}) %collective-permute-start.8) | collective-permute-done | bytes 16416 | tf_op jit(solution)/shard_map/ppermute | solution.py:321
  42.7 3.0 %collective-permute-start.11 = (f32[96,128]{1,0:T(8,128)S(1)}, f32[96,128]{1,0:T(8,128)S(1)}, u32[]{:S(2)}, u32[]{:S(2)}) collective-permute-start(f32[96,128]{1,0:T(8,128)S(1)} %constant_dynamic-update-slice_fusion.6.column), channel_id=1, source_target_pairs={{1,2},{3,4},{5,6},{7,0},{2,1},{4,3},{6,5},{0,7},{9,10},{11,12},{13... | collective-permute-start | bytes 147464 | tf_op jit(solution)/shard_map/ppermute | solution.py:323
  45.7 0.1 collective-permute-start.10
  45.8 1.6 %collective-permute-done.11.right = f32[96,128]{1,0:T(8,128)S(1)} collective-permute-done((f32[96,128]{1,0:T(8,128)S(1)}, f32[96,128]{1,0:T(8,128)S(1)}, u32[]{:S(2)}, u32[]{:S(2)}) %collective-permute-start.11) | collective-permute-done | bytes 49184 | tf_op jit(solution)/shard_map/ppermute | solution.py:323
  47.5 1.0 %shard_map.90 = (f32[32,512]{1,0:T(8,128)S(1)}, f32[8,64,128]{2,1,0:T(8,128)S(1)}) custom-call(f32[96,128]{1,0:T(8,128)S(1)} %collective-permute-done.10.left, f32[96,128]{1,0:T(8,128)S(1)} %constant_dynamic-update-slice_fusion.6.column, f32[96,128]{1,0:T(8,128)S(1)} %collective-permute-done.11.right, bf16[128,384]{1,0:T(8,128)(2,1)S(1)} %get-tuple-element.26.weights, ...), custom_call_target="tpu_custom_call" | custom-call | tf_op jit(solution)/shard_map/pallas_call | solution.py:23
  48.5 11.9 %all_to_all.16.slab = f32[8,64,128]{2,1,0:T(8,128)S(1)} all-to-all(f32[8,64,128]{2,1,0:T(8,128)S(1)} %get-tuple-element.34), channel_id=1, replica_groups=mesh['gx'=32,'gy'=8] {'gy'}, dimensions={0} | all-to-all | bytes 524288 | tf_op jit(solution)/shard_map/all_to_all | solution.py:373
  60.4 0.6 shard_map.91
  61.0 4.6 %all-to-all-start.1 = ((f32[32,1,128]{2,1,0:T(1,128)}), f32[32,1,128]{2,1,0:T(1,128)S(1)}, u32[]{:S(2)}, u32[]{:S(2)}) async-start(f32[32,1,128]{2,1,0:T(1,128)} %bitcast.3), calls=%async_computation.1 | async-start | bytes 32768 | tf_op jit(solution)/shard_map/all_to_all | solution.py:374
  65.6 1.2 %shard_map.92.vertices = f32[8,1024]{1,0:T(8,128)S(1)} custom-call(s32[2]{0:T(128)S(1)} %pad_add_fusion.index, f32[8,64,128]{2,1,0:T(8,128)S(1)} %all_to_all.16.slab, s32[1,1024]{1,0:T(1,128)S(1)} %bitcast.9, f32[64,1024]{1,0:T(8,128)S(1)} %copy-done.3), custom_call_target="tpu_custom_call" | custom-call | tf_op jit(solution)/shard_map/pallas_call | solution.py:23
  66.8 7.3 %all-to-all-done.1 = f32[32,1,128]{2,1,0:T(1,128)S(1)} async-done(((f32[32,1,128]{2,1,0:T(1,128)}), f32[32,1,128]{2,1,0:T(1,128)S(1)}, u32[]{:S(2)}, u32[]{:S(2)}) %all-to-all-start.1) | async-done | bytes 16416 | tf_op jit(solution)/shard_map/all_to_all | solution.py:374
  74.1 0.9 %shard_map.93 = (f32[32,512]{1,0:T(8,128)}, f32[32,512]{1,0:T(8,128)}, f32[1,1024]{1,0:T(1,128)}) custom-call(f32[32,128]{1,0:T(8,128)S(1)} %bitcast.8, f32[32,512]{1,0:T(8,128)S(1)} %copy-done.2, f32[32,512]{1,0:T(8,128)S(1)} %get-tuple-element.27.before.v1, f32[32,512]{1,0:T(8,128)S(1)} %get-tuple-element.31.before.v2, ...), custom_call_target="tpu_custom_call" | custom-call | tf_op jit(solution)/shard_map/pallas_call | solution.py:23
  (28 shorter events, 0.1 us)
Async XLA Ops:
  0.6 21.4 %copy-start.2 = (f32[32,512]{1,0:T(8,128)S(1)}, f32[32,512]{1,0:T(8,128)}, u32[]{:S(2)}) copy-start(f32[32,512]{1,0:T(8,128)} %v0.1) | copy-start | bytes 196612
  0.6 21.4 %copy-start.1 = (f32[32,512]{1,0:T(8,128)S(1)}, f32[32,512]{1,0:T(8,128)}, u32[]{:S(2)}) copy-start(f32[32,512]{1,0:T(8,128)} %diagonal.5) | copy-start | bytes 196612
  3.8 18.2 %copy-start.6 = (f32[1,128]{1,0:T(1,128)S(1)}, f32[1,128]{1,0:T(1,128)}, u32[]{:S(2)}) copy-start(f32[1,128]{1,0:T(1,128)} %get-tuple-element.24.moments) | copy-start | bytes 1540
  3.8 11.5 %collective-permute-start.1 = (f32[32,128]{1,0:T(8,128)}, f32[32,128]{1,0:T(8,128)S(1)}, u32[]{:S(2)}, u32[]{:S(2)}) collective-permute-start(f32[32,128]{1,0:T(8,128)} %get-tuple-element.21.block), channel_id=1, source_target_pairs={{8,16},{24,32},{40,48},{56,64},{72,80},{88,96},{104,112},{120,128}... | collective-permute-start | bytes 49160 | tf_op jit(solution)/shard_map/ppermute | solution.py:321
  12.5 2.8 %collective-permute-start = (f32[32,128]{1,0:T(8,128)}, f32[32,128]{1,0:T(8,128)S(1)}, u32[]{:S(2)}, u32[]{:S(2)}) collective-permute-start(f32[32,128]{1,0:T(8,128)} %get-tuple-element.21.block), channel_id=1, source_target_pairs={{0,8},{16,24},{32,40},{48,56},{64,72},{80,88},{96,104},{112,120},{... | collective-permute-start | bytes 49160 | tf_op jit(solution)/shard_map/ppermute | solution.py:321
  12.5 0.7 copy-start.4
  15.3 6.7 %collective-permute-start.3 = (f32[96,128]{1,0:T(8,128)S(1)}, f32[96,128]{1,0:T(8,128)S(1)}, u32[]{:S(2)}, u32[]{:S(2)}) collective-permute-start(f32[96,128]{1,0:T(8,128)S(1)} %constant_dynamic-update-slice_fusion.column), channel_id=1, source_target_pairs={{1,2},{3,4},{5,6},{7,0},{2,1},{4,3},{6,5},{0,7},{9,10},{11,12},{13... | collective-permute-start | bytes 147464 | tf_op jit(solution)/shard_map/ppermute | solution.py:323
  18.7 3.3 %collective-permute-start.2 = (f32[96,128]{1,0:T(8,128)S(1)}, f32[96,128]{1,0:T(8,128)S(1)}, u32[]{:S(2)}, u32[]{:S(2)}) collective-permute-start(f32[96,128]{1,0:T(8,128)S(1)} %constant_dynamic-update-slice_fusion.column), channel_id=1, source_target_pairs={{0,1},{2,3},{4,5},{6,7},{1,0},{3,2},{5,4},{7,6},{8,9},{10,11},{12,... | collective-permute-start | bytes 147464 | tf_op jit(solution)/shard_map/ppermute | solution.py:323
  18.7 2.2 %copy-start = (f32[32,64,512]{2,1,0:T(8,128)S(1)}, f32[32,64,512]{2,1,0:T(8,128)}, u32[]{:S(2)}) copy-start(f32[32,64,512]{2,1,0:T(8,128)} %features.9) | copy-start | bytes 12582916
  24.7 6.0 %collective-permute-start.4 = (f32[32,128]{1,0:T(8,128)S(1)}, f32[32,128]{1,0:T(8,128)S(1)}, u32[]{:S(2)}, u32[]{:S(2)}) collective-permute-start(f32[32,128]{1,0:T(8,128)S(1)} %get-tuple-element.25), channel_id=1, source_target_pairs={{8,16},{24,32},{40,48},{56,64},{72,80},{88,96},{104,112},{120,128}... | collective-permute-start | bytes 49160 | tf_op jit(solution)/shard_map/ppermute | solution.py:321
  27.8 2.9 %collective-permute-start.5 = (f32[32,128]{1,0:T(8,128)S(1)}, f32[32,128]{1,0:T(8,128)S(1)}, u32[]{:S(2)}, u32[]{:S(2)}) collective-permute-start(f32[32,128]{1,0:T(8,128)S(1)} %get-tuple-element.25), channel_id=1, source_target_pairs={{0,8},{16,24},{32,40},{48,56},{64,72},{80,88},{96,104},{112,120},{... | collective-permute-start | bytes 49160 | tf_op jit(solution)/shard_map/ppermute | solution.py:321
  30.7 4.7 %collective-permute-start.7 = (f32[96,128]{1,0:T(8,128)S(1)}, f32[96,128]{1,0:T(8,128)S(1)}, u32[]{:S(2)}, u32[]{:S(2)}) collective-permute-start(f32[96,128]{1,0:T(8,128)S(1)} %constant_dynamic-update-slice_fusion.3.column), channel_id=1, source_target_pairs={{1,2},{3,4},{5,6},{7,0},{2,1},{4,3},{6,5},{0,7},{9,10},{11,12},{13... | collective-permute-start | bytes 147464 | tf_op jit(solution)/shard_map/ppermute | solution.py:323
  33.6 1.8 %collective-permute-start.6 = (f32[96,128]{1,0:T(8,128)S(1)}, f32[96,128]{1,0:T(8,128)S(1)}, u32[]{:S(2)}, u32[]{:S(2)}) collective-permute-start(f32[96,128]{1,0:T(8,128)S(1)} %constant_dynamic-update-slice_fusion.3.column), channel_id=1, source_target_pairs={{0,1},{2,3},{4,5},{6,7},{1,0},{3,2},{5,4},{7,6},{8,9},{10,11},{12,... | collective-permute-start | bytes 147464 | tf_op jit(solution)/shard_map/ppermute | solution.py:323
  35.4 30.2 %copy-start.3 = (f32[64,1024]{1,0:T(8,128)S(1)}, f32[64,1024]{1,0:T(8,128)}, u32[]{:S(2)}) copy-start(f32[64,1024]{1,0:T(8,128)} %vertex_features.1) | copy-start | bytes 786436
  35.4 30.2 %copy-start.5 = (s32[1024]{0:T(1024)S(1)}, s32[1024]{0:T(1024)}, u32[]{:S(2)}) copy-start(s32[1024]{0:T(1024)} %param.11) | copy-start | bytes 12292
  36.8 6.0 %collective-permute-start.8 = (f32[32,128]{1,0:T(8,128)S(1)}, f32[32,128]{1,0:T(8,128)S(1)}, u32[]{:S(2)}, u32[]{:S(2)}) collective-permute-start(f32[32,128]{1,0:T(8,128)S(1)} %get-tuple-element.30), channel_id=1, source_target_pairs={{8,16},{24,32},{40,48},{56,64},{72,80},{88,96},{104,112},{120,128}... | collective-permute-start | bytes 49160 | tf_op jit(solution)/shard_map/ppermute | solution.py:321
  39.7 3.0 %collective-permute-start.9 = (f32[32,128]{1,0:T(8,128)S(1)}, f32[32,128]{1,0:T(8,128)S(1)}, u32[]{:S(2)}, u32[]{:S(2)}) collective-permute-start(f32[32,128]{1,0:T(8,128)S(1)} %get-tuple-element.30), channel_id=1, source_target_pairs={{0,8},{16,24},{32,40},{48,56},{64,72},{80,88},{96,104},{112,120},{... | collective-permute-start | bytes 49160 | tf_op jit(solution)/shard_map/ppermute | solution.py:321
  42.7 4.8 %collective-permute-start.11 = (f32[96,128]{1,0:T(8,128)S(1)}, f32[96,128]{1,0:T(8,128)S(1)}, u32[]{:S(2)}, u32[]{:S(2)}) collective-permute-start(f32[96,128]{1,0:T(8,128)S(1)} %constant_dynamic-update-slice_fusion.6.column), channel_id=1, source_target_pairs={{1,2},{3,4},{5,6},{7,0},{2,1},{4,3},{6,5},{0,7},{9,10},{11,12},{13... | collective-permute-start | bytes 147464 | tf_op jit(solution)/shard_map/ppermute | solution.py:323
  45.7 1.8 %collective-permute-start.10 = (f32[96,128]{1,0:T(8,128)S(1)}, f32[96,128]{1,0:T(8,128)S(1)}, u32[]{:S(2)}, u32[]{:S(2)}) collective-permute-start(f32[96,128]{1,0:T(8,128)S(1)} %constant_dynamic-update-slice_fusion.6.column), channel_id=1, source_target_pairs={{0,1},{2,3},{4,5},{6,7},{1,0},{3,2},{5,4},{7,6},{8,9},{10,11},{12,... | collective-permute-start | bytes 147464 | tf_op jit(solution)/shard_map/ppermute | solution.py:323
  61.0 13.1 %all-to-all-start.1 = ((f32[32,1,128]{2,1,0:T(1,128)}), f32[32,1,128]{2,1,0:T(1,128)S(1)}, u32[]{:S(2)}, u32[]{:S(2)}) async-start(f32[32,1,128]{2,1,0:T(1,128)} %bitcast.3), calls=%async_computation.1 | async-start | bytes 32768 | tf_op jit(solution)/shard_map/all_to_all | solution.py:374
